TPU v7x, 32 devices: a whole 2x2x4 slice. The times are simulated.
32 devices in a mesh: groups: 2 (over y), tgt: 4 (over z), src: 2 (over x), sub: 2 (over core).
Axes of the slice: x: 2, y: 2, z: 4, core: 2. Of those that a mesh axis runs over, the one named last changes fastest.
Arguments:
- positions: float32 [3, 8192], P(None, ('groups', 'tgt', 'src', 'sub')), parts along dimension 1, may hold values from 0 to 40
- forces: float32 [3, 8192], P(None, ('groups', 'tgt', 'src', 'sub')), parts along dimension 1, may hold values from -0.6 to 0.6
- membership: int32 [8192], P(('groups', 'tgt', 'src', 'sub')), parts along dimension 0, may hold values from 0 to 15, never falling along the last dimension, each value on 1 to 1024 neighbouring positions
- owner_slot: int32 [32], P('groups'), parts along dimension 0, may hold values from 0 to 15, each once
Outputs:
- velocity: float32 [3, 8192], P(None, ('groups', 'tgt', 'src', 'sub')), parts along dimension 1
- rigid: float32 [9, 32], P(None, ('groups', 'tgt', 'src', 'sub')), parts along dimension 1
There are 2 independent parts, one for each index of `groups`. A program takes and returns all parts, laid end to end along the dimension named above; each array names one. Nothing has to cross between parts.
Inputs may be any that keep to these rules, and one draw needn't show every extreme that they name: `membership`: monomers of one aggregate are consecutive; every aggregate holds 1 to 1024 monomers and one holds exactly 1024. `owner_slot`: a permutation; aggregate a's results go to column owner_slot[a] of rigid.
All inputs are finite; a program needn't handle non-finite values.
Results may differ from a plain program's by a relative error of at most 0.0003.
Values sent between devices are 32-bit elements; how exact they have to be, the bound alone decides.
No kernel may reach another device: no remote copies, remote signals or barrier semaphores. Data moves between devices by JAX's collectives and lax.ppermute only.
A program may use at most 64 MiB of HBM per device.

v0:
```python
import jax
import jax.numpy as jnp
from jax import lax
from jax.sharding import PartitionSpec as P

radius = 1.0


def pair_sum(target_pos, source_pos, source_force):
    offset = target_pos[:, :, None] - source_pos[:, None, :]
    dist_sq = jnp.sum(offset * offset, axis=0)
    nonzero = dist_sq > 0.0
    inverse = jnp.where(nonzero, lax.rsqrt(jnp.where(nonzero, dist_sq, 1.0)), 0.0)
    distance = dist_sq * inverse
    inverse_sq = inverse * inverse
    distant = dist_sq >= 4.0 * radius * radius
    iso_distant = 0.75 * radius * inverse * (1.0 + 2.0 / 3.0 * radius * radius * inverse_sq)
    dyad_distant = 0.75 * radius * inverse * (1.0 - 2.0 * radius * radius * inverse_sq) * inverse_sq
    iso_close = 1.0 - 9.0 * distance / (32.0 * radius)
    dyad_close = 3.0 * inverse / (32.0 * radius)
    iso_coef = jnp.where(distant, iso_distant, iso_close)
    dyad_coef = jnp.where(distant, dyad_distant, dyad_close)
    projected = jnp.sum(offset * source_force[:, None, :], axis=0)
    return jnp.sum(
        iso_coef[None] * source_force[:, None, :] + (dyad_coef * projected)[None] * offset, axis=2
    )


def accumulate(target_pos, source_pos, source_force):
    target_count = target_pos.shape[1]
    source_count = source_pos.shape[1]
    source_step = 512
    target_tiles = target_pos.reshape(3, target_count // target_count, target_count).transpose(
        1, 0, 2
    )
    source_tiles = (
        jnp.concatenate([source_pos, source_force], 0)
        .reshape(6, source_count // source_step, source_step)
        .transpose(1, 0, 2)
    )

    def one_target(target_tile):

        def add_tile(carry, source_tile):
            return (carry + pair_sum(target_tile, source_tile[:3], source_tile[3:]), None)

        result, unused = lax.scan(add_tile, jnp.zeros((3, target_count), jnp.float32), source_tiles)
        return result

    result = lax.map(one_target, target_tiles)
    return result.transpose(1, 0, 2).reshape(3, target_count)


def cross_product(left, right):
    return jnp.stack(
        [
            left[1] * right[2] - left[2] * right[1],
            left[2] * right[0] - left[0] * right[2],
            left[0] * right[1] - left[1] * right[0],
        ],
        0,
    )


def on_device(positions, forces, membership, owner_slot):
    velocity = accumulate(
        positions,
        lax.all_gather(positions, ("tgt", "src", "sub"), axis=1, tiled=True),
        lax.all_gather(forces, ("tgt", "src", "sub"), axis=1, tiled=True),
    )
    aggregate_count = owner_slot.shape[0]
    labels = jnp.arange(aggregate_count, dtype=jnp.int32)
    matches = membership[:, None] == labels[None, :]
    slot_row = jnp.sum(jnp.where(matches, owner_slot[None, :], 0), axis=1)
    indicator = (slot_row[:, None] == labels[None, :]).astype(jnp.float32)
    moments = jnp.concatenate([velocity, cross_product(positions, velocity), positions], 0)
    totals = jnp.dot(
        moments, indicator, precision=lax.Precision.HIGHEST, preferred_element_type=jnp.float32
    )
    counts = jnp.sum(indicator, axis=0)[None, :]
    mine, mine_counts = (
        lax.psum_scatter(totals, ("tgt", "src", "sub"), scatter_dimension=1, tiled=True),
        lax.psum_scatter(counts, ("tgt", "src", "sub"), scatter_dimension=1, tiled=True),
    )
    centre = mine[6:9] / mine_counts
    torque = mine[3:6] - cross_product(centre, mine[0:3])
    rigid = jnp.concatenate([mine[0:3], torque, centre], 0)
    return (velocity, rigid)


def solution(mesh):
    placed = (
        P(None, ("groups", "tgt", "src", "sub")),
        P(None, ("groups", "tgt", "src", "sub")),
        P(("groups", "tgt", "src", "sub")),
        P("groups"),
    )
    return jax.shard_map(
        on_device,
        mesh=mesh,
        in_specs=placed,
        out_specs=(
            P(None, ("groups", "tgt", "src", "sub")),
            P(None, ("groups", "tgt", "src", "sub")),
        ),
        check_vma=False,
    )
```

profile of v0, /device:TPU:0, one launch (start us, length us, event | category | flops | bytes accessed | tf_op | source)
XLA Modules:
  0.0 106.6 jit_solution(12333676045103217545)
XLA Ops:
  0.6 23.5 %all_gather.6 = f32[3,4096]{1,0:T(4,128)S(1)} all-gather(f32[3,256]{1,0:T(4,128)} %param.6), channel_id=1, replica_groups=mesh['groups'=2,'tgt'=4,'src'=2,'sub'=2] {'tgt','src','sub'}, dimensions={1}, use_global_device_ids=true | all-gather | bytes 52224 | tf_op jit(solution)/shard_map/all_gather | solution.py:68
  24.1 17.9 %all_gather.7 = f32[3,4096]{1,0:T(4,128)S(1)} all-gather(f32[3,256]{1,0:T(4,128)} %param.7), channel_id=1, replica_groups=mesh['groups'=2,'tgt'=4,'src'=2,'sub'=2] {'tgt','src','sub'}, dimensions={1}, use_global_device_ids=true | all-gather | bytes 52224 | tf_op jit(solution)/shard_map/all_gather | solution.py:69
  42.1 18.3 %while.20 = (s32[]{:T(128)}, f32[3,256]{1,0:T(4,128)S(1)}, f32[3,256]{1,0:T(4,128)}, f32[8,6,512]{2,1,0:T(8,128)S(1)}, s32[]{:T(128)}, /*index=5*/s32[]{:T(128)}, s32[]{}) while((s32[]{:T(128)}, f32[3,256]{1,0:T(4,128)S(1)}, f32[3,256]{1,0:T(4,128)}, f32[8,6,512]{2,1,0:T(8,128)S(1)}, s32[]{:T(128)}, /*index=5*/s32[]{:T(128)}, ...), condition=%wide.region_4.5_spmd.clone, body=%wide.region_0.4_spmd.clone.sunk | while | flops 6292228 | bytes 4274311 | solution.py:47
  42.1 1.1 %fusion.17 = (f32[256,512]{1,0:T(8,128)S(1)}, f32[256,512]{1,0:T(8,128)S(1)}) fusion(f32[3,512]{1,0:T(4,128)S(1)} %get-tuple-element.145, f32[3,256]{1,0:T(4,128)} %get-tuple-element.167, f32[3,512]{1,0:T(4,128)S(1)} %get-tuple-element.146), kind=kLoop, calls=%fused_computation.3.clone.1 | loop fusion | flops 1703936 | bytes 1063936 | tf_op jit(solution)/shard_map/while/body/eval_jaxpr/while/body/eval_jaxpr/reduce_sum | solution.py:11
  43.2 0.4 fusion.18
  43.6 0.3 copy-done
  43.9 0.4 fusion.19
  44.4 1.1 %fusion.17 = (f32[256,512]{1,0:T(8,128)S(1)}, f32[256,512]{1,0:T(8,128)S(1)}) fusion(f32[3,512]{1,0:T(4,128)S(1)} %get-tuple-element.145, f32[3,256]{1,0:T(4,128)} %get-tuple-element.167, f32[3,512]{1,0:T(4,128)S(1)} %get-tuple-element.146), kind=kLoop, calls=%fused_computation.3.clone.1 | loop fusion | flops 1703936 | bytes 1063936 | tf_op jit(solution)/shard_map/while/body/eval_jaxpr/while/body/eval_jaxpr/reduce_sum | solution.py:11
  45.5 0.4 fusion.18
  45.9 0.3 copy-done
  46.2 0.4 fusion.19
  46.7 1.1 %fusion.17 = (f32[256,512]{1,0:T(8,128)S(1)}, f32[256,512]{1,0:T(8,128)S(1)}) fusion(f32[3,512]{1,0:T(4,128)S(1)} %get-tuple-element.145, f32[3,256]{1,0:T(4,128)} %get-tuple-element.167, f32[3,512]{1,0:T(4,128)S(1)} %get-tuple-element.146), kind=kLoop, calls=%fused_computation.3.clone.1 | loop fusion | flops 1703936 | bytes 1063936 | tf_op jit(solution)/shard_map/while/body/eval_jaxpr/while/body/eval_jaxpr/reduce_sum | solution.py:11
  47.8 0.4 fusion.18
  48.2 0.3 copy-done
  48.5 0.4 fusion.19
  49.0 1.1 %fusion.17 = (f32[256,512]{1,0:T(8,128)S(1)}, f32[256,512]{1,0:T(8,128)S(1)}) fusion(f32[3,512]{1,0:T(4,128)S(1)} %get-tuple-element.145, f32[3,256]{1,0:T(4,128)} %get-tuple-element.167, f32[3,512]{1,0:T(4,128)S(1)} %get-tuple-element.146), kind=kLoop, calls=%fused_computation.3.clone.1 | loop fusion | flops 1703936 | bytes 1063936 | tf_op jit(solution)/shard_map/while/body/eval_jaxpr/while/body/eval_jaxpr/reduce_sum | solution.py:11
  50.1 0.4 fusion.18
  50.5 0.3 copy-done
  50.8 0.4 fusion.19
  51.3 1.1 %fusion.17 = (f32[256,512]{1,0:T(8,128)S(1)}, f32[256,512]{1,0:T(8,128)S(1)}) fusion(f32[3,512]{1,0:T(4,128)S(1)} %get-tuple-element.145, f32[3,256]{1,0:T(4,128)} %get-tuple-element.167, f32[3,512]{1,0:T(4,128)S(1)} %get-tuple-element.146), kind=kLoop, calls=%fused_computation.3.clone.1 | loop fusion | flops 1703936 | bytes 1063936 | tf_op jit(solution)/shard_map/while/body/eval_jaxpr/while/body/eval_jaxpr/reduce_sum | solution.py:11
  52.4 0.4 fusion.18
  52.8 0.3 copy-done
  53.1 0.4 fusion.19
  53.6 1.1 %fusion.17 = (f32[256,512]{1,0:T(8,128)S(1)}, f32[256,512]{1,0:T(8,128)S(1)}) fusion(f32[3,512]{1,0:T(4,128)S(1)} %get-tuple-element.145, f32[3,256]{1,0:T(4,128)} %get-tuple-element.167, f32[3,512]{1,0:T(4,128)S(1)} %get-tuple-element.146), kind=kLoop, calls=%fused_computation.3.clone.1 | loop fusion | flops 1703936 | bytes 1063936 | tf_op jit(solution)/shard_map/while/body/eval_jaxpr/while/body/eval_jaxpr/reduce_sum | solution.py:11
  54.7 0.4 fusion.18
  55.1 0.3 copy-done
  55.4 0.4 fusion.19
  55.9 1.1 %fusion.17 = (f32[256,512]{1,0:T(8,128)S(1)}, f32[256,512]{1,0:T(8,128)S(1)}) fusion(f32[3,512]{1,0:T(4,128)S(1)} %get-tuple-element.145, f32[3,256]{1,0:T(4,128)} %get-tuple-element.167, f32[3,512]{1,0:T(4,128)S(1)} %get-tuple-element.146), kind=kLoop, calls=%fused_computation.3.clone.1 | loop fusion | flops 1703936 | bytes 1063936 | tf_op jit(solution)/shard_map/while/body/eval_jaxpr/while/body/eval_jaxpr/reduce_sum | solution.py:11
  57.0 0.4 fusion.18
  57.3 0.3 copy-done
  57.7 0.4 fusion.19
  58.1 1.1 %fusion.17 = (f32[256,512]{1,0:T(8,128)S(1)}, f32[256,512]{1,0:T(8,128)S(1)}) fusion(f32[3,512]{1,0:T(4,128)S(1)} %get-tuple-element.145, f32[3,256]{1,0:T(4,128)} %get-tuple-element.167, f32[3,512]{1,0:T(4,128)S(1)} %get-tuple-element.146), kind=kLoop, calls=%fused_computation.3.clone.1 | loop fusion | flops 1703936 | bytes 1063936 | tf_op jit(solution)/shard_map/while/body/eval_jaxpr/while/body/eval_jaxpr/reduce_sum | solution.py:11
  59.3 0.4 fusion.18
  59.6 0.3 copy-done
  59.9 0.4 fusion.19
  60.4 0.8 multiply_subtract_fusion
  61.2 0.8 concatenate.10
  62.1 0.1 select_reduce_fusion
  62.1 0.1 fusion.8
  62.3 0.1 convert_reduce_fusion
  62.4 32.0 %all-reduce.2 = (f32[9,16]{0,1:T(8,128)S(1)}, f32[1,16]{1,0:T(1,128)S(1)}) all-reduce(f32[9,16]{0,1:T(8,128)S(1)} %fusion.8, f32[1,16]{1,0:T(1,128)S(1)} %bitcast.16), channel_id=2, replica_groups=mesh['groups'=2,'tgt'=4,'src'=2,'sub'=2] {'tgt','src','sub'}, use_global_device_ids=true, to_apply=%region_6.7.clone | all-reduce | flops 160 | bytes 1280
  94.4 0.6 dynamic-slice.1
  95.0 0.7 constant_dynamic-slice_fusion.1
  95.7 1.3 %constant_dynamic-slice_fusion = f32[1,1]{1,0:T(1,128)} fusion(f32[1,16]{1,0:T(1,128)S(1)} %get-tuple-element.95, u32[]{:T(128)} %bitcast.9), kind=kLoop, calls=%fused_computation.29 | loop fusion | bytes 12
  97.0 0.8 fusion.10
  97.7 0.7 fusion.11
  105.9 0.1 maximum_subtract_fusion
  106.0 0.6 pad_maximum_fusion.1
  (34 shorter events, 0.3 us)
Async XLA Ops:
  42.1 20.0 %copy-start.2 = (s32[256]{0:T(256)S(1)}, s32[256]{0:T(256)}, u32[]{:S(2)}) copy-start(s32[256]{0:T(256)} %param.8) | copy-start | bytes 3076
  42.1 20.0 %copy-start.3 = (s32[16]{0:T(128)S(1)}, s32[16]{0:T(128)}, u32[]{:S(2)}) copy-start(s32[16]{0:T(128)} %param.9) | copy-start | bytes 196
  42.1 52.3 %copy-start.4 = (u32[32]{0:T(128)S(1)}, u32[32]{0:T(128)}, u32[]{:S(2)}) copy-start(u32[32]{0:T(128)} %constant.83) | copy-start | bytes 388
  43.2 0.7 copy-start
  45.5 0.7 copy-start
  47.8 0.7 copy-start
  50.1 0.7 copy-start
  52.4 0.7 copy-start
  54.7 0.7 copy-start
  57.0 0.7 copy-start
  59.3 0.7 copy-start
  60.4 46.2 %copy-start.1 = (f32[3,256]{1,0:T(4,128)}, f32[3,256]{1,0:T(4,128)S(1)}, u32[]{:S(2)}) copy-start(f32[3,256]{1,0:T(4,128)S(1)} %get-tuple-element.66) | copy-start | bytes 9220
where the time goes:
time: 108 us; the launch traced here: 107 us
  blocking collectives  73.4 us (68%)
  other arithmetic  17.8 us (16%)
  between operations  8.27 us (8%)
  local copies, waits for them, and re-layouts  6.62 us (6%)
    unnamed x1, blocking collectives  32 us
    all_gather x1, blocking collectives, on_device(): lax.all_gather(positions, ('tgt', 'src', 'sub'), axis=1, tiled=True)  23.5 us
    all_gather x1, blocking collectives, on_device(): lax.all_gather(forces, ('tgt', 'src', 'sub'), axis=1, tiled=True)  17.9 us
    reduce_sum x8, other arithmetic, pair_sum(): dist_sq = jnp.sum(offset * offset, axis=0)  8.82 us
    reduce_sum x8, other arithmetic, pair_sum(): jnp.sum(iso_coef[None] * source_force[:, None, :] + (dyad_coef * projecte...  3.51 us
    select_n x8, other arithmetic, pair_sum(): iso_coef = jnp.where(distant, iso_distant, iso_close)  2.91 us
    unnamed x11, local copies, waits for them, and re-layouts  2.57 us
    while x16, local copies, waits for them, and re-layouts  2.48 us

commit v1 on v0

v1 whole, which is shorter than its diff:
```python
import functools
import math

import jax
import jax.numpy as jnp
from jax import lax
from jax.experimental import pallas as pl
from jax.experimental.pallas import tpu as pltpu
from jax.sharding import PartitionSpec as P

SCALE = math.sqrt(0.75)
ISO = 9.0 / (32.0 * SCALE)
DYAD = 3.0 * ISO
TOUCH = 2.0 * SCALE
TOUCH_INVERSE = 1.0 / TOUCH
SMALLEST = 1.1754944e-38

LANES = 128
SUBLANES = 8
GROUPS_AT_ONCE = 4
BLOCKS_AT_ONCE = 8
AXES = ("tgt", "src", "sub")


def pair_kernel(own_ref, source_ref, before_ref, out_ref, turned, total):
    count = own_ref.shape[1]
    sources = source_ref.shape[1]
    blocks = sources // LANES
    together = math.gcd(blocks, BLOCKS_AT_ONCE)
    rows = SUBLANES * math.gcd(count // SUBLANES, GROUPS_AT_ONCE)
    groups = rows // SUBLANES

    for start in range(0, count, LANES):
        tile = jnp.concatenate(
            [own_ref[:, start : start + LANES], jnp.zeros((2, LANES), jnp.float32)], axis=0
        )
        turned[start : start + LANES, :] = tile.T

    def target_step(step, unused):
        first = pl.multiple_of(step * rows, rows)
        points = []
        for group in range(groups):
            column = turned[pl.ds(first + group * SUBLANES, SUBLANES), :]
            points.append(
                [jnp.broadcast_to(column[:, k : k + 1], (SUBLANES, LANES)) for k in range(3)]
            )

        def source_step(number, carry):
            sums = [list(one) for one in carry]
            base = number * (together * LANES)
            for block in range(together):
                lanes = pl.ds(pl.multiple_of(base + block * LANES, LANES), LANES)
                x, y, z, fx, fy, fz = [
                    jnp.broadcast_to(source_ref[k : k + 1, lanes], (SUBLANES, LANES))
                    for k in range(6)
                ]
                for group in range(groups):
                    px, py, pz = points[group]
                    dx, dy, dz = px - x, py - y, pz - z
                    square = dx * dx + dy * dy + dz * dz
                    inverse = lax.rsqrt(jnp.maximum(square, SMALLEST))
                    held = jnp.minimum(inverse, TOUCH_INVERSE)
                    held_sq = held * held
                    gap = jnp.maximum(TOUCH - square * inverse, 0.0)
                    iso = held * (held_sq + 2.0) + gap
                    along = dx * fx + dy * fy + dz * fz
                    dyad = (inverse * (held_sq * (2.0 / 3.0 - held_sq))) * along
                    one = sums[group]
                    sums[group] = [
                        one[0] + iso * fx,
                        one[1] + iso * fy,
                        one[2] + iso * fz,
                        one[3] + dyad * dx,
                        one[4] + dyad * dy,
                        one[5] + dyad * dz,
                    ]
            return tuple(tuple(one) for one in sums)

        zero = jnp.zeros((SUBLANES, LANES), jnp.float32)
        carry = tuple((zero,) * 6 for _ in range(groups))
        if blocks == together:
            carry = source_step(0, carry)
        else:
            carry = lax.fori_loop(0, blocks // together, source_step, carry)
        for group in range(groups):
            for k in range(3):
                total[k, pl.ds(first + group * SUBLANES, SUBLANES), :] = (
                    ISO * carry[group][k] + DYAD * carry[group][3 + k]
                )
        return unused

    lax.fori_loop(0, count // rows, target_step, 0)
    ones = jnp.ones((SUBLANES, LANES), jnp.float32)
    for k in range(3):
        summed = lax.dot_general(
            ones,
            total[k],
            (((1,), (1,)), ((), ())),
            precision=lax.Precision.HIGHEST,
            preferred_element_type=jnp.float32,
        )
        out_ref[k : k + 1, :] = before_ref[k : k + 1, :] + summed[0:1, :]


def velocities(own, source, before):
    count, sources = own.shape[1], source.shape[1]
    whole = pl.BlockSpec(memory_space=pltpu.VMEM)
    return pl.pallas_call(
        pair_kernel,
        out_shape=jax.ShapeDtypeStruct((3, count), jnp.float32),
        in_specs=[whole] * 3,
        out_specs=whole,
        scratch_shapes=[
            pltpu.VMEM((count, SUBLANES), jnp.float32),
            pltpu.VMEM((3, count, LANES), jnp.float32),
        ],
        compiler_params=pltpu.CompilerParams(vmem_limit_bytes=16 << 20),
        cost_estimate=pl.CostEstimate(
            flops=40 * count * sources, bytes_accessed=4 * 9 * sources, transcendentals=count * sources
        ),
    )(own, source, before)


def sums_kernel(velocity_ref, position_ref, member_ref, out_ref):
    aggregates = out_ref.shape[1]
    count = velocity_ref.shape[1]
    u = [velocity_ref[k : k + 1, :] for k in range(3)]
    x = [position_ref[k : k + 1, :] for k in range(3)]
    moments = jnp.concatenate(
        u
        + [
            x[1] * u[2] - x[2] * u[1],
            x[2] * u[0] - x[0] * u[2],
            x[0] * u[1] - x[1] * u[0],
        ]
        + x
        + [jnp.ones((1, count), jnp.float32)]
        + [jnp.zeros((6, count), jnp.float32)],
        axis=0,
    )
    labels = lax.broadcasted_iota(jnp.int32, (aggregates, count), 0)
    matches = jnp.where(labels == member_ref[...], 1.0, 0.0)
    out_ref[...] = lax.dot_general(
        moments,
        matches,
        (((1,), (1,)), ((), ())),
        precision=lax.Precision.HIGHEST,
        preferred_element_type=jnp.float32,
    )


def aggregate_sums(velocity, positions, membership, aggregates):
    whole = pl.BlockSpec(memory_space=pltpu.VMEM)
    return pl.pallas_call(
        sums_kernel,
        out_shape=jax.ShapeDtypeStruct((16, aggregates), jnp.float32),
        in_specs=[whole] * 3,
        out_specs=whole,
        compiler_params=pltpu.CompilerParams(vmem_limit_bytes=16 << 20),
    )(velocity, positions, membership[None, :])


def rigid_kernel(first_ref, sums_ref, owner_ref, out_ref):
    columns = out_ref.shape[1]
    sums = sums_ref[...]
    for column in range(columns):
        chosen = owner_ref[...] == first_ref[0] + column
        mine = jnp.sum(jnp.where(chosen, sums, 0.0), axis=1, keepdims=True)
        u = [mine[k : k + 1] for k in range(3)]
        moment = [mine[3 + k : 4 + k] for k in range(3)]
        centre = [mine[6 + k : 7 + k] / mine[9:10] for k in range(3)]
        torque = [
            moment[0] - (centre[1] * u[2] - centre[2] * u[1]),
            moment[1] - (centre[2] * u[0] - centre[0] * u[2]),
            moment[2] - (centre[0] * u[1] - centre[1] * u[0]),
        ]
        for row, value in enumerate(u + torque + centre):
            out_ref[row : row + 1, column : column + 1] = value


def rigid_columns(first, sums, owner_slot, columns):
    whole = pl.BlockSpec(memory_space=pltpu.VMEM)
    return pl.pallas_call(
        rigid_kernel,
        out_shape=jax.ShapeDtypeStruct((9, columns), jnp.float32),
        in_specs=[pl.BlockSpec(memory_space=pltpu.SMEM), whole, whole],
        out_specs=whole,
        compiler_params=pltpu.CompilerParams(vmem_limit_bytes=16 << 20),
    )(first, sums, owner_slot[None, :])


def exchange_steps(mesh):
    steps = []
    for axis in reversed(AXES):
        size = mesh.shape[axis]
        reach = 1
        while reach < size:
            steps.append((axis, [(i, i ^ reach) for i in range(size)]))
            reach *= 2
    return steps


def on_device(steps, devices, positions, forces, membership, owner_slot):
    own = jnp.concatenate([SCALE * positions, forces], axis=0)
    velocity = jnp.zeros_like(positions)
    held, arrived = own, own
    for axis, pairs in steps:
        coming = lax.ppermute(held, axis, pairs)
        velocity = velocities(own, arrived, velocity)
        velocity, coming = lax.optimization_barrier((velocity, coming))
        held, arrived = jnp.concatenate([held, coming], axis=1), coming
    velocity = velocities(own, arrived, velocity)

    aggregates = owner_slot.shape[0]
    sums = aggregate_sums(velocity, positions, membership, aggregates)
    for axis, pairs in steps:
        sums = sums + lax.ppermute(sums, axis, pairs)
    columns = aggregates // devices
    first = (lax.axis_index(AXES) * columns).astype(jnp.int32).reshape(1)
    return velocity, rigid_columns(first, sums, owner_slot, columns)


def solution(mesh):
    placed = (
        P(None, ("groups",) + AXES),
        P(None, ("groups",) + AXES),
        P(("groups",) + AXES),
        P("groups"),
    )
    devices = math.prod(mesh.shape[axis] for axis in AXES)
    return jax.shard_map(
        functools.partial(on_device, exchange_steps(mesh), devices),
        mesh=mesh,
        in_specs=placed,
        out_specs=(P(None, ("groups",) + AXES), P(None, ("groups",) + AXES)),
        check_vma=False,
    )
```

time: 108 us -> 38.5 us (0.36); the launches traced: 107 us -> 38.3 us
  blocking collectives: 73.4 us -> 0 us
  other arithmetic: 17.8 us -> 0.77 us
  starting transfers between devices: 0 us -> 14.1 us
  Pallas kernels: 0 us -> 12.5 us
  between operations: 8.27 us -> 0.67 us
  waiting for transfers between devices: 0 us -> 7.57 us
  local copies, waits for them, and re-layouts: 6.62 us -> 2.62 us
    all_gather x2 -> x0, blocking collectives: 41.4 us -> none  [the longest x1 23.5 us: on_device(): lax.all_gather(positions, ('tgt', 'src', 'sub'), axis=1, tiled=True)]
    unnamed x1 -> x0, blocking collectives: 32 us -> none
    ppermute x0 -> x8, starting transfers between devices: none -> 14.1 us  [the longest x4 8.38 us: on_device(): coming = lax.ppermute(held, axis, pairs)]
    reduce_sum x18 -> x0, other arithmetic: 12.5 us -> none  [the longest x8 8.82 us: pair_sum(): dist_sq = jnp.sum(offset * offset, axis=0)]
    pallas_call x0 -> x7, Pallas kernels: none -> 12.5 us  [the longest x5 12.3 us: velocities(): pl.pallas_call(pair_kernel, out_shape=jax.ShapeDtypeStruct((3, count), jn...]
    ppermute x0 -> x8, waiting for transfers between devices: none -> 7.57 us  [the longest x4 7.3 us: on_device(): sums = sums + lax.ppermute(sums, axis, pairs)]
    select_n x8 -> x0, other arithmetic: 2.91 us -> none  [pair_sum(): iso_coef = jnp.where(distant, iso_distant, iso_close)]
    while x16 -> x0, local copies, waits for them, and re-layouts: 2.48 us -> none
  transfers between devices with their start and end apart: 0 -> 8, of which waited for: 0 -> 6; matrix products, arithmetic and copies ran while one was open for 0% -> 0% of each run, Pallas kernels for 0% -> 19%
where the time goes in v1:
time: 38.5 us; the launch traced here: 38.3 us
  starting transfers between devices  14.1 us (37%)
  Pallas kernels  12.5 us (32%)
  waiting for transfers between devices  7.57 us (20%)
  local copies, waits for them, and re-layouts  2.62 us (7%)
  other arithmetic  0.77 us (2%)
  between operations  0.67 us (2%)
    pallas_call x5, Pallas kernels, velocities(): pl.pallas_call(pair_kernel, out_shape=jax.ShapeDtypeStruct((3, count), jn...  12.3 us
    ppermute x4, starting transfers between devices, on_device(): coming = lax.ppermute(held, axis, pairs)  8.38 us
    ppermute x4, waiting for transfers between devices, on_device(): sums = sums + lax.ppermute(sums, axis, pairs)  7.3 us
    ppermute x4, starting transfers between devices, on_device(): sums = sums + lax.ppermute(sums, axis, pairs)  5.74 us
    unnamed x11, local copies, waits for them, and re-layouts  2.62 us
  transfers between devices with their start and end apart: 8, of which 6 were waited for; matrix products, arithmetic and copies ran while one was open for 0% of the time, Pallas kernels for 19%

profile of v1, /device:TPU:0, one launch (start us, length us, event | category | flops | bytes accessed | tf_op | source)
XLA Modules:
  0.0 38.3 jit_solution(13502330145785018938)
XLA Ops:
  0.6 0.0 copy-start.4
  0.6 0.7 %broadcast_multiply_fusion = f32[3,256]{1,0:T(4,128)S(1)} fusion(f32[3,256]{1,0:T(4,128)} %position_ref.1), kind=kLoop, calls=%fused_computation.4 | loop fusion | flops 768 | bytes 6144 | tf_op jit(solution)/shard_map/mul | solution.py:204
  1.3 0.0 copy-done.4
  1.3 0.6 %collective-permute-start = (f32[6,256]{1,0:T(8,128)S(1)}, f32[6,256]{1,0:T(8,128)S(1)}, u32[]{:S(2)}, u32[]{:S(2)}) collective-permute-start(f32[6,256]{1,0:T(8,128)S(1)} %pad_maximum_fusion.3.own_ref.source_ref), channel_id=1, source_target_pairs={{0,1},{1,0},{2,3},{3,2},{4,5},{5,4},{6,7},{7,6},{8,9},{9,8},{10,11... | collective-permute-start | bytes 18440 | tf_op jit(solution)/shard_map/ppermute | solution.py:208
  1.9 1.5 %shard_map.59.before_ref = f32[3,256]{1,0:T(4,128)S(1)} custom-call(f32[6,256]{1,0:T(8,128)S(1)} %pad_maximum_fusion.3.own_ref.source_ref, f32[6,256]{1,0:T(8,128)S(1)} %pad_maximum_fusion.3.own_ref.source_ref, f32[3,256]{1,0:T(4,128)S(1)} %broadcast_in_dim.9.before_ref), custom_call_target="tpu_custom_call" | custom-call | flops 2621440 | bytes 9216 | tf_op jit(solution)/shard_map/pallas_call | solution.py:108
  3.4 0.0 collective-permute-done.source_ref
  3.5 2.6 %collective-permute-start.1 = (f32[6,512]{1,0:T(8,128)S(1)}, f32[6,512]{1,0:T(8,128)S(1)}, u32[]{:S(2)}, u32[]{:S(2)}) collective-permute-start(f32[6,512]{1,0:T(8,128)S(1)} %pad_maximum_fusion.2), channel_id=1, source_target_pairs={{0,2},{2,0},{1,3},{3,1},{4,6},{6,4},{5,7},{7,5},{8,10},{10,8},{9,1... | collective-permute-start | bytes 36872 | tf_op jit(solution)/shard_map/ppermute | solution.py:208
  6.0 1.5 %shard_map.60.before_ref = f32[3,256]{1,0:T(4,128)S(1)} custom-call(f32[6,256]{1,0:T(8,128)S(1)} %pad_maximum_fusion.3.own_ref.source_ref, f32[6,256]{1,0:T(8,128)S(1)} %collective-permute-done.source_ref, f32[3,256]{1,0:T(4,128)S(1)} %shard_map.59.before_ref), custom_call_target="tpu_custom_call" | custom-call | flops 2621440 | bytes 9216 | tf_op jit(solution)/shard_map/pallas_call | solution.py:108
  7.5 0.2 collective-permute-done.1.source_ref
  7.7 2.2 %collective-permute-start.2 = (f32[6,1024]{1,0:T(8,128)S(1)}, f32[6,1024]{1,0:T(8,128)S(1)}, u32[]{:S(2)}, u32[]{:S(2)}) collective-permute-start(f32[6,1024]{1,0:T(8,128)S(1)} %pad_maximum_fusion.1), channel_id=1, source_target_pairs={{0,4},{4,0},{8,12},{12,8},{1,5},{5,1},{9,13},{13,9},{2,6},{6,2},{1... | collective-permute-start | bytes 73736 | tf_op jit(solution)/shard_map/ppermute | solution.py:208
  9.9 1.8 %shard_map.61.before_ref = f32[3,256]{1,0:T(4,128)S(1)} custom-call(f32[6,256]{1,0:T(8,128)S(1)} %pad_maximum_fusion.3.own_ref.source_ref, f32[6,512]{1,0:T(8,128)S(1)} %collective-permute-done.1.source_ref, f32[3,256]{1,0:T(4,128)S(1)} %shard_map.60.before_ref), custom_call_target="tpu_custom_call" | custom-call | flops 5242880 | bytes 18432 | tf_op jit(solution)/shard_map/pallas_call | solution.py:108
  11.8 0.1 collective-permute-done.2.source_ref
  11.8 3.1 %collective-permute-start.3 = (f32[6,2048]{1,0:T(8,128)S(1)}, f32[6,2048]{1,0:T(8,128)S(1)}, u32[]{:S(2)}, u32[]{:S(2)}) collective-permute-start(f32[6,2048]{1,0:T(8,128)S(1)} %pad_maximum_fusion), channel_id=1, source_target_pairs={{0,8},{4,12},{8,0},{12,4},{1,9},{5,13},{9,1},{13,5},{2,10},{6,14},... | collective-permute-start | bytes 147464 | tf_op jit(solution)/shard_map/ppermute | solution.py:208
  14.9 2.6 %shard_map.62.before_ref = f32[3,256]{1,0:T(4,128)S(1)} custom-call(f32[6,256]{1,0:T(8,128)S(1)} %pad_maximum_fusion.3.own_ref.source_ref, f32[6,1024]{1,0:T(8,128)S(1)} %collective-permute-done.2.source_ref, f32[3,256]{1,0:T(4,128)S(1)} %shard_map.61.before_ref), custom_call_target="tpu_custom_call" | custom-call | flops 10485760 | bytes 36864 | tf_op jit(solution)/shard_map/pallas_call | solution.py:108
  17.5 0.0 collective-permute-done.3.source_ref
  17.5 0.0 copy-start
  17.5 4.8 %shard_map.63.velocity_ref = f32[3,256]{1,0:T(4,128)} custom-call(f32[6,256]{1,0:T(8,128)S(1)} %pad_maximum_fusion.3.own_ref.source_ref, f32[6,2048]{1,0:T(8,128)S(1)} %collective-permute-done.3.source_ref, f32[3,256]{1,0:T(4,128)S(1)} %shard_map.62.before_ref), custom_call_target="tpu_custom_call" | custom-call | flops 20971520 | bytes 73728 | tf_op jit(solution)/shard_map/pallas_call | solution.py:108
  22.3 0.0 copy-start.2
  22.3 0.0 copy-done
  22.3 0.7 %copy-done.2 = s32[256]{0:T(256)S(1)} copy-done((s32[256]{0:T(256)S(1)}, s32[256]{0:T(256)}, u32[]{:S(2)}) %copy-start.2) | copy-done | bytes 1048
  23.0 0.0 copy-start.1
  23.0 0.7 %copy-done.1 = f32[3,256]{1,0:T(4,128)S(1)} copy-done((f32[3,256]{1,0:T(4,128)S(1)}, f32[3,256]{1,0:T(4,128)}, u32[]{:S(2)}) %copy-start.1) | copy-done | bytes 3096
  23.7 0.1 shard_map.64
  23.8 0.0 collective-permute-start.4
  23.8 1.2 %collective-permute-done.4 = f32[16,16]{1,0:T(8,128)S(1)} collective-permute-done((f32[16,16]{1,0:T(8,128)S(1)}, f32[16,16]{1,0:T(8,128)S(1)}, u32[]{:S(2)}, u32[]{:S(2)}) %collective-permute-start.4) | collective-permute-done | bytes 1056 | tf_op jit(solution)/shard_map/ppermute | solution.py:217
  25.0 1.5 %collective-permute-start.5 = (f32[16,16]{1,0:T(8,128)S(1)}, f32[16,16]{1,0:T(8,128)S(1)}, u32[]{:S(2)}, u32[]{:S(2)}) collective-permute-start(f32[16,16]{1,0:T(8,128)S(1)} %add.20), channel_id=1, source_target_pairs={{0,2},{2,0},{1,3},{3,1},{4,6},{6,4},{5,7},{7,5},{8,10},{10,8},{9,1... | collective-permute-start | bytes 3080 | tf_op jit(solution)/shard_map/ppermute | solution.py:217
  26.5 2.2 %collective-permute-done.5 = f32[16,16]{1,0:T(8,128)S(1)} collective-permute-done((f32[16,16]{1,0:T(8,128)S(1)}, f32[16,16]{1,0:T(8,128)S(1)}, u32[]{:S(2)}, u32[]{:S(2)}) %collective-permute-start.5) | collective-permute-done | bytes 1056 | tf_op jit(solution)/shard_map/ppermute | solution.py:217
  28.7 1.6 %collective-permute-start.6 = (f32[16,16]{1,0:T(8,128)S(1)}, f32[16,16]{1,0:T(8,128)S(1)}, u32[]{:S(2)}, u32[]{:S(2)}) collective-permute-start(f32[16,16]{1,0:T(8,128)S(1)} %add.21), channel_id=1, source_target_pairs={{0,4},{4,0},{8,12},{12,8},{1,5},{5,1},{9,13},{13,9},{2,6},{6,2},{1... | collective-permute-start | bytes 3080 | tf_op jit(solution)/shard_map/ppermute | solution.py:217
  30.3 2.1 %collective-permute-done.6 = f32[16,16]{1,0:T(8,128)S(1)} collective-permute-done((f32[16,16]{1,0:T(8,128)S(1)}, f32[16,16]{1,0:T(8,128)S(1)}, u32[]{:S(2)}, u32[]{:S(2)}) %collective-permute-start.6) | collective-permute-done | bytes 1056 | tf_op jit(solution)/shard_map/ppermute | solution.py:217
  32.3 2.7 %collective-permute-start.7 = (f32[16,16]{1,0:T(8,128)S(1)}, f32[16,16]{1,0:T(8,128)S(1)}, u32[]{:S(2)}, u32[]{:S(2)}) collective-permute-start(f32[16,16]{1,0:T(8,128)S(1)} %add.22), channel_id=1, source_target_pairs={{0,8},{4,12},{8,0},{12,4},{1,9},{5,13},{9,1},{13,5},{2,10},{6,14},... | collective-permute-start | bytes 3080 | tf_op jit(solution)/shard_map/ppermute | solution.py:217
  35.0 1.9 %collective-permute-done.7 = f32[16,16]{1,0:T(8,128)S(1)} collective-permute-done((f32[16,16]{1,0:T(8,128)S(1)}, f32[16,16]{1,0:T(8,128)S(1)}, u32[]{:S(2)}, u32[]{:S(2)}) %collective-permute-start.7) | collective-permute-done | bytes 1056 | tf_op jit(solution)/shard_map/ppermute | solution.py:217
  36.9 0.0 copy-start.3
  36.9 0.7 %copy-done.3 = s32[16]{0:T(128)S(1)} copy-done((s32[16]{0:T(128)S(1)}, s32[16]{0:T(128)}, u32[]{:S(2)}) %copy-start.3) | copy-done | bytes 88
  37.6 0.1 shard_map.65
  37.7 0.6 %copy.6 = f32[9,1]{0,1:T(1,128)} copy(f32[9,1]{1,0:T(8,128)S(1)} %shard_map.65) | data formatting | bytes 72
  (9 shorter events, 0.1 us)
Async XLA Ops:
  0.6 0.7 %copy-start.4 = (f32[3,256]{1,0:T(4,128)S(1)}, f32[3,256]{1,0:T(4,128)}, u32[]{:S(2)}) copy-start(f32[3,256]{1,0:T(4,128)} %param.5) | copy-start | bytes 9220
  1.3 2.1 %collective-permute-start = (f32[6,256]{1,0:T(8,128)S(1)}, f32[6,256]{1,0:T(8,128)S(1)}, u32[]{:S(2)}, u32[]{:S(2)}) collective-permute-start(f32[6,256]{1,0:T(8,128)S(1)} %pad_maximum_fusion.3.own_ref.source_ref), channel_id=1, source_target_pairs={{0,1},{1,0},{2,3},{3,2},{4,5},{5,4},{6,7},{7,6},{8,9},{9,8},{10,11... | collective-permute-start | bytes 18440 | tf_op jit(solution)/shard_map/ppermute | solution.py:208
  3.5 4.3 %collective-permute-start.1 = (f32[6,512]{1,0:T(8,128)S(1)}, f32[6,512]{1,0:T(8,128)S(1)}, u32[]{:S(2)}, u32[]{:S(2)}) collective-permute-start(f32[6,512]{1,0:T(8,128)S(1)} %pad_maximum_fusion.2), channel_id=1, source_target_pairs={{0,2},{2,0},{1,3},{3,1},{4,6},{6,4},{5,7},{7,5},{8,10},{10,8},{9,1... | collective-permute-start | bytes 36872 | tf_op jit(solution)/shard_map/ppermute | solution.py:208
  7.7 4.1 %collective-permute-start.2 = (f32[6,1024]{1,0:T(8,128)S(1)}, f32[6,1024]{1,0:T(8,128)S(1)}, u32[]{:S(2)}, u32[]{:S(2)}) collective-permute-start(f32[6,1024]{1,0:T(8,128)S(1)} %pad_maximum_fusion.1), channel_id=1, source_target_pairs={{0,4},{4,0},{8,12},{12,8},{1,5},{5,1},{9,13},{13,9},{2,6},{6,2},{1... | collective-permute-start | bytes 73736 | tf_op jit(solution)/shard_map/ppermute | solution.py:208
  11.8 5.7 %collective-permute-start.3 = (f32[6,2048]{1,0:T(8,128)S(1)}, f32[6,2048]{1,0:T(8,128)S(1)}, u32[]{:S(2)}, u32[]{:S(2)}) collective-permute-start(f32[6,2048]{1,0:T(8,128)S(1)} %pad_maximum_fusion), channel_id=1, source_target_pairs={{0,8},{4,12},{8,0},{12,4},{1,9},{5,13},{9,1},{13,5},{2,10},{6,14},... | collective-permute-start | bytes 147464 | tf_op jit(solution)/shard_map/ppermute | solution.py:208
  17.5 4.8 %copy-start = (f32[3,256]{1,0:T(4,128)S(1)}, f32[3,256]{1,0:T(4,128)}, u32[]{:S(2)}) copy-start(f32[3,256]{1,0:T(4,128)} %position_ref.1) | copy-start | bytes 9220
  22.3 0.7 %copy-start.2 = (s32[256]{0:T(256)S(1)}, s32[256]{0:T(256)}, u32[]{:S(2)}) copy-start(s32[256]{0:T(256)} %param.6) | copy-start | bytes 3076
  23.0 0.7 %copy-start.1 = (f32[3,256]{1,0:T(4,128)S(1)}, f32[3,256]{1,0:T(4,128)}, u32[]{:S(2)}) copy-start(f32[3,256]{1,0:T(4,128)} %shard_map.63.velocity_ref) | copy-start | bytes 9220
  23.8 1.2 %collective-permute-start.4 = (f32[16,16]{1,0:T(8,128)S(1)}, f32[16,16]{1,0:T(8,128)S(1)}, u32[]{:S(2)}, u32[]{:S(2)}) collective-permute-start(f32[16,16]{1,0:T(8,128)S(1)} %shard_map.64), channel_id=1, source_target_pairs={{0,1},{1,0},{2,3},{3,2},{4,5},{5,4},{6,7},{7,6},{8,9},{9,8},{10,11... | collective-permute-start | bytes 3080 | tf_op jit(solution)/shard_map/ppermute | solution.py:217
  25.0 3.7 %collective-permute-start.5 = (f32[16,16]{1,0:T(8,128)S(1)}, f32[16,16]{1,0:T(8,128)S(1)}, u32[]{:S(2)}, u32[]{:S(2)}) collective-permute-start(f32[16,16]{1,0:T(8,128)S(1)} %add.20), channel_id=1, source_target_pairs={{0,2},{2,0},{1,3},{3,1},{4,6},{6,4},{5,7},{7,5},{8,10},{10,8},{9,1... | collective-permute-start | bytes 3080 | tf_op jit(solution)/shard_map/ppermute | solution.py:217
  28.7 3.7 %collective-permute-start.6 = (f32[16,16]{1,0:T(8,128)S(1)}, f32[16,16]{1,0:T(8,128)S(1)}, u32[]{:S(2)}, u32[]{:S(2)}) collective-permute-start(f32[16,16]{1,0:T(8,128)S(1)} %add.21), channel_id=1, source_target_pairs={{0,4},{4,0},{8,12},{12,8},{1,5},{5,1},{9,13},{13,9},{2,6},{6,2},{1... | collective-permute-start | bytes 3080 | tf_op jit(solution)/shard_map/ppermute | solution.py:217
  32.3 4.5 %collective-permute-start.7 = (f32[16,16]{1,0:T(8,128)S(1)}, f32[16,16]{1,0:T(8,128)S(1)}, u32[]{:S(2)}, u32[]{:S(2)}) collective-permute-start(f32[16,16]{1,0:T(8,128)S(1)} %add.22), channel_id=1, source_target_pairs={{0,8},{4,12},{8,0},{12,4},{1,9},{5,13},{9,1},{13,5},{2,10},{6,14},... | collective-permute-start | bytes 3080 | tf_op jit(solution)/shard_map/ppermute | solution.py:217
  36.9 0.7 %copy-start.3 = (s32[16]{0:T(128)S(1)}, s32[16]{0:T(128)}, u32[]{:S(2)}) copy-start(s32[16]{0:T(128)} %param.7) | copy-start | bytes 196

commit v2 on v1

v2 whole, which is shorter than its diff:
```python
import functools
import math

import jax
import jax.numpy as jnp
from jax import lax
from jax.experimental import pallas as pl
from jax.experimental.pallas import tpu as pltpu
from jax.sharding import PartitionSpec as P

SCALE = math.sqrt(0.75)
ISO = 9.0 / (32.0 * SCALE)
DYAD = 3.0 * ISO
TOUCH = 2.0 * SCALE
TOUCH_INVERSE = 1.0 / TOUCH
SMALLEST = 1.1754944e-38

LANES = 128
SUBLANES = 8
GROUPS_AT_ONCE = 2
BLOCKS_AT_ONCE = 16
AXES = ("tgt", "src", "sub")
NEAR = 1.0 / ISO


def add_pairs(points_ref, source_ref, before_ref, total_ref):
    count = points_ref.shape[1]
    blocks = source_ref.shape[1] // LANES
    together = math.gcd(blocks, BLOCKS_AT_ONCE)
    groups = math.gcd(count // SUBLANES, GROUPS_AT_ONCE)
    rows = SUBLANES * groups

    def target_step(step, unused):
        first = pl.multiple_of(step * rows, rows)
        slices = [pl.ds(first + group * SUBLANES, SUBLANES) for group in range(groups)]
        points = [[points_ref[k, one, :] for k in range(3)] for one in slices]

        def source_step(number, carry):
            sums = [list(one) for one in carry]
            base = number * (together * LANES)
            for block in range(together):
                lanes = pl.ds(pl.multiple_of(base + block * LANES, LANES), LANES)
                x, y, z, fx, fy, fz = [
                    jnp.broadcast_to(source_ref[k : k + 1, lanes], (SUBLANES, LANES))
                    for k in range(6)
                ]
                for group in range(groups):
                    px, py, pz = points[group]
                    dx, dy, dz = px - x, py - y, pz - z
                    square = dx * dx + dy * dy + dz * dz
                    inverse = lax.rsqrt(jnp.maximum(square, SMALLEST))
                    held = jnp.minimum(inverse, TOUCH_INVERSE)
                    held_sq = held * held
                    iso = jnp.maximum(held * (held_sq + 2.0), NEAR - square * inverse)
                    along = dx * fx + dy * fy + dz * fz
                    dyad = (inverse * (held_sq * (2.0 / 3.0 - held_sq))) * along
                    one = sums[group]
                    sums[group] = [
                        one[0] + iso * fx,
                        one[1] + iso * fy,
                        one[2] + iso * fz,
                        one[3] + dyad * dx,
                        one[4] + dyad * dy,
                        one[5] + dyad * dz,
                    ]
            return tuple(tuple(one) for one in sums)

        zero = jnp.zeros((SUBLANES, LANES), jnp.float32)
        carry = tuple((zero,) * 6 for _ in range(groups))
        if blocks == together:
            carry = source_step(0, carry)
        else:
            carry = lax.fori_loop(0, blocks // together, source_step, carry)
        for group in range(groups):
            for k in range(3):
                value = ISO * carry[group][k] + DYAD * carry[group][3 + k]
                if before_ref is not None:
                    value = before_ref[k, slices[group], :] + value
                total_ref[k, slices[group], :] = value
        return unused

    lax.fori_loop(0, count // rows, target_step, 0)


def first_kernel(
    own_ref, position_ref, member_ref, owner_ref, points_ref, total_ref, match_ref, kept_ref
):
    count = own_ref.shape[1]
    for start in range(0, count, LANES):
        tile = jnp.concatenate(
            [own_ref[:, start : start + LANES], jnp.zeros((2, LANES), jnp.float32)], axis=0
        ).T
        for k in range(3):
            points_ref[k, start : start + LANES, :] = jnp.broadcast_to(
                tile[:, k : k + 1], (LANES, LANES)
            )
    aggregates = match_ref.shape[0]
    labels = lax.broadcasted_iota(jnp.int32, (aggregates, count), 0)
    member = jnp.where(labels == member_ref[...], 1.0, 0.0).astype(jnp.bfloat16)
    columns = lax.broadcasted_iota(jnp.int32, (aggregates, aggregates), 0)
    owner = jnp.where(columns == owner_ref[...], 1.0, 0.0).astype(jnp.bfloat16)
    match_ref[...] = jnp.dot(owner, member, preferred_element_type=jnp.float32).astype(
        jnp.bfloat16
    )
    kept_ref[...] = position_ref[...]
    add_pairs(points_ref, own_ref, None, total_ref)


def middle_kernel(points_ref, source_ref, before_ref, total_ref):
    add_pairs(points_ref, source_ref, before_ref, total_ref)


def last_kernel(
    points_ref, source_ref, before_ref, match_ref, kept_ref, velocity_ref, sums_ref, total
):
    add_pairs(points_ref, source_ref, before_ref, total)
    count = points_ref.shape[1]
    u = []
    for k in range(3):
        parts = [
            jnp.sum(total[k, start : start + LANES, :].T, axis=0, keepdims=True)
            for start in range(0, count, LANES)
        ]
        u.append(jnp.concatenate(parts, axis=1))
        velocity_ref[k : k + 1, :] = u[k]
    x = [kept_ref[k : k + 1, :] for k in range(3)]
    moments = jnp.concatenate(
        u
        + [
            x[1] * u[2] - x[2] * u[1],
            x[2] * u[0] - x[0] * u[2],
            x[0] * u[1] - x[1] * u[0],
        ]
        + x
        + [jnp.ones((1, count), jnp.float32), jnp.zeros((6, count), jnp.float32)],
        axis=0,
    )
    parts, rest = [], moments
    for _ in range(3):
        part = rest.astype(jnp.bfloat16)
        rest = rest - part.astype(jnp.float32)
        parts.append(part)
    summed = [
        lax.dot_general(
            part,
            match_ref[...],
            (((1,), (1,)), ((), ())),
            preferred_element_type=jnp.float32,
        )
        for part in parts
    ]
    sums_ref[...] = (summed[2] + summed[1]) + summed[0]


def rigid_kernel(first_ref, sums_ref, out_ref):
    columns = out_ref.shape[0]
    sums = sums_ref[...]
    lane = lax.broadcasted_iota(jnp.int32, sums.shape, 1)
    for column in range(columns):
        chosen = lane == first_ref[0] + column
        mine = jnp.sum(jnp.where(chosen, sums, 0.0), axis=1, keepdims=True)
        u = [mine[k : k + 1] for k in range(3)]
        moment = [mine[3 + k : 4 + k] for k in range(3)]
        centre = [mine[6 + k : 7 + k] / mine[9:10] for k in range(3)]
        torque = [
            moment[0] - (centre[1] * u[2] - centre[2] * u[1]),
            moment[1] - (centre[2] * u[0] - centre[0] * u[2]),
            moment[2] - (centre[0] * u[1] - centre[1] * u[0]),
        ]
        for row, value in enumerate(u + torque + centre):
            out_ref[column : column + 1, row : row + 1] = value


WHOLE = pl.BlockSpec(memory_space=pltpu.VMEM)


def call(kernel, shapes, arguments, pairs=0, scratch=(), specs=None, aliases={}):
    return pl.pallas_call(
        kernel,
        out_shape=[jax.ShapeDtypeStruct(shape, dtype) for shape, dtype in shapes],
        in_specs=specs or [WHOLE] * len(arguments),
        out_specs=[WHOLE] * len(shapes),
        scratch_shapes=list(scratch),
        input_output_aliases=aliases,
        compiler_params=pltpu.CompilerParams(vmem_limit_bytes=16 << 20),
        cost_estimate=pl.CostEstimate(
            flops=40 * pairs + 1000, bytes_accessed=1000, transcendentals=pairs
        ),
    )(*arguments)


def exchange_steps(mesh):
    steps = []
    for axis in reversed(AXES):
        size = mesh.shape[axis]
        reach = 1
        while reach < size:
            steps.append((axis, [(i, i ^ reach) for i in range(size)]))
            reach *= 2
    return steps


def on_device(steps, devices, positions, forces, membership, owner_slot):
    count, aggregates = positions.shape[1], owner_slot.shape[0]
    real = jnp.float32
    own = jnp.concatenate([SCALE * positions, forces], axis=0)
    wide = ((3, count, LANES), real)
    held, arrived = own, own
    for number, (axis, pairs) in enumerate(steps):
        coming = lax.ppermute(held, axis, pairs)
        if number == 0:
            points, total, match, kept = call(
                first_kernel,
                [wide, wide, ((aggregates, count), jnp.bfloat16), ((3, count), real)],
                (own, positions, membership[None, :], owner_slot[None, :]),
                pairs=count * count,
            )
        else:
            (total,) = call(
                middle_kernel,
                [wide],
                (points, arrived, total),
                pairs=count * arrived.shape[1],
                aliases={2: 0},
            )
        total, coming = lax.optimization_barrier((total, coming))
        held, arrived = jnp.concatenate([held, coming], axis=1), coming
    velocity, sums = call(
        last_kernel,
        [((3, count), real), ((16, aggregates), real)],
        (points, arrived, total, match, kept),
        pairs=count * arrived.shape[1],
        scratch=[pltpu.VMEM((3, count, LANES), real)],
    )
    for axis, pairs in steps:
        sums = sums + lax.ppermute(sums, axis, pairs)
    columns = aggregates // devices
    first = (lax.axis_index(AXES) * columns).astype(jnp.int32).reshape(1)
    (rigid,) = call(
        rigid_kernel,
        [((columns, 9), real)],
        (first, sums),
        specs=[pl.BlockSpec(memory_space=pltpu.SMEM), WHOLE],
    )
    return velocity, rigid.T


def solution(mesh):
    placed = (
        P(None, ("groups",) + AXES),
        P(None, ("groups",) + AXES),
        P(("groups",) + AXES),
        P("groups"),
    )
    devices = math.prod(mesh.shape[axis] for axis in AXES)
    return jax.shard_map(
        functools.partial(on_device, exchange_steps(mesh), devices),
        mesh=mesh,
        in_specs=placed,
        out_specs=(P(None, ("groups",) + AXES), P(None, ("groups",) + AXES)),
        check_vma=False,
    )
```

time: 38.5 us -> 35 us (0.909)
  Pallas kernels: 12.5 us -> 8.18 us
  local copies, waits for them, and re-layouts: 2.62 us -> 0.69 us
  waiting for transfers between devices: 7.57 us -> 9.24 us
  starting transfers between devices: 14.1 us -> 15.2 us
    pallas_call x7 -> x6, Pallas kernels: 12.5 us -> 8.18 us  [call(): pl.pallas_call(kernel, out_shape=[jax.ShapeDtypeStruct(shape, dtype) for...]
    ppermute x4, waiting for transfers between devices: 0.27 us -> 2.87 us  [on_device(): coming = lax.ppermute(held, axis, pairs)]
    unnamed x11 -> x8, local copies, waits for them, and re-layouts: 2.62 us -> 0.69 us
    ppermute x4, starting transfers between devices: 5.74 us -> 6.79 us  [on_device(): sums = sums + lax.ppermute(sums, axis, pairs)]
    ppermute x4, waiting for transfers between devices: 7.3 us -> 6.37 us  [on_device(): sums = sums + lax.ppermute(sums, axis, pairs)]
  transfers between devices with their start and end apart: 8 -> 8, of which waited for: 6 -> 7; matrix products, arithmetic and copies ran while one was open for 0% -> 0% of each run, Pallas kernels for 19% -> 11%
where the time goes in v2:
time: 35 us; the launch traced here: 34.7 us
  starting transfers between devices  15.2 us (43%)
  waiting for transfers between devices  9.24 us (26%)
  Pallas kernels  8.18 us (23%)
  other arithmetic  0.74 us (2%)
  between operations  0.7 us (2%)
  local copies, waits for them, and re-layouts  0.69 us (2%)
    ppermute x4, starting transfers between devices, on_device(): coming = lax.ppermute(held, axis, pairs)  8.38 us
    pallas_call x6, Pallas kernels, call(): pl.pallas_call(kernel, out_shape=[jax.ShapeDtypeStruct(shape, dtype) for...  8.18 us
    ppermute x4, starting transfers between devices, on_device(): sums = sums + lax.ppermute(sums, axis, pairs)  6.79 us
    ppermute x4, waiting for transfers between devices, on_device(): sums = sums + lax.ppermute(sums, axis, pairs)  6.37 us
    ppermute x4, waiting for transfers between devices, on_device(): coming = lax.ppermute(held, axis, pairs)  2.87 us
  transfers between devices with their start and end apart: 8, of which 7 were waited for; matrix products, arithmetic and copies ran while one was open for 0% of the time, Pallas kernels for 11%

profile of v2, /device:TPU:0, one launch (start us, length us, event | category | flops | bytes accessed | tf_op | source)
XLA Modules:
  0.0 34.7 jit_solution(11635010517060496881)
XLA Ops:
  0.6 0.0 copy-start.3
  0.6 0.7 %broadcast_multiply_fusion = f32[3,256]{1,0:T(4,128)S(1)} fusion(f32[3,256]{1,0:T(4,128)} %position_ref.1), kind=kLoop, calls=%fused_computation.4 | loop fusion | flops 768 | bytes 6144 | tf_op jit(solution)/shard_map/mul | solution.py:206
  1.3 0.0 copy-done.3
  1.3 0.0 copy-start
  1.3 0.6 %collective-permute-start = (f32[6,256]{1,0:T(8,128)S(1)}, f32[6,256]{1,0:T(8,128)S(1)}, u32[]{:S(2)}, u32[]{:S(2)}) collective-permute-start(f32[6,256]{1,0:T(8,128)S(1)} %pad_maximum_fusion.3.own_ref), channel_id=1, source_target_pairs={{0,1},{1,0},{2,3},{3,2},{4,5},{5,4},{6,7},{7,6},{8,9},{9,8},{10,11... | collective-permute-start | bytes 18440 | tf_op jit(solution)/shard_map/ppermute | solution.py:210
  1.9 0.0 copy-start.1
  1.9 0.0 copy-start.2
  1.9 0.1 copy-done
  2.0 0.6 %copy-done.1 = s32[256]{0:T(256)S(1)} copy-done((s32[256]{0:T(256)S(1)}, s32[256]{0:T(256)}, u32[]{:S(2)}) %copy-start.1) | copy-done | bytes 1048
  2.6 0.0 copy-done.2
  2.6 0.9 %shard_map.59 = (f32[3,256,128]{2,1,0:T(8,128)S(1)}, f32[3,256,128]{2,1,0:T(8,128)S(1)}, bf16[16,256]{1,0:T(8,128)(2,1)S(1)}, f32[3,256]{1,0:T(4,128)S(1)}) custom-call(f32[6,256]{1,0:T(8,128)S(1)} %pad_maximum_fusion.3.own_ref, f32[3,256]{1,0:T(4,128)S(1)} %copy-done, s32[1,256]{1,0:T(1,128)S(1)} %bitcast.4, s32[1,16]{1,0:T(1,128)S(1)} %bitcast.5), custom_call_target="tpu_custom_call" | custom-call | flops 2622440 | bytes 1000 | tf_op jit(solution)/shard_map/pallas_call | solution.py:178
  3.5 0.0 collective-permute-done.source_ref
  3.5 2.6 %collective-permute-start.1 = (f32[6,512]{1,0:T(8,128)S(1)}, f32[6,512]{1,0:T(8,128)S(1)}, u32[]{:S(2)}, u32[]{:S(2)}) collective-permute-start(f32[6,512]{1,0:T(8,128)S(1)} %pad_maximum_fusion.2), channel_id=1, source_target_pairs={{0,2},{2,0},{1,3},{3,1},{4,6},{6,4},{5,7},{7,5},{8,10},{10,8},{9,1... | collective-permute-start | bytes 36872 | tf_op jit(solution)/shard_map/ppermute | solution.py:210
  6.1 0.6 %shard_map.60.before_ref = f32[3,256,128]{2,1,0:T(8,128)S(1)} custom-call(f32[3,256,128]{2,1,0:T(8,128)S(1)} %get-tuple-element.16.points_ref, f32[6,256]{1,0:T(8,128)S(1)} %collective-permute-done.source_ref, f32[3,256,128]{2,1,0:T(8,128)S(1)} %get-tuple-element.19.before_ref), custom_call_target="tpu_custom_call", output_to_operand_aliasing={{}: (2, {})} | custom-call | flops 2622440 | bytes 1000 | tf_op jit(solution)/shard_map/pallas_call | solution.py:178
  6.7 1.1 %collective-permute-done.1.source_ref = f32[6,512]{1,0:T(8,128)S(1)} collective-permute-done((f32[6,512]{1,0:T(8,128)S(1)}, f32[6,512]{1,0:T(8,128)S(1)}, u32[]{:S(2)}, u32[]{:S(2)}) %collective-permute-start.1) | collective-permute-done | bytes 12320 | tf_op jit(solution)/shard_map/ppermute | solution.py:210
  7.8 2.2 %collective-permute-start.2 = (f32[6,1024]{1,0:T(8,128)S(1)}, f32[6,1024]{1,0:T(8,128)S(1)}, u32[]{:S(2)}, u32[]{:S(2)}) collective-permute-start(f32[6,1024]{1,0:T(8,128)S(1)} %pad_maximum_fusion.1), channel_id=1, source_target_pairs={{0,4},{4,0},{8,12},{12,8},{1,5},{5,1},{9,13},{13,9},{2,6},{6,2},{1... | collective-permute-start | bytes 73736 | tf_op jit(solution)/shard_map/ppermute | solution.py:210
  10.0 0.9 %shard_map.61.before_ref = f32[3,256,128]{2,1,0:T(8,128)S(1)} custom-call(f32[3,256,128]{2,1,0:T(8,128)S(1)} %get-tuple-element.16.points_ref, f32[6,512]{1,0:T(8,128)S(1)} %collective-permute-done.1.source_ref, f32[3,256,128]{2,1,0:T(8,128)S(1)} %shard_map.60.before_ref), custom_call_target="tpu_custom_call", output_to_operand_aliasing={{}: (2, {})} | custom-call | flops 5243880 | bytes 1000 | tf_op jit(solution)/shard_map/pallas_call | solution.py:178
  10.8 1.0 %collective-permute-done.2.source_ref = f32[6,1024]{1,0:T(8,128)S(1)} collective-permute-done((f32[6,1024]{1,0:T(8,128)S(1)}, f32[6,1024]{1,0:T(8,128)S(1)}, u32[]{:S(2)}, u32[]{:S(2)}) %collective-permute-start.2) | collective-permute-done | bytes 24608 | tf_op jit(solution)/shard_map/ppermute | solution.py:210
  11.9 3.1 %collective-permute-start.3 = (f32[6,2048]{1,0:T(8,128)S(1)}, f32[6,2048]{1,0:T(8,128)S(1)}, u32[]{:S(2)}, u32[]{:S(2)}) collective-permute-start(f32[6,2048]{1,0:T(8,128)S(1)} %pad_maximum_fusion), channel_id=1, source_target_pairs={{0,8},{4,12},{8,0},{12,4},{1,9},{5,13},{9,1},{13,5},{2,10},{6,14},... | collective-permute-start | bytes 147464 | tf_op jit(solution)/shard_map/ppermute | solution.py:210
  15.0 1.5 %shard_map.62.before_ref = f32[3,256,128]{2,1,0:T(8,128)S(1)} custom-call(f32[3,256,128]{2,1,0:T(8,128)S(1)} %get-tuple-element.16.points_ref, f32[6,1024]{1,0:T(8,128)S(1)} %collective-permute-done.2.source_ref, f32[3,256,128]{2,1,0:T(8,128)S(1)} %shard_map.61.before_ref), custom_call_target="tpu_custom_call", output_to_operand_aliasing={{}: (2, {})} | custom-call | flops 10486760 | bytes 1000 | tf_op jit(solution)/shard_map/pallas_call | solution.py:178
  16.4 0.8 %collective-permute-done.3.source_ref = f32[6,2048]{1,0:T(8,128)S(1)} collective-permute-done((f32[6,2048]{1,0:T(8,128)S(1)}, f32[6,2048]{1,0:T(8,128)S(1)}, u32[]{:S(2)}, u32[]{:S(2)}) %collective-permute-start.3) | collective-permute-done | bytes 49184 | tf_op jit(solution)/shard_map/ppermute | solution.py:210
  17.2 3.6 %shard_map.63 = (f32[3,256]{1,0:T(4,128)}, f32[16,16]{1,0:T(8,128)S(1)}) custom-call(f32[3,256,128]{2,1,0:T(8,128)S(1)} %get-tuple-element.16.points_ref, f32[6,2048]{1,0:T(8,128)S(1)} %collective-permute-done.3.source_ref, f32[3,256,128]{2,1,0:T(8,128)S(1)} %shard_map.62.before_ref, bf16[16,256]{1,0:T(8,128)(2,1)S(1)} %get-tuple-element.26.match_ref, ...), custom_call_target="tpu_custom_call" | custom-call | flops 20972520 | bytes 1000 | tf_op jit(solution)/shard_map/pallas_call | solution.py:178
  20.8 0.0 collective-permute-start.4
  20.8 1.2 %collective-permute-done.4 = f32[16,16]{1,0:T(8,128)S(1)} collective-permute-done((f32[16,16]{1,0:T(8,128)S(1)}, f32[16,16]{1,0:T(8,128)S(1)}, u32[]{:S(2)}, u32[]{:S(2)}) %collective-permute-start.4) | collective-permute-done | bytes 1056 | tf_op jit(solution)/shard_map/ppermute | solution.py:236
  22.0 1.8 %collective-permute-start.5 = (f32[16,16]{1,0:T(8,128)S(1)}, f32[16,16]{1,0:T(8,128)S(1)}, u32[]{:S(2)}, u32[]{:S(2)}) collective-permute-start(f32[16,16]{1,0:T(8,128)S(1)} %add.20), channel_id=1, source_target_pairs={{0,2},{2,0},{1,3},{3,1},{4,6},{6,4},{5,7},{7,5},{8,10},{10,8},{9,1... | collective-permute-start | bytes 3080 | tf_op jit(solution)/shard_map/ppermute | solution.py:236
  23.8 1.8 %collective-permute-done.5 = f32[16,16]{1,0:T(8,128)S(1)} collective-permute-done((f32[16,16]{1,0:T(8,128)S(1)}, f32[16,16]{1,0:T(8,128)S(1)}, u32[]{:S(2)}, u32[]{:S(2)}) %collective-permute-start.5) | collective-permute-done | bytes 1056 | tf_op jit(solution)/shard_map/ppermute | solution.py:236
  25.7 1.9 %collective-permute-start.6 = (f32[16,16]{1,0:T(8,128)S(1)}, f32[16,16]{1,0:T(8,128)S(1)}, u32[]{:S(2)}, u32[]{:S(2)}) collective-permute-start(f32[16,16]{1,0:T(8,128)S(1)} %add.21), channel_id=1, source_target_pairs={{0,4},{4,0},{8,12},{12,8},{1,5},{5,1},{9,13},{13,9},{2,6},{6,2},{1... | collective-permute-start | bytes 3080 | tf_op jit(solution)/shard_map/ppermute | solution.py:236
  27.6 1.7 %collective-permute-done.6 = f32[16,16]{1,0:T(8,128)S(1)} collective-permute-done((f32[16,16]{1,0:T(8,128)S(1)}, f32[16,16]{1,0:T(8,128)S(1)}, u32[]{:S(2)}, u32[]{:S(2)}) %collective-permute-start.6) | collective-permute-done | bytes 1056 | tf_op jit(solution)/shard_map/ppermute | solution.py:236
  29.3 3.1 %collective-permute-start.7 = (f32[16,16]{1,0:T(8,128)S(1)}, f32[16,16]{1,0:T(8,128)S(1)}, u32[]{:S(2)}, u32[]{:S(2)}) collective-permute-start(f32[16,16]{1,0:T(8,128)S(1)} %add.22), channel_id=1, source_target_pairs={{0,8},{4,12},{8,0},{12,4},{1,9},{5,13},{9,1},{13,5},{2,10},{6,14},... | collective-permute-start | bytes 3080 | tf_op jit(solution)/shard_map/ppermute | solution.py:236
  32.4 1.6 %collective-permute-done.7 = f32[16,16]{1,0:T(8,128)S(1)} collective-permute-done((f32[16,16]{1,0:T(8,128)S(1)}, f32[16,16]{1,0:T(8,128)S(1)}, u32[]{:S(2)}, u32[]{:S(2)}) %collective-permute-start.7) | collective-permute-done | bytes 1056 | tf_op jit(solution)/shard_map/ppermute | solution.py:236
  34.0 0.7 %shard_map.64 = f32[1,9]{1,0:T(1,128)} custom-call(s32[1]{0:T(128)} %bitcast.2.first_ref, f32[16,16]{1,0:T(8,128)S(1)} %add.23.sums_ref), custom_call_target="tpu_custom_call" | custom-call | flops 1000 | bytes 1000 | tf_op jit(solution)/shard_map/pallas_call | solution.py:178
  (8 shorter events, 0.0 us)
Async XLA Ops:
  0.6 0.7 %copy-start.3 = (f32[3,256]{1,0:T(4,128)S(1)}, f32[3,256]{1,0:T(4,128)}, u32[]{:S(2)}) copy-start(f32[3,256]{1,0:T(4,128)} %param.5) | copy-start | bytes 9220
  1.3 0.7 %copy-start = (f32[3,256]{1,0:T(4,128)S(1)}, f32[3,256]{1,0:T(4,128)}, u32[]{:S(2)}) copy-start(f32[3,256]{1,0:T(4,128)} %position_ref.1) | copy-start | bytes 9220
  1.3 2.1 %collective-permute-start = (f32[6,256]{1,0:T(8,128)S(1)}, f32[6,256]{1,0:T(8,128)S(1)}, u32[]{:S(2)}, u32[]{:S(2)}) collective-permute-start(f32[6,256]{1,0:T(8,128)S(1)} %pad_maximum_fusion.3.own_ref), channel_id=1, source_target_pairs={{0,1},{1,0},{2,3},{3,2},{4,5},{5,4},{6,7},{7,6},{8,9},{9,8},{10,11... | collective-permute-start | bytes 18440 | tf_op jit(solution)/shard_map/ppermute | solution.py:210
  1.9 0.7 %copy-start.1 = (s32[256]{0:T(256)S(1)}, s32[256]{0:T(256)}, u32[]{:S(2)}) copy-start(s32[256]{0:T(256)} %param.6) | copy-start | bytes 3076
  1.9 0.7 %copy-start.2 = (s32[16]{0:T(128)S(1)}, s32[16]{0:T(128)}, u32[]{:S(2)}) copy-start(s32[16]{0:T(128)} %param.7) | copy-start | bytes 196
  3.5 4.3 %collective-permute-start.1 = (f32[6,512]{1,0:T(8,128)S(1)}, f32[6,512]{1,0:T(8,128)S(1)}, u32[]{:S(2)}, u32[]{:S(2)}) collective-permute-start(f32[6,512]{1,0:T(8,128)S(1)} %pad_maximum_fusion.2), channel_id=1, source_target_pairs={{0,2},{2,0},{1,3},{3,1},{4,6},{6,4},{5,7},{7,5},{8,10},{10,8},{9,1... | collective-permute-start | bytes 36872 | tf_op jit(solution)/shard_map/ppermute | solution.py:210
  7.8 4.1 %collective-permute-start.2 = (f32[6,1024]{1,0:T(8,128)S(1)}, f32[6,1024]{1,0:T(8,128)S(1)}, u32[]{:S(2)}, u32[]{:S(2)}) collective-permute-start(f32[6,1024]{1,0:T(8,128)S(1)} %pad_maximum_fusion.1), channel_id=1, source_target_pairs={{0,4},{4,0},{8,12},{12,8},{1,5},{5,1},{9,13},{13,9},{2,6},{6,2},{1... | collective-permute-start | bytes 73736 | tf_op jit(solution)/shard_map/ppermute | solution.py:210
  11.9 5.3 %collective-permute-start.3 = (f32[6,2048]{1,0:T(8,128)S(1)}, f32[6,2048]{1,0:T(8,128)S(1)}, u32[]{:S(2)}, u32[]{:S(2)}) collective-permute-start(f32[6,2048]{1,0:T(8,128)S(1)} %pad_maximum_fusion), channel_id=1, source_target_pairs={{0,8},{4,12},{8,0},{12,4},{1,9},{5,13},{9,1},{13,5},{2,10},{6,14},... | collective-permute-start | bytes 147464 | tf_op jit(solution)/shard_map/ppermute | solution.py:210
  20.8 1.2 %collective-permute-start.4 = (f32[16,16]{1,0:T(8,128)S(1)}, f32[16,16]{1,0:T(8,128)S(1)}, u32[]{:S(2)}, u32[]{:S(2)}) collective-permute-start(f32[16,16]{1,0:T(8,128)S(1)} %get-tuple-element.29), channel_id=1, source_target_pairs={{0,1},{1,0},{2,3},{3,2},{4,5},{5,4},{6,7},{7,6},{8,9},{9,8},{10,11... | collective-permute-start | bytes 3080 | tf_op jit(solution)/shard_map/ppermute | solution.py:236
  22.0 3.7 %collective-permute-start.5 = (f32[16,16]{1,0:T(8,128)S(1)}, f32[16,16]{1,0:T(8,128)S(1)}, u32[]{:S(2)}, u32[]{:S(2)}) collective-permute-start(f32[16,16]{1,0:T(8,128)S(1)} %add.20), channel_id=1, source_target_pairs={{0,2},{2,0},{1,3},{3,1},{4,6},{6,4},{5,7},{7,5},{8,10},{10,8},{9,1... | collective-permute-start | bytes 3080 | tf_op jit(solution)/shard_map/ppermute | solution.py:236
  25.7 3.7 %collective-permute-start.6 = (f32[16,16]{1,0:T(8,128)S(1)}, f32[16,16]{1,0:T(8,128)S(1)}, u32[]{:S(2)}, u32[]{:S(2)}) collective-permute-start(f32[16,16]{1,0:T(8,128)S(1)} %add.21), channel_id=1, source_target_pairs={{0,4},{4,0},{8,12},{12,8},{1,5},{5,1},{9,13},{13,9},{2,6},{6,2},{1... | collective-permute-start | bytes 3080 | tf_op jit(solution)/shard_map/ppermute | solution.py:236
  29.3 4.7 %collective-permute-start.7 = (f32[16,16]{1,0:T(8,128)S(1)}, f32[16,16]{1,0:T(8,128)S(1)}, u32[]{:S(2)}, u32[]{:S(2)}) collective-permute-start(f32[16,16]{1,0:T(8,128)S(1)} %add.22), channel_id=1, source_target_pairs={{0,8},{4,12},{8,0},{12,4},{1,9},{5,13},{9,1},{13,5},{2,10},{6,14},... | collective-permute-start | bytes 3080 | tf_op jit(solution)/shard_map/ppermute | solution.py:236

commit v3 on v2

v3 whole, which is shorter than its diff:
```python
import functools
import math

import jax
import jax.numpy as jnp
from jax import lax
from jax.experimental import pallas as pl
from jax.experimental.pallas import tpu as pltpu
from jax.sharding import PartitionSpec as P

SCALE = math.sqrt(0.75)
ISO = 9.0 / (32.0 * SCALE)
DYAD = 3.0 * ISO
NEAR = 1.0 / ISO
TOUCH_INVERSE = 1.0 / (2.0 * SCALE)
SMALLEST = 1.1754944e-38

LANES = 128
SUBLANES = 8
GROUPS_AT_ONCE = 8
BLOCKS_AT_ONCE = 16
SUM_ROWS = 16
SOURCE_AXES = ("tgt",)
TARGET_AXES = ("sub", "src")
AXES = ("tgt", "src", "sub")


def add_pairs(points_ref, source_ref, before_ref, total_ref, scaled):
    count = points_ref.shape[1]
    blocks = source_ref.shape[1] // LANES
    together = math.gcd(blocks, BLOCKS_AT_ONCE)
    groups = math.gcd(count // SUBLANES, GROUPS_AT_ONCE)
    rows = SUBLANES * groups
    scaled[0:3, :] = SCALE * source_ref[0:3, :]
    scaled[3:6, :] = source_ref[3:6, :]

    def target_step(step, unused):
        first = pl.multiple_of(step * rows, rows)
        slices = [pl.ds(first + group * SUBLANES, SUBLANES) for group in range(groups)]
        points = [[points_ref[k, one, :] for k in range(3)] for one in slices]

        def source_step(number, carry):
            sums = [list(one) for one in carry]
            base = number * (together * LANES)
            for block in range(together):
                lanes = pl.ds(pl.multiple_of(base + block * LANES, LANES), LANES)
                x, y, z, fx, fy, fz = [
                    jnp.broadcast_to(scaled[k : k + 1, lanes], (SUBLANES, LANES))
                    for k in range(6)
                ]
                for group in range(groups):
                    px, py, pz = points[group]
                    dx, dy, dz = px - x, py - y, pz - z
                    square = dx * dx + dy * dy + dz * dz
                    inverse = lax.rsqrt(jnp.maximum(square, SMALLEST))
                    held = jnp.minimum(inverse, TOUCH_INVERSE)
                    held_sq = held * held
                    iso = jnp.maximum(held * (held_sq + 2.0), NEAR - square * inverse)
                    along = dx * fx + dy * fy + dz * fz
                    dyad = (inverse * (held_sq * (2.0 / 3.0 - held_sq))) * along
                    one = sums[group]
                    sums[group] = [
                        one[0] + iso * fx,
                        one[1] + iso * fy,
                        one[2] + iso * fz,
                        one[3] + dyad * dx,
                        one[4] + dyad * dy,
                        one[5] + dyad * dz,
                    ]
            return tuple(tuple(one) for one in sums)

        zero = jnp.zeros((SUBLANES, LANES), jnp.float32)
        carry = tuple((zero,) * 6 for _ in range(groups))
        if blocks == together:
            carry = source_step(0, carry)
        else:
            carry = lax.fori_loop(0, blocks // together, source_step, carry)
        for group in range(groups):
            for k in range(3):
                value = ISO * carry[group][k] + DYAD * carry[group][3 + k]
                if before_ref is not None:
                    value = before_ref[k, slices[group], :] + value
                total_ref[k, slices[group], :] = value
        return unused

    lax.fori_loop(0, count // rows, target_step, 0)


def head_kernel(
    position_in,
    force_in,
    member_in,
    owner_in,
    source_ref,
    target_ref,
    owner_ref,
    position,
    force,
    member,
    arrived,
):
    moves = [(position_in, position), (force_in, force), (member_in, member), (owner_in, owner_ref)]
    copies = [
        pltpu.make_async_copy(there, here, arrived.at[number])
        for number, (there, here) in enumerate(moves)
    ]
    for copy in copies:
        copy.start()
    for copy in copies:
        copy.wait()
    source_ref[0:3, :] = position[...]
    source_ref[3:6, :] = force[...]
    target_ref[0:3, :] = position[...]
    target_ref[3:4, :] = member[...].astype(jnp.float32)


def first_kernel(target_ref, source_ref, owner_ref, points_ref, total_ref, match_ref, scaled):
    count = target_ref.shape[1]
    for start in range(0, count, LANES):
        tile = jnp.concatenate(
            [target_ref[:, start : start + LANES], jnp.zeros((4, LANES), jnp.float32)], axis=0
        )
        turned = (SCALE * tile).T
        for k in range(3):
            points_ref[k, start : start + LANES, :] = jnp.broadcast_to(
                turned[:, k : k + 1], (LANES, LANES)
            )
    aggregates = match_ref.shape[0]
    labels = lax.broadcasted_iota(jnp.int32, (aggregates, count), 0)
    member = jnp.where(labels == target_ref[3:4, :].astype(jnp.int32), 1.0, 0.0)
    columns = lax.broadcasted_iota(jnp.int32, (aggregates, aggregates), 0)
    owner = jnp.where(columns == owner_ref[...], 1.0, 0.0)
    match_ref[...] = jnp.dot(
        owner.astype(jnp.bfloat16),
        member.astype(jnp.bfloat16),
        preferred_element_type=jnp.float32,
    ).astype(jnp.bfloat16)
    add_pairs(points_ref, source_ref, None, total_ref, scaled)


def last_kernel(
    unit_count,
    points_ref,
    source_ref,
    before_ref,
    match_ref,
    target_ref,
    keep_ref,
    send_ref,
    total,
    scaled,
):
    add_pairs(points_ref, source_ref, before_ref, total, scaled)
    count = points_ref.shape[1]
    aggregates = match_ref.shape[0]
    per_unit, units = unit_count // LANES, count // unit_count
    first_row, unit_rows = sum_rows(aggregates), velocity_rows(unit_count)
    keep_ref[...] = jnp.zeros_like(keep_ref)
    send_ref[...] = jnp.zeros_like(send_ref)
    u = []
    for k in range(3):
        parts = []
        for tile in range(count // LANES):
            part = jnp.sum(
                total[k, tile * LANES : (tile + 1) * LANES, :].T, axis=0, keepdims=True
            )
            parts.append(part)
            unit, block = divmod(tile, per_unit)
            packed, unit = (keep_ref, unit) if unit < units // 2 else (send_ref, unit - units // 2)
            row = first_row + unit * unit_rows + k * per_unit + block
            packed[row : row + 1, :] = part
        u.append(jnp.concatenate(parts, axis=1))
    x = [target_ref[k : k + 1, :] for k in range(3)]
    moments = jnp.concatenate(
        u
        + [
            x[1] * u[2] - x[2] * u[1],
            x[2] * u[0] - x[0] * u[2],
            x[0] * u[1] - x[1] * u[0],
        ]
        + x
        + [jnp.ones((1, count), jnp.float32), jnp.zeros((SUM_ROWS - 10, count), jnp.float32)],
        axis=0,
    )
    parts, rest = [], moments
    for _ in range(3):
        part = rest.astype(jnp.bfloat16)
        rest = rest - part.astype(jnp.float32)
        parts.append(part)
    summed = [
        lax.dot_general(
            part,
            match_ref[...],
            (((1,), (1,)), ((), ())),
            preferred_element_type=jnp.float32,
        )
        for part in parts
    ]
    sums = (summed[2] + summed[1]) + summed[0]
    for chunk, start in enumerate(range(0, aggregates, LANES)):
        width = min(LANES, aggregates - start)
        for packed in (keep_ref, send_ref):
            packed[chunk * SUM_ROWS : (chunk + 1) * SUM_ROWS, 0:width] = sums[
                :, start : start + width
            ]


def velocity_kernel(packed_ref, out_ref):
    per_unit = out_ref.shape[1] // LANES
    for k in range(3):
        for block in range(per_unit):
            row = k * per_unit + block
            out_ref[k : k + 1, block * LANES : (block + 1) * LANES] = packed_ref[row : row + 1, :]


def rigid_kernel(first_ref, sums_ref, out_ref):
    columns = out_ref.shape[0]
    lane = lax.broadcasted_iota(jnp.int32, (SUM_ROWS, LANES), 1)
    for column in range(columns):
        wanted = first_ref[0] + column
        mine = jnp.zeros((SUM_ROWS, LANES), jnp.float32)
        for chunk in range(sums_ref.shape[0] // SUM_ROWS):
            sums = sums_ref[chunk * SUM_ROWS : (chunk + 1) * SUM_ROWS, :]
            mine = jnp.where(lane + chunk * LANES == wanted, sums, mine)
        mine = jnp.where(lane == wanted % LANES, mine, 0.0)
        mine = jnp.sum(mine, axis=1, keepdims=True)
        u = [mine[k : k + 1] for k in range(3)]
        moment = [mine[3 + k : 4 + k] for k in range(3)]
        centre = [mine[6 + k : 7 + k] / mine[9:10] for k in range(3)]
        torque = [
            moment[0] - (centre[1] * u[2] - centre[2] * u[1]),
            moment[1] - (centre[2] * u[0] - centre[0] * u[2]),
            moment[2] - (centre[0] * u[1] - centre[1] * u[0]),
        ]
        for row, value in enumerate(u + torque + centre):
            out_ref[column : column + 1, row : row + 1] = value


def sum_rows(aggregates):
    return SUM_ROWS * pl.cdiv(aggregates, LANES)


def velocity_rows(count):
    return SUBLANES * pl.cdiv(3 * (count // LANES), SUBLANES)


WHOLE = pl.BlockSpec(memory_space=pltpu.VMEM)


def call(kernel, shapes, arguments, pairs=0, scratch=(), specs=None, vmem=8 << 20):
    return pl.pallas_call(
        kernel,
        out_shape=[jax.ShapeDtypeStruct(shape, dtype) for shape, dtype in shapes],
        in_specs=specs or [WHOLE] * len(arguments),
        out_specs=[WHOLE] * len(shapes),
        scratch_shapes=list(scratch),
        compiler_params=pltpu.CompilerParams(vmem_limit_bytes=vmem),
        cost_estimate=pl.CostEstimate(
            flops=40 * pairs + 1000, bytes_accessed=1000, transcendentals=pairs
        ),
    )(*arguments)


def doubling(mesh, axes):
    steps = []
    for axis in axes:
        size = mesh.shape[axis]
        reach = 1
        while reach < size:
            steps.append((axis, [(i, i ^ reach) for i in range(size)]))
            reach *= 2
    return steps


def on_device(source_steps, target_steps, devices, positions, forces, membership, owner_slot):
    count, aggregates = positions.shape[1], owner_slot.shape[0]
    real = jnp.float32
    sources, targets, owner = call(
        head_kernel,
        [((6, count), real), ((4, count), real), ((1, aggregates), jnp.int32)],
        [
            pltpu.with_memory_space_constraint(one, pltpu.HBM)
            for one in (positions, forces, membership[None, :], owner_slot[None, :])
        ],
        scratch=[
            pltpu.VMEM((3, count), real),
            pltpu.VMEM((3, count), real),
            pltpu.VMEM((1, count), jnp.int32),
            pltpu.SemaphoreType.DMA((4,)),
        ],
        specs=[pl.BlockSpec(memory_space=pltpu.HBM)] * 4,
    )

    coming = None
    for number in range(max(len(source_steps), len(target_steps))):
        if number < len(target_steps):
            axis, pairs = target_steps[number]
            targets = jnp.concatenate([targets, lax.ppermute(targets, axis, pairs)], axis=1)
        if number < len(source_steps):
            if coming is not None:
                sources = jnp.concatenate([sources, coming], axis=1)
            axis, pairs = source_steps[number]
            coming = lax.ppermute(sources, axis, pairs)
    seen = targets.shape[1]
    wide = ((3, seen, LANES), real)
    scaled = pltpu.VMEM((SUBLANES, sources.shape[1]), real)
    vmem = (8 << 20) + 4 * (4 * 3 * seen * LANES)
    points, total, match = call(
        first_kernel,
        [wide, wide, ((aggregates, seen), jnp.bfloat16)],
        (targets, sources, owner),
        pairs=seen * sources.shape[1],
        scratch=[scaled],
        vmem=vmem,
    )
    total, coming = lax.optimization_barrier((total, coming))
    first_row, units = sum_rows(aggregates), seen // count
    unit_rows = velocity_rows(count)
    packed = ((first_row + units // 2 * unit_rows, LANES), real)
    keep, send = call(
        functools.partial(last_kernel, count),
        [packed, packed],
        (points, coming, total, match, targets),
        pairs=seen * coming.shape[1],
        scratch=[pltpu.VMEM((3, seen, LANES), real), scaled],
        vmem=vmem,
    )

    for axis, pairs in reversed(target_steps):
        if keep is None:
            half = (both.shape[0] - first_row) // 2
            keep = both[: first_row + half]
            send = jnp.concatenate([both[:first_row], both[first_row + half :]], axis=0)
        both = keep + lax.ppermute(send, axis, pairs)
        keep = None
    sums, mine = both[:first_row], both[first_row:]
    for number, (axis, pairs) in enumerate(source_steps):
        coming = lax.ppermute(sums, axis, pairs)
        if number == 0:
            (velocity,) = call(velocity_kernel, [((3, count), real)], (mine,))
            velocity, coming = lax.optimization_barrier((velocity, coming))
        sums = sums + coming
    columns = aggregates // devices
    first = (lax.axis_index(AXES) * columns).astype(jnp.int32).reshape(1)
    (rigid,) = call(
        rigid_kernel,
        [((columns, 9), real)],
        (first, sums),
        specs=[pl.BlockSpec(memory_space=pltpu.SMEM), WHOLE],
    )
    return velocity, rigid.T


def solution(mesh):
    placed = (
        P(None, ("groups",) + AXES),
        P(None, ("groups",) + AXES),
        P(("groups",) + AXES),
        P("groups"),
    )
    devices = math.prod(mesh.shape[axis] for axis in AXES)
    return jax.shard_map(
        functools.partial(
            on_device, doubling(mesh, SOURCE_AXES), doubling(mesh, TARGET_AXES), devices
        ),
        mesh=mesh,
        in_specs=placed,
        out_specs=(P(None, ("groups",) + AXES), P(None, ("groups",) + AXES)),
        check_vma=False,
    )
```

time: 35 us -> 30.4 us (0.87)
  starting transfers between devices: 15.2 us -> 12.6 us
  waiting for transfers between devices: 9.24 us -> 7.84 us
  Pallas kernels: 8.18 us -> 9.05 us
  other arithmetic: 0.74 us -> 0.02 us
  local copies, waits for them, and re-layouts: 0.69 us -> 0.03 us
    ppermute x8, starting transfers between devices: 15.2 us -> 12.6 us  [the longest x2 5.67 us: on_device(): coming = lax.ppermute(sources, axis, pairs)]
    ppermute x8, waiting for transfers between devices: 9.24 us -> 7.84 us  [the longest x2 4.37 us: on_device(): coming = lax.ppermute(sums, axis, pairs)]
    pallas_call x6 -> x5, Pallas kernels: 8.18 us -> 9.05 us  [call(): pl.pallas_call(kernel, out_shape=[jax.ShapeDtypeStruct(shape, dtype) for...]
    mul x1 -> x0, other arithmetic: 0.7 us -> none  [on_device(): own = jnp.concatenate([SCALE * positions, forces], axis=0)]
    unnamed x8 -> x3, local copies, waits for them, and re-layouts: 0.69 us -> 0.01 us
  transfers between devices with their start and end apart: 8 -> 8, of which waited for: 7 -> 5; matrix products, arithmetic and copies ran while one was open for 0% -> 0% of each run, Pallas kernels for 11% -> 14%
where the time goes in v3:
time: 30.4 us; the launch traced here: 30.2 us
  starting transfers between devices  12.6 us (41%)
  Pallas kernels  9.05 us (30%)
  waiting for transfers between devices  7.84 us (26%)
  between operations  0.69 us (2%)
    pallas_call x5, Pallas kernels, call(): pl.pallas_call(kernel, out_shape=[jax.ShapeDtypeStruct(shape, dtype) for...  9.05 us
    ppermute x2, starting transfers between devices, on_device(): coming = lax.ppermute(sources, axis, pairs)  5.67 us
    ppermute x2, waiting for transfers between devices, on_device(): coming = lax.ppermute(sums, axis, pairs)  4.37 us
    ppermute x2, waiting for transfers between devices, on_device(): both = keep + lax.ppermute(send, axis, pairs)  3.41 us
    ppermute x2, starting transfers between devices, on_device(): coming = lax.ppermute(sums, axis, pairs)  3.23 us
    ppermute x2, starting transfers between devices, on_device(): lax.ppermute(targets, axis, pairs)  2.11 us
    ppermute x2, starting transfers between devices, on_device(): both = keep + lax.ppermute(send, axis, pairs)  1.59 us
  transfers between devices with their start and end apart: 8, of which 5 were waited for; matrix products, arithmetic and copies ran while one was open for 0% of the time, Pallas kernels for 14%

profile of v3, /device:TPU:0, one launch (start us, length us, event | category | flops | bytes accessed | tf_op | source)
XLA Modules:
  0.0 30.2 jit_solution(8056403699257886713)
XLA Ops:
  0.6 0.8 %shard_map.59 = (f32[6,256]{1,0:T(8,128)S(1)}, f32[4,256]{1,0:T(4,128)S(1)}, s32[1,16]{1,0:T(1,128)S(1)}) custom-call(f32[3,256]{1,0:T(4,128)} %position_in.1, f32[3,256]{1,0:T(4,128)} %force_in.1, s32[1,256]{1,0:T(1,128)} %bitcast.4, s32[1,16]{1,0:T(1,128)} %bitcast.5), custom_call_target="tpu_custom_call" | custom-call | flops 1000 | bytes 1000 | tf_op jit(solution)/shard_map/pallas_call | solution.py:251
  1.4 0.6 %collective-permute-start = (f32[4,256]{1,0:T(4,128)S(1)}, f32[4,256]{1,0:T(4,128)S(1)}, u32[]{:S(2)}, u32[]{:S(2)}) collective-permute-start(f32[4,256]{1,0:T(4,128)S(1)} %get-tuple-element.14), channel_id=1, source_target_pairs={{0,1},{1,0},{2,3},{3,2},{4,5},{5,4},{6,7},{7,6},{8,9},{9,8},{10,11... | collective-permute-start | bytes 12296 | tf_op jit(solution)/shard_map/ppermute | solution.py:298
  1.9 2.6 %collective-permute-start.2 = (f32[6,256]{1,0:T(8,128)S(1)}, f32[6,256]{1,0:T(8,128)S(1)}, u32[]{:S(2)}, u32[]{:S(2)}) collective-permute-start(f32[6,256]{1,0:T(8,128)S(1)} %get-tuple-element.15), channel_id=1, source_target_pairs={{0,4},{4,0},{8,12},{12,8},{1,5},{5,1},{9,13},{13,9},{2,6},{6,2},{1... | collective-permute-start | bytes 18440 | tf_op jit(solution)/shard_map/ppermute | solution.py:303
  4.6 0.0 collective-permute-done
  4.6 1.6 %collective-permute-start.1 = (f32[4,512]{1,0:T(4,128)S(1)}, f32[4,512]{1,0:T(4,128)S(1)}, u32[]{:S(2)}, u32[]{:S(2)}) collective-permute-start(f32[4,512]{1,0:T(4,128)S(1)} %pad_maximum_fusion.1), channel_id=1, source_target_pairs={{0,2},{2,0},{1,3},{3,1},{4,6},{6,4},{5,7},{7,5},{8,10},{10,8},{9,1... | collective-permute-start | bytes 24584 | tf_op jit(solution)/shard_map/ppermute | solution.py:298
  6.2 0.1 collective-permute-done.2
  6.2 3.0 %collective-permute-start.3 = (f32[6,512]{1,0:T(8,128)S(1)}, f32[6,512]{1,0:T(8,128)S(1)}, u32[]{:S(2)}, u32[]{:S(2)}) collective-permute-start(f32[6,512]{1,0:T(8,128)S(1)} %constant_dynamic-update-slice_fusion.3.source_ref), channel_id=1, source_target_pairs={{0,8},{4,12},{8,0},{12,4},{1,9},{5,13},{9,1},{13,5},{2,10},{6,14},... | collective-permute-start | bytes 36872 | tf_op jit(solution)/shard_map/ppermute | solution.py:303
  9.3 0.0 collective-permute-done.1
  9.3 3.5 %shard_map.60 = (f32[3,1024,128]{2,1,0:T(8,128)S(1)}, f32[3,1024,128]{2,1,0:T(8,128)S(1)}, bf16[16,1024]{1,0:T(8,128)(2,1)S(1)}) custom-call(f32[4,1024]{1,0:T(4,128)S(1)} %constant_dynamic-update-slice_fusion.target_ref, f32[6,512]{1,0:T(8,128)S(1)} %constant_dynamic-update-slice_fusion.3.source_ref, s32[1,16]{1,0:T(1,128)S(1)} %get-tuple-element.16.owner_ref), custom_call_target="tpu_custom_call" | custom-call | flops 20972520 | bytes 1000 | tf_op jit(solution)/shard_map/pallas_call | solution.py:251
  12.8 0.0 collective-permute-done.3.source_ref
  12.8 3.5 %shard_map.61 = (f32[32,128]{1,0:T(8,128)S(1)}, f32[32,128]{1,0:T(8,128)S(1)}) custom-call(f32[3,1024,128]{2,1,0:T(8,128)S(1)} %get-tuple-element.17.points_ref, f32[6,512]{1,0:T(8,128)S(1)} %collective-permute-done.3.source_ref, f32[3,1024,128]{2,1,0:T(8,128)S(1)} %get-tuple-element.20.before_ref, bf16[16,1024]{1,0:T(8,128)(2,1)S(1)} %get-tuple-element.21.match_ref, ...), custom_call_target="tpu_custom_call" | custom-call | flops 20972520 | bytes 1000 | tf_op jit(solution)/shard_map/pallas_call | solution.py:251
  16.3 1.5 %collective-permute-start.4 = (f32[32,128]{1,0:T(8,128)S(1)}, f32[32,128]{1,0:T(8,128)S(1)}, u32[]{:S(2)}, u32[]{:S(2)}) collective-permute-start(f32[32,128]{1,0:T(8,128)S(1)} %get-tuple-element.23), channel_id=1, source_target_pairs={{0,2},{2,0},{1,3},{3,1},{4,6},{6,4},{5,7},{7,5},{8,10},{10,8},{9,1... | collective-permute-start | bytes 49160 | tf_op jit(solution)/shard_map/ppermute | solution.py:334
  17.8 2.2 %collective-permute-done.4 = f32[32,128]{1,0:T(8,128)S(1)} collective-permute-done((f32[32,128]{1,0:T(8,128)S(1)}, f32[32,128]{1,0:T(8,128)S(1)}, u32[]{:S(2)}, u32[]{:S(2)}) %collective-permute-start.4) | collective-permute-done | bytes 16416 | tf_op jit(solution)/shard_map/ppermute | solution.py:334
  20.1 0.1 collective-permute-start.5
  20.2 1.2 %collective-permute-done.5 = f32[24,128]{1,0:T(8,128)S(1)} collective-permute-done((f32[24,128]{1,0:T(8,128)S(1)}, f32[24,128]{1,0:T(8,128)S(1)}, u32[]{:S(2)}, u32[]{:S(2)}) %collective-permute-start.5) | collective-permute-done | bytes 12320 | tf_op jit(solution)/shard_map/ppermute | solution.py:334
  21.3 1.6 %collective-permute-start.6 = (f32[16,128]{1,0:T(8,128)S(1)}, f32[16,128]{1,0:T(8,128)S(1)}, u32[]{:S(2)}, u32[]{:S(2)}) collective-permute-start(f32[16,128]{1,0:T(8,128)S(1)} %slice.24), channel_id=1, source_target_pairs={{0,4},{4,0},{8,12},{12,8},{1,5},{5,1},{9,13},{13,9},{2,6},{6,2},{1... | collective-permute-start | bytes 24584 | tf_op jit(solution)/shard_map/ppermute | solution.py:338
  22.9 0.6 %shard_map.62 = f32[3,256]{1,0:T(4,128)} custom-call(f32[8,128]{1,0:T(8,128)S(1)} %slice.23.packed_ref), custom_call_target="tpu_custom_call" | custom-call | flops 1000 | bytes 1000 | tf_op jit(solution)/shard_map/pallas_call | solution.py:251
  23.5 1.5 %collective-permute-done.6 = f32[16,128]{1,0:T(8,128)S(1)} collective-permute-done((f32[16,128]{1,0:T(8,128)S(1)}, f32[16,128]{1,0:T(8,128)S(1)}, u32[]{:S(2)}, u32[]{:S(2)}) %collective-permute-start.6) | collective-permute-done | bytes 8224 | tf_op jit(solution)/shard_map/ppermute | solution.py:338
  25.0 1.7 %collective-permute-start.7 = (f32[16,128]{1,0:T(8,128)S(1)}, f32[16,128]{1,0:T(8,128)S(1)}, u32[]{:S(2)}, u32[]{:S(2)}) collective-permute-start(f32[16,128]{1,0:T(8,128)S(1)} %slice_add_fusion.1), channel_id=1, source_target_pairs={{0,8},{4,12},{8,0},{12,4},{1,9},{5,13},{9,1},{13,5},{2,10},{6,14},... | collective-permute-start | bytes 24584 | tf_op jit(solution)/shard_map/ppermute | solution.py:338
  26.6 2.9 %collective-permute-done.7 = f32[16,128]{1,0:T(8,128)S(1)} collective-permute-done((f32[16,128]{1,0:T(8,128)S(1)}, f32[16,128]{1,0:T(8,128)S(1)}, u32[]{:S(2)}, u32[]{:S(2)}) %collective-permute-start.7) | collective-permute-done | bytes 8224 | tf_op jit(solution)/shard_map/ppermute | solution.py:338
  29.6 0.7 %shard_map.63 = f32[1,9]{1,0:T(1,128)} custom-call(s32[1]{0:T(128)} %bitcast.2.first_ref, f32[16,128]{1,0:T(8,128)S(1)} %add.23.sums_ref), custom_call_target="tpu_custom_call" | custom-call | flops 1000 | bytes 1000 | tf_op jit(solution)/shard_map/pallas_call | solution.py:251
  (15 shorter events, 0.1 us)
Async XLA Ops:
  1.4 3.2 %collective-permute-start = (f32[4,256]{1,0:T(4,128)S(1)}, f32[4,256]{1,0:T(4,128)S(1)}, u32[]{:S(2)}, u32[]{:S(2)}) collective-permute-start(f32[4,256]{1,0:T(4,128)S(1)} %get-tuple-element.14), channel_id=1, source_target_pairs={{0,1},{1,0},{2,3},{3,2},{4,5},{5,4},{6,7},{7,6},{8,9},{9,8},{10,11... | collective-permute-start | bytes 12296 | tf_op jit(solution)/shard_map/ppermute | solution.py:298
  1.9 4.3 %collective-permute-start.2 = (f32[6,256]{1,0:T(8,128)S(1)}, f32[6,256]{1,0:T(8,128)S(1)}, u32[]{:S(2)}, u32[]{:S(2)}) collective-permute-start(f32[6,256]{1,0:T(8,128)S(1)} %get-tuple-element.15), channel_id=1, source_target_pairs={{0,4},{4,0},{8,12},{12,8},{1,5},{5,1},{9,13},{13,9},{2,6},{6,2},{1... | collective-permute-start | bytes 18440 | tf_op jit(solution)/shard_map/ppermute | solution.py:303
  4.6 4.7 %collective-permute-start.1 = (f32[4,512]{1,0:T(4,128)S(1)}, f32[4,512]{1,0:T(4,128)S(1)}, u32[]{:S(2)}, u32[]{:S(2)}) collective-permute-start(f32[4,512]{1,0:T(4,128)S(1)} %pad_maximum_fusion.1), channel_id=1, source_target_pairs={{0,2},{2,0},{1,3},{3,1},{4,6},{6,4},{5,7},{7,5},{8,10},{10,8},{9,1... | collective-permute-start | bytes 24584 | tf_op jit(solution)/shard_map/ppermute | solution.py:298
  6.2 6.6 %collective-permute-start.3 = (f32[6,512]{1,0:T(8,128)S(1)}, f32[6,512]{1,0:T(8,128)S(1)}, u32[]{:S(2)}, u32[]{:S(2)}) collective-permute-start(f32[6,512]{1,0:T(8,128)S(1)} %constant_dynamic-update-slice_fusion.3.source_ref), channel_id=1, source_target_pairs={{0,8},{4,12},{8,0},{12,4},{1,9},{5,13},{9,1},{13,5},{2,10},{6,14},... | collective-permute-start | bytes 36872 | tf_op jit(solution)/shard_map/ppermute | solution.py:303
  16.3 3.8 %collective-permute-start.4 = (f32[32,128]{1,0:T(8,128)S(1)}, f32[32,128]{1,0:T(8,128)S(1)}, u32[]{:S(2)}, u32[]{:S(2)}) collective-permute-start(f32[32,128]{1,0:T(8,128)S(1)} %get-tuple-element.23), channel_id=1, source_target_pairs={{0,2},{2,0},{1,3},{3,1},{4,6},{6,4},{5,7},{7,5},{8,10},{10,8},{9,1... | collective-permute-start | bytes 49160 | tf_op jit(solution)/shard_map/ppermute | solution.py:334
  20.1 1.2 %collective-permute-start.5 = (f32[24,128]{1,0:T(8,128)S(1)}, f32[24,128]{1,0:T(8,128)S(1)}, u32[]{:S(2)}, u32[]{:S(2)}) collective-permute-start(f32[24,128]{1,0:T(8,128)S(1)} %pad_maximum_fusion), channel_id=1, source_target_pairs={{0,1},{1,0},{2,3},{3,2},{4,5},{5,4},{6,7},{7,6},{8,9},{9,8},{10,11... | collective-permute-start | bytes 36872 | tf_op jit(solution)/shard_map/ppermute | solution.py:334
  21.3 3.7 %collective-permute-start.6 = (f32[16,128]{1,0:T(8,128)S(1)}, f32[16,128]{1,0:T(8,128)S(1)}, u32[]{:S(2)}, u32[]{:S(2)}) collective-permute-start(f32[16,128]{1,0:T(8,128)S(1)} %slice.24), channel_id=1, source_target_pairs={{0,4},{4,0},{8,12},{12,8},{1,5},{5,1},{9,13},{13,9},{2,6},{6,2},{1... | collective-permute-start | bytes 24584 | tf_op jit(solution)/shard_map/ppermute | solution.py:338
  25.0 4.5 %collective-permute-start.7 = (f32[16,128]{1,0:T(8,128)S(1)}, f32[16,128]{1,0:T(8,128)S(1)}, u32[]{:S(2)}, u32[]{:S(2)}) collective-permute-start(f32[16,128]{1,0:T(8,128)S(1)} %slice_add_fusion.1), channel_id=1, source_target_pairs={{0,8},{4,12},{8,0},{12,4},{1,9},{5,13},{9,1},{13,5},{2,10},{6,14},... | collective-permute-start | bytes 24584 | tf_op jit(solution)/shard_map/ppermute | solution.py:338

commit v4 on v3

--- a/solution.py
+++ b/solution.py
@@ -17,73 +17,66 @@
 
 LANES = 128
 SUBLANES = 8
-GROUPS_AT_ONCE = 8
-BLOCKS_AT_ONCE = 16
+BLOCKS_AT_ONCE = 4
 SUM_ROWS = 16
 SOURCE_AXES = ("tgt",)
 TARGET_AXES = ("sub", "src")
 AXES = ("tgt", "src", "sub")
 
 
-def add_pairs(points_ref, source_ref, before_ref, total_ref, scaled):
-    count = points_ref.shape[1]
+def add_pairs(points_ref, source_ref, before_ref, total_ref, scaled, beside=None, shift=0):
+    count = total_ref.shape[1] - shift
     blocks = source_ref.shape[1] // LANES
     together = math.gcd(blocks, BLOCKS_AT_ONCE)
-    groups = math.gcd(count // SUBLANES, GROUPS_AT_ONCE)
-    rows = SUBLANES * groups
     scaled[0:3, :] = SCALE * source_ref[0:3, :]
-    scaled[3:6, :] = source_ref[3:6, :]
-
-    def target_step(step, unused):
-        first = pl.multiple_of(step * rows, rows)
-        slices = [pl.ds(first + group * SUBLANES, SUBLANES) for group in range(groups)]
-        points = [[points_ref[k, one, :] for k in range(3)] for one in slices]
-
-        def source_step(number, carry):
-            sums = [list(one) for one in carry]
-            base = number * (together * LANES)
-            for block in range(together):
-                lanes = pl.ds(pl.multiple_of(base + block * LANES, LANES), LANES)
-                x, y, z, fx, fy, fz = [
-                    jnp.broadcast_to(scaled[k : k + 1, lanes], (SUBLANES, LANES))
-                    for k in range(6)
-                ]
-                for group in range(groups):
-                    px, py, pz = points[group]
-                    dx, dy, dz = px - x, py - y, pz - z
-                    square = dx * dx + dy * dy + dz * dz
-                    inverse = lax.rsqrt(jnp.maximum(square, SMALLEST))
-                    held = jnp.minimum(inverse, TOUCH_INVERSE)
-                    held_sq = held * held
-                    iso = jnp.maximum(held * (held_sq + 2.0), NEAR - square * inverse)
-                    along = dx * fx + dy * fy + dz * fz
-                    dyad = (inverse * (held_sq * (2.0 / 3.0 - held_sq))) * along
-                    one = sums[group]
-                    sums[group] = [
-                        one[0] + iso * fx,
-                        one[1] + iso * fy,
-                        one[2] + iso * fz,
-                        one[3] + dyad * dx,
-                        one[4] + dyad * dy,
-                        one[5] + dyad * dz,
-                    ]
-            return tuple(tuple(one) for one in sums)
-
-        zero = jnp.zeros((SUBLANES, LANES), jnp.float32)
-        carry = tuple((zero,) * 6 for _ in range(groups))
-        if blocks == together:
-            carry = source_step(0, carry)
-        else:
-            carry = lax.fori_loop(0, blocks // together, source_step, carry)
-        for group in range(groups):
+    scaled[3:6, :] = ISO * source_ref[3:6, :]
+    scaled[6:9, :] = DYAD * source_ref[3:6, :]
+
+    def add_block(point, base, block, sums):
+        lanes = pl.ds(pl.multiple_of(base + block * LANES, LANES), LANES)
+        x, y, z, fx, fy, fz, gx, gy, gz = [
+            jnp.broadcast_to(scaled[k : k + 1, lanes], (SUBLANES, LANES)) for k in range(9)
+        ]
+        dx, dy, dz = point[0] - x, point[1] - y, point[2] - z
+        square = dx * dx + dy * dy + dz * dz
+        inverse = lax.rsqrt(jnp.maximum(square, SMALLEST))
+        held = jnp.minimum(inverse, TOUCH_INVERSE)
+        held_sq = held * held
+        iso = jnp.maximum(held * (held_sq + 2.0), NEAR - square * inverse)
+        along = dx * gx + dy * gy + dz * gz
+        dyad = (inverse * (held_sq * (2.0 / 3.0 - held_sq))) * along
+        terms = (iso * fx + dyad * dx, iso * fy + dyad * dy, iso * fz + dyad * dz)
+        return terms if sums is None else tuple(one + term for one, term in zip(sums, terms))
+
+    def tile_step(step, unused):
+        first = pl.multiple_of(step * LANES, LANES)
+        if beside is not None:
+            beside(first)
+        for group in range(LANES // SUBLANES):
+            rows = pl.ds(first + group * SUBLANES, SUBLANES)
+            point = [points_ref[k, rows, :] for k in range(3)]
+            sums = None
+            if before_ref is not None:
+                sums = tuple(before_ref[k, rows, :] for k in range(3))
+            if blocks == together:
+                for block in range(together):
+                    sums = add_block(point, 0, block, sums)
+            else:
+
+                def source_step(number, sums):
+                    for block in range(together):
+                        sums = add_block(point, number * (together * LANES), block, sums)
+                    return sums
+
+                zero = jnp.zeros((SUBLANES, LANES), jnp.float32)
+                sums = lax.fori_loop(
+                    0, blocks // together, source_step, sums or (zero, zero, zero)
+                )
             for k in range(3):
-                value = ISO * carry[group][k] + DYAD * carry[group][3 + k]
-                if before_ref is not None:
-                    value = before_ref[k, slices[group], :] + value
-                total_ref[k, slices[group], :] = value
+                total_ref[k, pl.ds(first + shift + group * SUBLANES, SUBLANES), :] = sums[k]
         return unused
 
-    lax.fori_loop(0, count // rows, target_step, 0)
+    lax.fori_loop(0, count // LANES, tile_step, 0)
 
 
 def head_kernel(
@@ -114,17 +107,27 @@
     target_ref[3:4, :] = member[...].astype(jnp.float32)
 
 
-def first_kernel(target_ref, source_ref, owner_ref, points_ref, total_ref, match_ref, scaled):
+def first_kernel(
+    target_ref, source_ref, owner_ref, points_ref, total_ref, match_ref, scaled
+):
     count = target_ref.shape[1]
-    for start in range(0, count, LANES):
-        tile = jnp.concatenate(
-            [target_ref[:, start : start + LANES], jnp.zeros((4, LANES), jnp.float32)], axis=0
-        )
-        turned = (SCALE * tile).T
-        for k in range(3):
-            points_ref[k, start : start + LANES, :] = jnp.broadcast_to(
-                turned[:, k : k + 1], (LANES, LANES)
-            )
+    parts, rest = [], SCALE * target_ref[0:3, :]
+    for _ in range(3):
+        part = rest.astype(jnp.bfloat16).astype(jnp.float32)
+        rest = rest - part
+        parts.append(part)
+    parts.append(jnp.zeros((7, count), jnp.float32))
+    row = lax.broadcasted_iota(jnp.int32, (16, 3 * LANES), 0)
+    lane = lax.broadcasted_iota(jnp.int32, (16, 3 * LANES), 1)
+    chosen = jnp.where((row % 3 == lane // LANES) & (row < 9), 1.0, 0.0)
+    points = lax.dot_general(
+        jnp.concatenate(parts, axis=0).astype(jnp.bfloat16),
+        chosen.astype(jnp.bfloat16),
+        (((0,), (0,)), ((), ())),
+        preferred_element_type=jnp.float32,
+    )
+    for k in range(3):
+        points_ref[k, :, :] = points[:, k * LANES : (k + 1) * LANES]
     aggregates = match_ref.shape[0]
     labels = lax.broadcasted_iota(jnp.int32, (aggregates, count), 0)
     member = jnp.where(labels == target_ref[3:4, :].astype(jnp.int32), 1.0, 0.0)
@@ -135,6 +138,7 @@
         member.astype(jnp.bfloat16),
         preferred_element_type=jnp.float32,
     ).astype(jnp.bfloat16)
+
     add_pairs(points_ref, source_ref, None, total_ref, scaled)
 
 
@@ -149,9 +153,28 @@
     send_ref,
     total,
     scaled,
+    summed,
 ):
-    add_pairs(points_ref, source_ref, before_ref, total, scaled)
-    count = points_ref.shape[1]
+    count = target_ref.shape[1]
+    tiles = count // LANES
+
+    def sum_tile(first, tile):
+        rows = pl.ds(first, LANES)
+        for k in range(3):
+            summed[tile, k : k + 1, :] = jnp.sum(total[k, rows, :].T, axis=0, keepdims=True)
+
+    total[:, 0:LANES, :] = jnp.zeros((3, LANES, LANES), jnp.float32)
+    add_pairs(
+        points_ref,
+        source_ref,
+        before_ref,
+        total,
+        scaled,
+        lambda first: sum_tile(first, first // LANES),
+        LANES,
+    )
+    sum_tile(count, tiles)
+
     aggregates = match_ref.shape[0]
     per_unit, units = unit_count // LANES, count // unit_count
     first_row, unit_rows = sum_rows(aggregates), velocity_rows(unit_count)
@@ -159,17 +182,13 @@
     send_ref[...] = jnp.zeros_like(send_ref)
     u = []
     for k in range(3):
-        parts = []
-        for tile in range(count // LANES):
-            part = jnp.sum(
-                total[k, tile * LANES : (tile + 1) * LANES, :].T, axis=0, keepdims=True
-            )
-            parts.append(part)
+        parts = [summed[tile + 1, k : k + 1, :] for tile in range(tiles)]
+        u.append(jnp.concatenate(parts, axis=1))
+        for tile in range(tiles):
             unit, block = divmod(tile, per_unit)
             packed, unit = (keep_ref, unit) if unit < units // 2 else (send_ref, unit - units // 2)
             row = first_row + unit * unit_rows + k * per_unit + block
-            packed[row : row + 1, :] = part
-        u.append(jnp.concatenate(parts, axis=1))
+            packed[row : row + 1, :] = parts[tile]
     x = [target_ref[k : k + 1, :] for k in range(3)]
     moments = jnp.concatenate(
         u
@@ -187,7 +206,7 @@
         part = rest.astype(jnp.bfloat16)
         rest = rest - part.astype(jnp.float32)
         parts.append(part)
-    summed = [
+    products = [
         lax.dot_general(
             part,
             match_ref[...],
@@ -196,7 +215,7 @@
         )
         for part in parts
     ]
-    sums = (summed[2] + summed[1]) + summed[0]
+    sums = (products[2] + products[1]) + products[0]
     for chunk, start in enumerate(range(0, aggregates, LANES)):
         width = min(LANES, aggregates - start)
         for packed in (keep_ref, send_ref):
@@ -302,12 +321,15 @@
             axis, pairs = source_steps[number]
             coming = lax.ppermute(sources, axis, pairs)
     seen = targets.shape[1]
-    wide = ((3, seen, LANES), real)
-    scaled = pltpu.VMEM((SUBLANES, sources.shape[1]), real)
+    scaled = pltpu.VMEM((2 * SUBLANES, sources.shape[1]), real)
     vmem = (8 << 20) + 4 * (4 * 3 * seen * LANES)
     points, total, match = call(
         first_kernel,
-        [wide, wide, ((aggregates, seen), jnp.bfloat16)],
+        [
+            ((3, seen, LANES), real),
+            ((3, seen, LANES), real),
+            ((aggregates, seen), jnp.bfloat16),
+        ],
         (targets, sources, owner),
         pairs=seen * sources.shape[1],
         scratch=[scaled],
@@ -322,7 +344,11 @@
         [packed, packed],
         (points, coming, total, match, targets),
         pairs=seen * coming.shape[1],
-        scratch=[pltpu.VMEM((3, seen, LANES), real), scaled],
+        scratch=[
+            pltpu.VMEM((3, seen + LANES, LANES), real),
+            scaled,
+            pltpu.VMEM((seen // LANES + 1, SUBLANES, LANES), real),
+        ],
         vmem=vmem,
     )
 

time: 30.4 us -> 29.6 us (0.974)
  Pallas kernels: 9.05 us -> 8.19 us
    pallas_call x5, Pallas kernels: 9.05 us -> 8.19 us  [call(): pl.pallas_call(kernel, out_shape=[jax.ShapeDtypeStruct(shape, dtype) for...]
  transfers between devices with their start and end apart: 8 -> 8, of which waited for: 5 -> 5; matrix products, arithmetic and copies ran while one was open for 0% -> 0% of each run, Pallas kernels for 14% -> 12%
where the time goes in v4:
time: 29.6 us; the launch traced here: 29.4 us
  starting transfers between devices  12.6 us (43%)
  Pallas kernels  8.19 us (28%)
  waiting for transfers between devices  7.84 us (26%)
  between operations  0.69 us (2%)
    pallas_call x5, Pallas kernels, call(): pl.pallas_call(kernel, out_shape=[jax.ShapeDtypeStruct(shape, dtype) for...  8.19 us
    ppermute x2, starting transfers between devices, on_device(): coming = lax.ppermute(sources, axis, pairs)  5.67 us
    ppermute x2, waiting for transfers between devices, on_device(): coming = lax.ppermute(sums, axis, pairs)  4.37 us
    ppermute x2, waiting for transfers between devices, on_device(): both = keep + lax.ppermute(send, axis, pairs)  3.41 us
    ppermute x2, starting transfers between devices, on_device(): coming = lax.ppermute(sums, axis, pairs)  3.23 us
    ppermute x2, starting transfers between devices, on_device(): lax.ppermute(targets, axis, pairs)  2.11 us
    ppermute x2, starting transfers between devices, on_device(): both = keep + lax.ppermute(send, axis, pairs)  1.59 us
  transfers between devices with their start and end apart: 8, of which 5 were waited for; matrix products, arithmetic and copies ran while one was open for 0% of the time, Pallas kernels for 12%

profile of v4, /device:TPU:0, one launch (start us, length us, event | category | flops | bytes accessed | tf_op | source)
XLA Modules:
  0.0 29.4 jit_solution(15077981619529105135)
XLA Ops:
  0.6 0.8 %shard_map.59 = (f32[6,256]{1,0:T(8,128)S(1)}, f32[4,256]{1,0:T(4,128)S(1)}, s32[1,16]{1,0:T(1,128)S(1)}) custom-call(f32[3,256]{1,0:T(4,128)} %position_in.1, f32[3,256]{1,0:T(4,128)} %force_in.1, s32[1,256]{1,0:T(1,128)} %bitcast.4, s32[1,16]{1,0:T(1,128)} %bitcast.5), custom_call_target="tpu_custom_call" | custom-call | flops 1000 | bytes 1000 | tf_op jit(solution)/shard_map/pallas_call | solution.py:270
  1.4 0.6 %collective-permute-start = (f32[4,256]{1,0:T(4,128)S(1)}, f32[4,256]{1,0:T(4,128)S(1)}, u32[]{:S(2)}, u32[]{:S(2)}) collective-permute-start(f32[4,256]{1,0:T(4,128)S(1)} %get-tuple-element.14), channel_id=1, source_target_pairs={{0,1},{1,0},{2,3},{3,2},{4,5},{5,4},{6,7},{7,6},{8,9},{9,8},{10,11... | collective-permute-start | bytes 12296 | tf_op jit(solution)/shard_map/ppermute | solution.py:317
  1.9 2.6 %collective-permute-start.2 = (f32[6,256]{1,0:T(8,128)S(1)}, f32[6,256]{1,0:T(8,128)S(1)}, u32[]{:S(2)}, u32[]{:S(2)}) collective-permute-start(f32[6,256]{1,0:T(8,128)S(1)} %get-tuple-element.15), channel_id=1, source_target_pairs={{0,4},{4,0},{8,12},{12,8},{1,5},{5,1},{9,13},{13,9},{2,6},{6,2},{1... | collective-permute-start | bytes 18440 | tf_op jit(solution)/shard_map/ppermute | solution.py:322
  4.6 0.0 collective-permute-done
  4.6 1.6 %collective-permute-start.1 = (f32[4,512]{1,0:T(4,128)S(1)}, f32[4,512]{1,0:T(4,128)S(1)}, u32[]{:S(2)}, u32[]{:S(2)}) collective-permute-start(f32[4,512]{1,0:T(4,128)S(1)} %pad_maximum_fusion.1), channel_id=1, source_target_pairs={{0,2},{2,0},{1,3},{3,1},{4,6},{6,4},{5,7},{7,5},{8,10},{10,8},{9,1... | collective-permute-start | bytes 24584 | tf_op jit(solution)/shard_map/ppermute | solution.py:317
  6.2 0.1 collective-permute-done.2
  6.2 3.0 %collective-permute-start.3 = (f32[6,512]{1,0:T(8,128)S(1)}, f32[6,512]{1,0:T(8,128)S(1)}, u32[]{:S(2)}, u32[]{:S(2)}) collective-permute-start(f32[6,512]{1,0:T(8,128)S(1)} %constant_dynamic-update-slice_fusion.3.source_ref), channel_id=1, source_target_pairs={{0,8},{4,12},{8,0},{12,4},{1,9},{5,13},{9,1},{13,5},{2,10},{6,14},... | collective-permute-start | bytes 36872 | tf_op jit(solution)/shard_map/ppermute | solution.py:322
  9.3 0.0 collective-permute-done.1
  9.3 3.0 %shard_map.60 = (f32[3,1024,128]{2,1,0:T(8,128)S(1)}, f32[3,1024,128]{2,1,0:T(8,128)S(1)}, bf16[16,1024]{1,0:T(8,128)(2,1)S(1)}) custom-call(f32[4,1024]{1,0:T(4,128)S(1)} %constant_dynamic-update-slice_fusion.target_ref, f32[6,512]{1,0:T(8,128)S(1)} %constant_dynamic-update-slice_fusion.3.source_ref, s32[1,16]{1,0:T(1,128)S(1)} %get-tuple-element.16.owner_ref), custom_call_target="tpu_custom_call" | custom-call | flops 20972520 | bytes 1000 | tf_op jit(solution)/shard_map/pallas_call | solution.py:270
  12.3 0.0 collective-permute-done.3.source_ref
  12.3 3.1 %shard_map.61 = (f32[32,128]{1,0:T(8,128)S(1)}, f32[32,128]{1,0:T(8,128)S(1)}) custom-call(f32[3,1024,128]{2,1,0:T(8,128)S(1)} %get-tuple-element.17.points_ref, f32[6,512]{1,0:T(8,128)S(1)} %collective-permute-done.3.source_ref, f32[3,1024,128]{2,1,0:T(8,128)S(1)} %get-tuple-element.20.before_ref, bf16[16,1024]{1,0:T(8,128)(2,1)S(1)} %get-tuple-element.21.match_ref, ...), custom_call_target="tpu_custom_call" | custom-call | flops 20972520 | bytes 1000 | tf_op jit(solution)/shard_map/pallas_call | solution.py:270
  15.4 1.5 %collective-permute-start.4 = (f32[32,128]{1,0:T(8,128)S(1)}, f32[32,128]{1,0:T(8,128)S(1)}, u32[]{:S(2)}, u32[]{:S(2)}) collective-permute-start(f32[32,128]{1,0:T(8,128)S(1)} %get-tuple-element.23), channel_id=1, source_target_pairs={{0,2},{2,0},{1,3},{3,1},{4,6},{6,4},{5,7},{7,5},{8,10},{10,8},{9,1... | collective-permute-start | bytes 49160 | tf_op jit(solution)/shard_map/ppermute | solution.py:360
  17.0 2.2 %collective-permute-done.4 = f32[32,128]{1,0:T(8,128)S(1)} collective-permute-done((f32[32,128]{1,0:T(8,128)S(1)}, f32[32,128]{1,0:T(8,128)S(1)}, u32[]{:S(2)}, u32[]{:S(2)}) %collective-permute-start.4) | collective-permute-done | bytes 16416 | tf_op jit(solution)/shard_map/ppermute | solution.py:360
  19.2 0.1 collective-permute-start.5
  19.3 1.2 %collective-permute-done.5 = f32[24,128]{1,0:T(8,128)S(1)} collective-permute-done((f32[24,128]{1,0:T(8,128)S(1)}, f32[24,128]{1,0:T(8,128)S(1)}, u32[]{:S(2)}, u32[]{:S(2)}) %collective-permute-start.5) | collective-permute-done | bytes 12320 | tf_op jit(solution)/shard_map/ppermute | solution.py:360
  20.5 1.6 %collective-permute-start.6 = (f32[16,128]{1,0:T(8,128)S(1)}, f32[16,128]{1,0:T(8,128)S(1)}, u32[]{:S(2)}, u32[]{:S(2)}) collective-permute-start(f32[16,128]{1,0:T(8,128)S(1)} %slice.24), channel_id=1, source_target_pairs={{0,4},{4,0},{8,12},{12,8},{1,5},{5,1},{9,13},{13,9},{2,6},{6,2},{1... | collective-permute-start | bytes 24584 | tf_op jit(solution)/shard_map/ppermute | solution.py:364
  22.1 0.6 %shard_map.62 = f32[3,256]{1,0:T(4,128)} custom-call(f32[8,128]{1,0:T(8,128)S(1)} %slice.23.packed_ref), custom_call_target="tpu_custom_call" | custom-call | flops 1000 | bytes 1000 | tf_op jit(solution)/shard_map/pallas_call | solution.py:270
  22.7 1.5 %collective-permute-done.6 = f32[16,128]{1,0:T(8,128)S(1)} collective-permute-done((f32[16,128]{1,0:T(8,128)S(1)}, f32[16,128]{1,0:T(8,128)S(1)}, u32[]{:S(2)}, u32[]{:S(2)}) %collective-permute-start.6) | collective-permute-done | bytes 8224 | tf_op jit(solution)/shard_map/ppermute | solution.py:364
  24.1 1.6 %collective-permute-start.7 = (f32[16,128]{1,0:T(8,128)S(1)}, f32[16,128]{1,0:T(8,128)S(1)}, u32[]{:S(2)}, u32[]{:S(2)}) collective-permute-start(f32[16,128]{1,0:T(8,128)S(1)} %slice_add_fusion.1), channel_id=1, source_target_pairs={{0,8},{4,12},{8,0},{12,4},{1,9},{5,13},{9,1},{13,5},{2,10},{6,14},... | collective-permute-start | bytes 24584 | tf_op jit(solution)/shard_map/ppermute | solution.py:364
  25.8 2.9 %collective-permute-done.7 = f32[16,128]{1,0:T(8,128)S(1)} collective-permute-done((f32[16,128]{1,0:T(8,128)S(1)}, f32[16,128]{1,0:T(8,128)S(1)}, u32[]{:S(2)}, u32[]{:S(2)}) %collective-permute-start.7) | collective-permute-done | bytes 8224 | tf_op jit(solution)/shard_map/ppermute | solution.py:364
  28.7 0.7 %shard_map.63 = f32[1,9]{1,0:T(1,128)} custom-call(s32[1]{0:T(128)} %bitcast.2.first_ref, f32[16,128]{1,0:T(8,128)S(1)} %add.23.sums_ref), custom_call_target="tpu_custom_call" | custom-call | flops 1000 | bytes 1000 | tf_op jit(solution)/shard_map/pallas_call | solution.py:270
  (15 shorter events, 0.1 us)
Async XLA Ops:
  1.4 3.2 %collective-permute-start = (f32[4,256]{1,0:T(4,128)S(1)}, f32[4,256]{1,0:T(4,128)S(1)}, u32[]{:S(2)}, u32[]{:S(2)}) collective-permute-start(f32[4,256]{1,0:T(4,128)S(1)} %get-tuple-element.14), channel_id=1, source_target_pairs={{0,1},{1,0},{2,3},{3,2},{4,5},{5,4},{6,7},{7,6},{8,9},{9,8},{10,11... | collective-permute-start | bytes 12296 | tf_op jit(solution)/shard_map/ppermute | solution.py:317
  1.9 4.3 %collective-permute-start.2 = (f32[6,256]{1,0:T(8,128)S(1)}, f32[6,256]{1,0:T(8,128)S(1)}, u32[]{:S(2)}, u32[]{:S(2)}) collective-permute-start(f32[6,256]{1,0:T(8,128)S(1)} %get-tuple-element.15), channel_id=1, source_target_pairs={{0,4},{4,0},{8,12},{12,8},{1,5},{5,1},{9,13},{13,9},{2,6},{6,2},{1... | collective-permute-start | bytes 18440 | tf_op jit(solution)/shard_map/ppermute | solution.py:322
  4.6 4.7 %collective-permute-start.1 = (f32[4,512]{1,0:T(4,128)S(1)}, f32[4,512]{1,0:T(4,128)S(1)}, u32[]{:S(2)}, u32[]{:S(2)}) collective-permute-start(f32[4,512]{1,0:T(4,128)S(1)} %pad_maximum_fusion.1), channel_id=1, source_target_pairs={{0,2},{2,0},{1,3},{3,1},{4,6},{6,4},{5,7},{7,5},{8,10},{10,8},{9,1... | collective-permute-start | bytes 24584 | tf_op jit(solution)/shard_map/ppermute | solution.py:317
  6.2 6.1 %collective-permute-start.3 = (f32[6,512]{1,0:T(8,128)S(1)}, f32[6,512]{1,0:T(8,128)S(1)}, u32[]{:S(2)}, u32[]{:S(2)}) collective-permute-start(f32[6,512]{1,0:T(8,128)S(1)} %constant_dynamic-update-slice_fusion.3.source_ref), channel_id=1, source_target_pairs={{0,8},{4,12},{8,0},{12,4},{1,9},{5,13},{9,1},{13,5},{2,10},{6,14},... | collective-permute-start | bytes 36872 | tf_op jit(solution)/shard_map/ppermute | solution.py:322
  15.4 3.8 %collective-permute-start.4 = (f32[32,128]{1,0:T(8,128)S(1)}, f32[32,128]{1,0:T(8,128)S(1)}, u32[]{:S(2)}, u32[]{:S(2)}) collective-permute-start(f32[32,128]{1,0:T(8,128)S(1)} %get-tuple-element.23), channel_id=1, source_target_pairs={{0,2},{2,0},{1,3},{3,1},{4,6},{6,4},{5,7},{7,5},{8,10},{10,8},{9,1... | collective-permute-start | bytes 49160 | tf_op jit(solution)/shard_map/ppermute | solution.py:360
  19.2 1.2 %collective-permute-start.5 = (f32[24,128]{1,0:T(8,128)S(1)}, f32[24,128]{1,0:T(8,128)S(1)}, u32[]{:S(2)}, u32[]{:S(2)}) collective-permute-start(f32[24,128]{1,0:T(8,128)S(1)} %pad_maximum_fusion), channel_id=1, source_target_pairs={{0,1},{1,0},{2,3},{3,2},{4,5},{5,4},{6,7},{7,6},{8,9},{9,8},{10,11... | collective-permute-start | bytes 36872 | tf_op jit(solution)/shard_map/ppermute | solution.py:360
  20.5 3.7 %collective-permute-start.6 = (f32[16,128]{1,0:T(8,128)S(1)}, f32[16,128]{1,0:T(8,128)S(1)}, u32[]{:S(2)}, u32[]{:S(2)}) collective-permute-start(f32[16,128]{1,0:T(8,128)S(1)} %slice.24), channel_id=1, source_target_pairs={{0,4},{4,0},{8,12},{12,8},{1,5},{5,1},{9,13},{13,9},{2,6},{6,2},{1... | collective-permute-start | bytes 24584 | tf_op jit(solution)/shard_map/ppermute | solution.py:364
  24.1 4.5 %collective-permute-start.7 = (f32[16,128]{1,0:T(8,128)S(1)}, f32[16,128]{1,0:T(8,128)S(1)}, u32[]{:S(2)}, u32[]{:S(2)}) collective-permute-start(f32[16,128]{1,0:T(8,128)S(1)} %slice_add_fusion.1), channel_id=1, source_target_pairs={{0,8},{4,12},{8,0},{12,4},{1,9},{5,13},{9,1},{13,5},{2,10},{6,14},... | collective-permute-start | bytes 24584 | tf_op jit(solution)/shard_map/ppermute | solution.py:364

commit v5 on v4

--- a/solution.py
+++ b/solution.py
@@ -282,11 +282,17 @@
 
 def doubling(mesh, axes):
     steps = []
+    cores = mesh.shape["sub"]
+    other = 1 if cores == 2 else 0
     for axis in axes:
         size = mesh.shape[axis]
         reach = 1
         while reach < size:
-            steps.append((axis, [(i, i ^ reach) for i in range(size)]))
+            if axis == "sub":
+                steps.append((axis, [(i, i ^ reach) for i in range(size)]))
+            else:
+                flip = reach * cores + other
+                steps.append(((axis, "sub"), [(i, i ^ flip) for i in range(size * cores)]))
             reach *= 2
     return steps
 

time: 29.6 us -> 27.3 us (0.922)
  starting transfers between devices: 12.6 us -> 11.4 us
  waiting for transfers between devices: 7.84 us -> 6.84 us
    ppermute x2, waiting for transfers between devices: 4.37 us -> 3.67 us  [on_device(): coming = lax.ppermute(sums, axis, pairs)]
    ppermute x2, starting transfers between devices: 3.23 us -> 2.77 us  [on_device(): coming = lax.ppermute(sums, axis, pairs)]
    ppermute x2, waiting for transfers between devices: 3.41 us -> 3.05 us  [on_device(): both = keep + lax.ppermute(send, axis, pairs)]
    ppermute x2, starting transfers between devices: 2.11 us -> 1.8 us  [on_device(): lax.ppermute(targets, axis, pairs)]
  transfers between devices with their start and end apart: 8 -> 8, of which waited for: 5 -> 5; matrix products, arithmetic and copies ran while one was open for 0% -> 0% of each run, Pallas kernels for 12% -> 13%
where the time goes in v5:
time: 27.3 us; the launch traced here: 27.1 us
  starting transfers between devices  11.4 us (42%)
  Pallas kernels  8.19 us (30%)
  waiting for transfers between devices  6.84 us (25%)
  between operations  0.68 us (2%)
    pallas_call x5, Pallas kernels, call(): pl.pallas_call(kernel, out_shape=[jax.ShapeDtypeStruct(shape, dtype) for...  8.19 us
    ppermute x2, starting transfers between devices, on_device(): coming = lax.ppermute(sources, axis, pairs)  5.4 us
    ppermute x2, waiting for transfers between devices, on_device(): coming = lax.ppermute(sums, axis, pairs)  3.67 us
    ppermute x2, waiting for transfers between devices, on_device(): both = keep + lax.ppermute(send, axis, pairs)  3.05 us
    ppermute x2, starting transfers between devices, on_device(): coming = lax.ppermute(sums, axis, pairs)  2.77 us
    ppermute x2, starting transfers between devices, on_device(): lax.ppermute(targets, axis, pairs)  1.8 us
    ppermute x2, starting transfers between devices, on_device(): both = keep + lax.ppermute(send, axis, pairs)  1.38 us
  transfers between devices with their start and end apart: 8, of which 5 were waited for; matrix products, arithmetic and copies ran while one was open for 0% of the time, Pallas kernels for 13%

profile of v5, /device:TPU:0, one launch (start us, length us, event | category | flops | bytes accessed | tf_op | source)
XLA Modules:
  0.0 27.1 jit_solution(12455493374458690541)
XLA Ops:
  0.6 0.8 %shard_map.59 = (f32[6,256]{1,0:T(8,128)S(1)}, f32[4,256]{1,0:T(4,128)S(1)}, s32[1,16]{1,0:T(1,128)S(1)}) custom-call(f32[3,256]{1,0:T(4,128)} %position_in.1, f32[3,256]{1,0:T(4,128)} %force_in.1, s32[1,256]{1,0:T(1,128)} %bitcast.4, s32[1,16]{1,0:T(1,128)} %bitcast.5), custom_call_target="tpu_custom_call" | custom-call | flops 1000 | bytes 1000 | tf_op jit(solution)/shard_map/pallas_call | solution.py:270
  1.4 0.6 %collective-permute-start = (f32[4,256]{1,0:T(4,128)S(1)}, f32[4,256]{1,0:T(4,128)S(1)}, u32[]{:S(2)}, u32[]{:S(2)}) collective-permute-start(f32[4,256]{1,0:T(4,128)S(1)} %get-tuple-element.14), channel_id=1, source_target_pairs={{0,1},{1,0},{2,3},{3,2},{4,5},{5,4},{6,7},{7,6},{8,9},{9,8},{10,11... | collective-permute-start | bytes 12296 | tf_op jit(solution)/shard_map/ppermute | solution.py:323
  1.9 2.7 %collective-permute-start.2 = (f32[6,256]{1,0:T(8,128)S(1)}, f32[6,256]{1,0:T(8,128)S(1)}, u32[]{:S(2)}, u32[]{:S(2)}) collective-permute-start(f32[6,256]{1,0:T(8,128)S(1)} %get-tuple-element.15), channel_id=1, source_target_pairs={{0,5},{1,4},{4,1},{5,0},{8,13},{9,12},{12,9},{13,8},{2,7},{3,6},{6... | collective-permute-start | bytes 18440 | tf_op jit(solution)/shard_map/ppermute | solution.py:328
  4.6 0.0 collective-permute-done
  4.6 1.2 %collective-permute-start.1 = (f32[4,512]{1,0:T(4,128)S(1)}, f32[4,512]{1,0:T(4,128)S(1)}, u32[]{:S(2)}, u32[]{:S(2)}) collective-permute-start(f32[4,512]{1,0:T(4,128)S(1)} %pad_maximum_fusion.1), channel_id=1, source_target_pairs={{0,3},{1,2},{2,1},{3,0},{4,7},{5,6},{6,5},{7,4},{8,11},{9,10},{10,... | collective-permute-start | bytes 24584 | tf_op jit(solution)/shard_map/ppermute | solution.py:323
  5.9 0.1 collective-permute-done.2
  6.0 2.7 %collective-permute-start.3 = (f32[6,512]{1,0:T(8,128)S(1)}, f32[6,512]{1,0:T(8,128)S(1)}, u32[]{:S(2)}, u32[]{:S(2)}) collective-permute-start(f32[6,512]{1,0:T(8,128)S(1)} %constant_dynamic-update-slice_fusion.3.source_ref), channel_id=1, source_target_pairs={{0,9},{1,8},{4,13},{5,12},{8,1},{9,0},{12,5},{13,4},{2,11},{3,10},... | collective-permute-start | bytes 36872 | tf_op jit(solution)/shard_map/ppermute | solution.py:328
  8.7 0.0 collective-permute-done.1
  8.7 3.0 %shard_map.60 = (f32[3,1024,128]{2,1,0:T(8,128)S(1)}, f32[3,1024,128]{2,1,0:T(8,128)S(1)}, bf16[16,1024]{1,0:T(8,128)(2,1)S(1)}) custom-call(f32[4,1024]{1,0:T(4,128)S(1)} %constant_dynamic-update-slice_fusion.target_ref, f32[6,512]{1,0:T(8,128)S(1)} %constant_dynamic-update-slice_fusion.3.source_ref, s32[1,16]{1,0:T(1,128)S(1)} %get-tuple-element.16.owner_ref), custom_call_target="tpu_custom_call" | custom-call | flops 20972520 | bytes 1000 | tf_op jit(solution)/shard_map/pallas_call | solution.py:270
  11.8 0.0 collective-permute-done.3.source_ref
  11.8 3.1 %shard_map.61 = (f32[32,128]{1,0:T(8,128)S(1)}, f32[32,128]{1,0:T(8,128)S(1)}) custom-call(f32[3,1024,128]{2,1,0:T(8,128)S(1)} %get-tuple-element.17.points_ref, f32[6,512]{1,0:T(8,128)S(1)} %collective-permute-done.3.source_ref, f32[3,1024,128]{2,1,0:T(8,128)S(1)} %get-tuple-element.20.before_ref, bf16[16,1024]{1,0:T(8,128)(2,1)S(1)} %get-tuple-element.21.match_ref, ...), custom_call_target="tpu_custom_call" | custom-call | flops 20972520 | bytes 1000 | tf_op jit(solution)/shard_map/pallas_call | solution.py:270
  14.9 1.2 %collective-permute-start.4 = (f32[32,128]{1,0:T(8,128)S(1)}, f32[32,128]{1,0:T(8,128)S(1)}, u32[]{:S(2)}, u32[]{:S(2)}) collective-permute-start(f32[32,128]{1,0:T(8,128)S(1)} %get-tuple-element.23), channel_id=1, source_target_pairs={{0,3},{1,2},{2,1},{3,0},{4,7},{5,6},{6,5},{7,4},{8,11},{9,10},{10,... | collective-permute-start | bytes 49160 | tf_op jit(solution)/shard_map/ppermute | solution.py:366
  16.1 2.0 %collective-permute-done.4 = f32[32,128]{1,0:T(8,128)S(1)} collective-permute-done((f32[32,128]{1,0:T(8,128)S(1)}, f32[32,128]{1,0:T(8,128)S(1)}, u32[]{:S(2)}, u32[]{:S(2)}) %collective-permute-start.4) | collective-permute-done | bytes 16416 | tf_op jit(solution)/shard_map/ppermute | solution.py:366
  18.1 0.2 collective-permute-start.5
  18.3 1.1 %collective-permute-done.5 = f32[24,128]{1,0:T(8,128)S(1)} collective-permute-done((f32[24,128]{1,0:T(8,128)S(1)}, f32[24,128]{1,0:T(8,128)S(1)}, u32[]{:S(2)}, u32[]{:S(2)}) %collective-permute-start.5) | collective-permute-done | bytes 12320 | tf_op jit(solution)/shard_map/ppermute | solution.py:366
  19.4 1.3 %collective-permute-start.6 = (f32[16,128]{1,0:T(8,128)S(1)}, f32[16,128]{1,0:T(8,128)S(1)}, u32[]{:S(2)}, u32[]{:S(2)}) collective-permute-start(f32[16,128]{1,0:T(8,128)S(1)} %slice.24), channel_id=1, source_target_pairs={{0,5},{1,4},{4,1},{5,0},{8,13},{9,12},{12,9},{13,8},{2,7},{3,6},{6... | collective-permute-start | bytes 24584 | tf_op jit(solution)/shard_map/ppermute | solution.py:370
  20.7 0.6 %shard_map.62 = f32[3,256]{1,0:T(4,128)} custom-call(f32[8,128]{1,0:T(8,128)S(1)} %slice.23.packed_ref), custom_call_target="tpu_custom_call" | custom-call | flops 1000 | bytes 1000 | tf_op jit(solution)/shard_map/pallas_call | solution.py:270
  21.3 1.1 %collective-permute-done.6 = f32[16,128]{1,0:T(8,128)S(1)} collective-permute-done((f32[16,128]{1,0:T(8,128)S(1)}, f32[16,128]{1,0:T(8,128)S(1)}, u32[]{:S(2)}, u32[]{:S(2)}) %collective-permute-start.6) | collective-permute-done | bytes 8224 | tf_op jit(solution)/shard_map/ppermute | solution.py:370
  22.4 1.4 %collective-permute-start.7 = (f32[16,128]{1,0:T(8,128)S(1)}, f32[16,128]{1,0:T(8,128)S(1)}, u32[]{:S(2)}, u32[]{:S(2)}) collective-permute-start(f32[16,128]{1,0:T(8,128)S(1)} %slice_add_fusion.1), channel_id=1, source_target_pairs={{0,9},{1,8},{4,13},{5,12},{8,1},{9,0},{12,5},{13,4},{2,11},{3,10},... | collective-permute-start | bytes 24584 | tf_op jit(solution)/shard_map/ppermute | solution.py:370
  23.9 2.5 %collective-permute-done.7 = f32[16,128]{1,0:T(8,128)S(1)} collective-permute-done((f32[16,128]{1,0:T(8,128)S(1)}, f32[16,128]{1,0:T(8,128)S(1)}, u32[]{:S(2)}, u32[]{:S(2)}) %collective-permute-start.7) | collective-permute-done | bytes 8224 | tf_op jit(solution)/shard_map/ppermute | solution.py:370
  26.4 0.7 %shard_map.63 = f32[1,9]{1,0:T(1,128)} custom-call(s32[1]{0:T(128)} %bitcast.2.first_ref, f32[16,128]{1,0:T(8,128)S(1)} %add.23.sums_ref), custom_call_target="tpu_custom_call" | custom-call | flops 1000 | bytes 1000 | tf_op jit(solution)/shard_map/pallas_call | solution.py:270
  (15 shorter events, 0.1 us)
Async XLA Ops:
  1.4 3.2 %collective-permute-start = (f32[4,256]{1,0:T(4,128)S(1)}, f32[4,256]{1,0:T(4,128)S(1)}, u32[]{:S(2)}, u32[]{:S(2)}) collective-permute-start(f32[4,256]{1,0:T(4,128)S(1)} %get-tuple-element.14), channel_id=1, source_target_pairs={{0,1},{1,0},{2,3},{3,2},{4,5},{5,4},{6,7},{7,6},{8,9},{9,8},{10,11... | collective-permute-start | bytes 12296 | tf_op jit(solution)/shard_map/ppermute | solution.py:323
  1.9 4.0 %collective-permute-start.2 = (f32[6,256]{1,0:T(8,128)S(1)}, f32[6,256]{1,0:T(8,128)S(1)}, u32[]{:S(2)}, u32[]{:S(2)}) collective-permute-start(f32[6,256]{1,0:T(8,128)S(1)} %get-tuple-element.15), channel_id=1, source_target_pairs={{0,5},{1,4},{4,1},{5,0},{8,13},{9,12},{12,9},{13,8},{2,7},{3,6},{6... | collective-permute-start | bytes 18440 | tf_op jit(solution)/shard_map/ppermute | solution.py:328
  4.6 4.1 %collective-permute-start.1 = (f32[4,512]{1,0:T(4,128)S(1)}, f32[4,512]{1,0:T(4,128)S(1)}, u32[]{:S(2)}, u32[]{:S(2)}) collective-permute-start(f32[4,512]{1,0:T(4,128)S(1)} %pad_maximum_fusion.1), channel_id=1, source_target_pairs={{0,3},{1,2},{2,1},{3,0},{4,7},{5,6},{6,5},{7,4},{8,11},{9,10},{10,... | collective-permute-start | bytes 24584 | tf_op jit(solution)/shard_map/ppermute | solution.py:323
  6.0 5.8 %collective-permute-start.3 = (f32[6,512]{1,0:T(8,128)S(1)}, f32[6,512]{1,0:T(8,128)S(1)}, u32[]{:S(2)}, u32[]{:S(2)}) collective-permute-start(f32[6,512]{1,0:T(8,128)S(1)} %constant_dynamic-update-slice_fusion.3.source_ref), channel_id=1, source_target_pairs={{0,9},{1,8},{4,13},{5,12},{8,1},{9,0},{12,5},{13,4},{2,11},{3,10},... | collective-permute-start | bytes 36872 | tf_op jit(solution)/shard_map/ppermute | solution.py:328
  14.9 3.2 %collective-permute-start.4 = (f32[32,128]{1,0:T(8,128)S(1)}, f32[32,128]{1,0:T(8,128)S(1)}, u32[]{:S(2)}, u32[]{:S(2)}) collective-permute-start(f32[32,128]{1,0:T(8,128)S(1)} %get-tuple-element.23), channel_id=1, source_target_pairs={{0,3},{1,2},{2,1},{3,0},{4,7},{5,6},{6,5},{7,4},{8,11},{9,10},{10,... | collective-permute-start | bytes 49160 | tf_op jit(solution)/shard_map/ppermute | solution.py:366
  18.1 1.2 %collective-permute-start.5 = (f32[24,128]{1,0:T(8,128)S(1)}, f32[24,128]{1,0:T(8,128)S(1)}, u32[]{:S(2)}, u32[]{:S(2)}) collective-permute-start(f32[24,128]{1,0:T(8,128)S(1)} %pad_maximum_fusion), channel_id=1, source_target_pairs={{0,1},{1,0},{2,3},{3,2},{4,5},{5,4},{6,7},{7,6},{8,9},{9,8},{10,11... | collective-permute-start | bytes 36872 | tf_op jit(solution)/shard_map/ppermute | solution.py:366
  19.4 3.1 %collective-permute-start.6 = (f32[16,128]{1,0:T(8,128)S(1)}, f32[16,128]{1,0:T(8,128)S(1)}, u32[]{:S(2)}, u32[]{:S(2)}) collective-permute-start(f32[16,128]{1,0:T(8,128)S(1)} %slice.24), channel_id=1, source_target_pairs={{0,5},{1,4},{4,1},{5,0},{8,13},{9,12},{12,9},{13,8},{2,7},{3,6},{6... | collective-permute-start | bytes 24584 | tf_op jit(solution)/shard_map/ppermute | solution.py:370
  22.4 4.0 %collective-permute-start.7 = (f32[16,128]{1,0:T(8,128)S(1)}, f32[16,128]{1,0:T(8,128)S(1)}, u32[]{:S(2)}, u32[]{:S(2)}) collective-permute-start(f32[16,128]{1,0:T(8,128)S(1)} %slice_add_fusion.1), channel_id=1, source_target_pairs={{0,9},{1,8},{4,13},{5,12},{8,1},{9,0},{12,5},{13,4},{2,11},{3,10},... | collective-permute-start | bytes 24584 | tf_op jit(solution)/shard_map/ppermute | solution.py:370

commit v6 on v5

--- a/solution.py
+++ b/solution.py
@@ -107,9 +107,7 @@
     target_ref[3:4, :] = member[...].astype(jnp.float32)
 
 
-def first_kernel(
-    target_ref, source_ref, owner_ref, points_ref, total_ref, match_ref, scaled
-):
+def place_targets(offset, target_ref, owner_ref, points_ref, match_ref):
     count = target_ref.shape[1]
     parts, rest = [], SCALE * target_ref[0:3, :]
     for _ in range(3):
@@ -127,19 +125,46 @@
         preferred_element_type=jnp.float32,
     )
     for k in range(3):
-        points_ref[k, :, :] = points[:, k * LANES : (k + 1) * LANES]
+        points_ref[k, offset : offset + count, :] = points[:, k * LANES : (k + 1) * LANES]
     aggregates = match_ref.shape[0]
     labels = lax.broadcasted_iota(jnp.int32, (aggregates, count), 0)
     member = jnp.where(labels == target_ref[3:4, :].astype(jnp.int32), 1.0, 0.0)
     columns = lax.broadcasted_iota(jnp.int32, (aggregates, aggregates), 0)
     owner = jnp.where(columns == owner_ref[...], 1.0, 0.0)
-    match_ref[...] = jnp.dot(
+    match_ref[:, offset : offset + count] = jnp.dot(
         owner.astype(jnp.bfloat16),
         member.astype(jnp.bfloat16),
         preferred_element_type=jnp.float32,
     ).astype(jnp.bfloat16)
 
-    add_pairs(points_ref, source_ref, None, total_ref, scaled)
+
+def first_kernel(early, target_ref, source_ref, owner_ref, *refs):
+    points_ref, total_ref, match_ref, scaled = refs[-4:]
+    near = pl.ds(0, target_ref.shape[1])
+    axis = SOURCE_AXES[0]
+    first_half = 2 * lax.axis_index(axis) < lax.axis_size(axis)
+
+    @pl.when(first_half if early else jnp.logical_not(first_half))
+    def _():
+        place_targets(0, target_ref, owner_ref, points_ref, match_ref)
+        add_pairs(points_ref.at[:, near, :], source_ref, None, total_ref.at[:, near, :], scaled)
+
+
+def middle_kernel(count, target_ref, source_ref, owner_ref, *refs):
+    points_ref, total_ref, match_ref, scaled = refs[-4:]
+    half, sources = target_ref.shape[1], source_ref.shape[1]
+    near, far, rest = pl.ds(0, half), pl.ds(half, half), sources - count
+    some = total_ref.at[:, near, :]
+    if rest:
+        add_pairs(
+            points_ref.at[:, near, :],
+            source_ref.at[:, pl.ds(count, rest)],
+            some,
+            some,
+            scaled.at[:, pl.ds(0, rest)],
+        )
+    place_targets(half, target_ref, owner_ref, points_ref, match_ref)
+    add_pairs(points_ref.at[:, far, :], source_ref, None, total_ref.at[:, far, :], scaled)
 
 
 def last_kernel(
@@ -232,11 +257,12 @@
             out_ref[k : k + 1, block * LANES : (block + 1) * LANES] = packed_ref[row : row + 1, :]
 
 
-def rigid_kernel(first_ref, sums_ref, out_ref):
+def rigid_kernel(sums_ref, out_ref):
     columns = out_ref.shape[0]
+    first = lax.axis_index(AXES) * columns
     lane = lax.broadcasted_iota(jnp.int32, (SUM_ROWS, LANES), 1)
     for column in range(columns):
-        wanted = first_ref[0] + column
+        wanted = first + column
         mine = jnp.zeros((SUM_ROWS, LANES), jnp.float32)
         for chunk in range(sums_ref.shape[0] // SUM_ROWS):
             sums = sums_ref[chunk * SUM_ROWS : (chunk + 1) * SUM_ROWS, :]
@@ -266,13 +292,16 @@
 WHOLE = pl.BlockSpec(memory_space=pltpu.VMEM)
 
 
-def call(kernel, shapes, arguments, pairs=0, scratch=(), specs=None, vmem=8 << 20):
+def call(
+    kernel, shapes, arguments, pairs=0, scratch=(), specs=None, vmem=8 << 20, aliases={}
+):
     return pl.pallas_call(
         kernel,
         out_shape=[jax.ShapeDtypeStruct(shape, dtype) for shape, dtype in shapes],
         in_specs=specs or [WHOLE] * len(arguments),
         out_specs=[WHOLE] * len(shapes),
         scratch_shapes=list(scratch),
+        input_output_aliases=aliases,
         compiler_params=pltpu.CompilerParams(vmem_limit_bytes=vmem),
         cost_estimate=pl.CostEstimate(
             flops=40 * pairs + 1000, bytes_accessed=1000, transcendentals=pairs
@@ -316,31 +345,64 @@
         specs=[pl.BlockSpec(memory_space=pltpu.HBM)] * 4,
     )
 
-    coming = None
-    for number in range(max(len(source_steps), len(target_steps))):
+    arriving = coming = None
+    own = sources
+    for number in range(max(len(source_steps) - 1, len(target_steps))):
         if number < len(target_steps):
+            if number:
+                targets = jnp.concatenate([targets, arriving], axis=1)
             axis, pairs = target_steps[number]
-            targets = jnp.concatenate([targets, lax.ppermute(targets, axis, pairs)], axis=1)
-        if number < len(source_steps):
-            if coming is not None:
+            arriving = lax.ppermute(targets, axis, pairs)
+        if number < len(source_steps) - 1:
+            if number:
                 sources = jnp.concatenate([sources, coming], axis=1)
             axis, pairs = source_steps[number]
             coming = lax.ppermute(sources, axis, pairs)
-    seen = targets.shape[1]
-    scaled = pltpu.VMEM((2 * SUBLANES, sources.shape[1]), real)
+    half = targets.shape[1]
+    seen = 2 * half
     vmem = (8 << 20) + 4 * (4 * 3 * seen * LANES)
+    shapes = [
+        ((3, seen, LANES), real),
+        ((3, seen, LANES), real),
+        ((aggregates, seen), jnp.bfloat16),
+    ]
+
+    def scaled(width):
+        return pltpu.VMEM((2 * SUBLANES, width), real)
+
+    filled = call(
+        functools.partial(first_kernel, True),
+        shapes,
+        (targets, own, owner),
+        pairs=half * count,
+        scratch=[scaled(count)],
+        vmem=vmem,
+    )
+    if coming is not None:
+        *filled, coming = lax.optimization_barrier((*filled, coming))
+        sources = jnp.concatenate([sources, coming], axis=1)
+    axis, pairs = source_steps[-1]
+    coming = lax.ppermute(sources, axis, pairs)
+    filled = call(
+        functools.partial(first_kernel, False),
+        shapes,
+        (targets, own, owner, *filled),
+        pairs=half * count,
+        scratch=[scaled(count)],
+        vmem=vmem,
+        aliases={3: 0, 4: 1, 5: 2},
+    )
+    *filled, arriving = lax.optimization_barrier((*filled, arriving))
     points, total, match = call(
-        first_kernel,
-        [
-            ((3, seen, LANES), real),
-            ((3, seen, LANES), real),
-            ((aggregates, seen), jnp.bfloat16),
-        ],
-        (targets, sources, owner),
-        pairs=seen * sources.shape[1],
-        scratch=[scaled],
+        functools.partial(middle_kernel, count),
+        shapes,
+        (arriving, sources, owner, *filled),
+        pairs=seen * sources.shape[1] - half * count,
+        scratch=[scaled(sources.shape[1])],
         vmem=vmem,
-    )
+        aliases={3: 0, 4: 1, 5: 2},
+    )
+    targets = jnp.concatenate([targets, arriving], axis=1)
     total, coming = lax.optimization_barrier((total, coming))
     first_row, units = sum_rows(aggregates), seen // count
     unit_rows = velocity_rows(count)
@@ -352,7 +414,7 @@
         pairs=seen * coming.shape[1],
         scratch=[
             pltpu.VMEM((3, seen + LANES, LANES), real),
-            scaled,
+            scaled(sources.shape[1]),
             pltpu.VMEM((seen // LANES + 1, SUBLANES, LANES), real),
         ],
         vmem=vmem,
@@ -373,13 +435,7 @@
             velocity, coming = lax.optimization_barrier((velocity, coming))
         sums = sums + coming
     columns = aggregates // devices
-    first = (lax.axis_index(AXES) * columns).astype(jnp.int32).reshape(1)
-    (rigid,) = call(
-        rigid_kernel,
-        [((columns, 9), real)],
-        (first, sums),
-        specs=[pl.BlockSpec(memory_space=pltpu.SMEM), WHOLE],
-    )
+    (rigid,) = call(rigid_kernel, [((columns, 9), real)], (sums,))
     return velocity, rigid.T
 
 

time: 27.3 us -> 26.6 us (0.974)
  waiting for transfers between devices: 6.84 us -> 6.2 us
  starting transfers between devices: 11.4 us -> 11.1 us
    ppermute x2, starting transfers between devices: 5.4 us -> 4.5 us  [on_device(): coming = lax.ppermute(sources, axis, pairs)]
    ppermute x2, starting transfers between devices: 1.38 us -> 1.74 us  [on_device(): both = keep + lax.ppermute(send, axis, pairs)]
    ppermute x2, waiting for transfers between devices: 3.67 us -> 3.37 us  [on_device(): coming = lax.ppermute(sums, axis, pairs)]
    ppermute x2, starting transfers between devices: 2.77 us -> 3.08 us  [on_device(): coming = lax.ppermute(sums, axis, pairs)]
    pallas_call x5 -> x7, Pallas kernels: 8.19 us -> 8.36 us  [call(): pl.pallas_call(kernel, out_shape=[jax.ShapeDtypeStruct(shape, dtype) for...]
  transfers between devices with their start and end apart: 8 -> 8, of which waited for: 5 -> 4; matrix products, arithmetic and copies ran while one was open for 0% -> 0% of each run, Pallas kernels for 13% -> 15%
where the time goes in v6:
time: 26.6 us; the launch traced here: 26.4 us
  starting transfers between devices  11.1 us (42%)
  Pallas kernels  8.36 us (31%)
  waiting for transfers between devices  6.2 us (23%)
  between operations  0.7 us (3%)
    pallas_call x7, Pallas kernels, call(): pl.pallas_call(kernel, out_shape=[jax.ShapeDtypeStruct(shape, dtype) for...  8.36 us
    ppermute x2, starting transfers between devices, on_device(): coming = lax.ppermute(sources, axis, pairs)  4.5 us
    ppermute x2, waiting for transfers between devices, on_device(): coming = lax.ppermute(sums, axis, pairs)  3.37 us
    ppermute x2, starting transfers between devices, on_device(): coming = lax.ppermute(sums, axis, pairs)  3.08 us
    ppermute x2, waiting for transfers between devices, on_device(): both = keep + lax.ppermute(send, axis, pairs)  2.82 us
    ppermute x2, starting transfers between devices, on_device(): arriving = lax.ppermute(targets, axis, pairs)  1.8 us
    ppermute x2, starting transfers between devices, on_device(): both = keep + lax.ppermute(send, axis, pairs)  1.74 us
  transfers between devices with their start and end apart: 8, of which 4 were waited for; matrix products, arithmetic and copies ran while one was open for 0% of the time, Pallas kernels for 15%

profile of v6, /device:TPU:0, one launch (start us, length us, event | category | flops | bytes accessed | tf_op | source)
XLA Modules:
  0.0 26.4 jit_solution(556221936228983851)
XLA Ops:
  0.6 0.8 %shard_map.59 = (f32[6,256]{1,0:T(8,128)S(1)}, f32[4,256]{1,0:T(4,128)S(1)}, s32[1,16]{1,0:T(1,128)S(1)}) custom-call(f32[3,256]{1,0:T(4,128)} %position_in.1, f32[3,256]{1,0:T(4,128)} %force_in.1, s32[1,256]{1,0:T(1,128)} %bitcast.3, s32[1,16]{1,0:T(1,128)} %bitcast.4), custom_call_target="tpu_custom_call" | custom-call | flops 1000 | bytes 1000 | tf_op jit(solution)/shard_map/pallas_call | solution.py:298
  1.4 0.6 %collective-permute-start = (f32[4,256]{1,0:T(4,128)S(1)}, f32[4,256]{1,0:T(4,128)S(1)}, u32[]{:S(2)}, u32[]{:S(2)}) collective-permute-start(f32[4,256]{1,0:T(4,128)S(1)} %get-tuple-element.28), channel_id=1, source_target_pairs={{0,1},{1,0},{2,3},{3,2},{4,5},{5,4},{6,7},{7,6},{8,9},{9,8},{10,11... | collective-permute-start | bytes 12296 | tf_op jit(solution)/shard_map/ppermute | solution.py:355
  1.9 2.7 %collective-permute-start.1 = (f32[6,256]{1,0:T(8,128)S(1)}, f32[6,256]{1,0:T(8,128)S(1)}, u32[]{:S(2)}, u32[]{:S(2)}) collective-permute-start(f32[6,256]{1,0:T(8,128)S(1)} %get-tuple-element.29.source_ref), channel_id=1, source_target_pairs={{0,5},{1,4},{4,1},{5,0},{8,13},{9,12},{12,9},{13,8},{2,7},{3,6},{6... | collective-permute-start | bytes 18440 | tf_op jit(solution)/shard_map/ppermute | solution.py:360
  4.6 0.0 collective-permute-done
  4.6 1.2 %collective-permute-start.2 = (f32[4,512]{1,0:T(4,128)S(1)}, f32[4,512]{1,0:T(4,128)S(1)}, u32[]{:S(2)}, u32[]{:S(2)}) collective-permute-start(f32[4,512]{1,0:T(4,128)S(1)} %constant_dynamic-update-slice_fusion.target_ref), channel_id=1, source_target_pairs={{0,3},{1,2},{2,1},{3,0},{4,7},{5,6},{6,5},{7,4},{8,11},{9,10},{10,... | collective-permute-start | bytes 24584 | tf_op jit(solution)/shard_map/ppermute | solution.py:355
  5.9 1.0 %shard_map.60 = (f32[3,1024,128]{2,1,0:T(8,128)S(1)}, f32[3,1024,128]{2,1,0:T(8,128)S(1)}, bf16[16,1024]{1,0:T(8,128)(2,1)S(1)}) custom-call(f32[4,512]{1,0:T(4,128)S(1)} %constant_dynamic-update-slice_fusion.target_ref, f32[6,256]{1,0:T(8,128)S(1)} %get-tuple-element.29.source_ref, s32[1,16]{1,0:T(1,128)S(1)} %get-tuple-element.30.owner_ref), custom_call_target="tpu_custom_call" | custom-call | flops 5243880 | bytes 1000 | tf_op jit(solution)/shard_map/pallas_call | solution.py:298
  6.9 0.0 collective-permute-done.1
  6.9 1.8 %collective-permute-start.3 = (f32[6,512]{1,0:T(8,128)S(1)}, f32[6,512]{1,0:T(8,128)S(1)}, u32[]{:S(2)}, u32[]{:S(2)}) collective-permute-start(f32[6,512]{1,0:T(8,128)S(1)} %constant_dynamic-update-slice_fusion.2.source_ref), channel_id=1, source_target_pairs={{0,9},{1,8},{4,13},{5,12},{8,1},{9,0},{12,5},{13,4},{2,11},{3,10},... | collective-permute-start | bytes 36872 | tf_op jit(solution)/shard_map/ppermute | solution.py:385
  8.7 0.0 collective-permute-done.2.target_ref
  8.7 2.3 %shard_map.62 = (f32[3,1024,128]{2,1,0:T(8,128)S(1)}, f32[3,1024,128]{2,1,0:T(8,128)S(1)}, bf16[16,1024]{1,0:T(8,128)(2,1)S(1)}) custom-call(f32[4,512]{1,0:T(4,128)S(1)} %collective-permute-done.2.target_ref, f32[6,512]{1,0:T(8,128)S(1)} %constant_dynamic-update-slice_fusion.2.source_ref, ...), custom_call_target="tpu_custom_call", output_to_operand_aliasing={{0}: (3, {}), {1}: (4, {}), {2}: (5, {})} | custom-call | flops 15729640 | bytes 1000 | tf_op jit(solution)/shard_map/pallas_call | solution.py:298
  11.0 0.0 collective-permute-done.3.source_ref
  11.0 3.0 %shard_map.63 = (f32[32,128]{1,0:T(8,128)S(1)}, f32[32,128]{1,0:T(8,128)S(1)}) custom-call(f32[3,1024,128]{2,1,0:T(8,128)S(1)} %get-tuple-element.45.points_ref, f32[6,512]{1,0:T(8,128)S(1)} %collective-permute-done.3.source_ref, f32[3,1024,128]{2,1,0:T(8,128)S(1)} %get-tuple-element.48.before_ref, bf16[16,1024]{1,0:T(8,128)(2,1)S(1)} %get-tuple-element.49.match_ref, ...), custom_call_target="tpu_custom_call" | custom-call | flops 20972520 | bytes 1000 | tf_op jit(solution)/shard_map/pallas_call | solution.py:298
  14.1 1.2 %collective-permute-start.4 = (f32[32,128]{1,0:T(8,128)S(1)}, f32[32,128]{1,0:T(8,128)S(1)}, u32[]{:S(2)}, u32[]{:S(2)}) collective-permute-start(f32[32,128]{1,0:T(8,128)S(1)} %get-tuple-element.51), channel_id=1, source_target_pairs={{0,3},{1,2},{2,1},{3,0},{4,7},{5,6},{6,5},{7,4},{8,11},{9,10},{10,... | collective-permute-start | bytes 49160 | tf_op jit(solution)/shard_map/ppermute | solution.py:428
  15.3 2.0 %collective-permute-done.4 = f32[32,128]{1,0:T(8,128)S(1)} collective-permute-done((f32[32,128]{1,0:T(8,128)S(1)}, f32[32,128]{1,0:T(8,128)S(1)}, u32[]{:S(2)}, u32[]{:S(2)}) %collective-permute-start.4) | collective-permute-done | bytes 16416 | tf_op jit(solution)/shard_map/ppermute | solution.py:428
  17.3 0.5 %collective-permute-start.5 = (f32[24,128]{1,0:T(8,128)S(1)}, f32[24,128]{1,0:T(8,128)S(1)}, u32[]{:S(2)}, u32[]{:S(2)}) collective-permute-start(f32[24,128]{1,0:T(8,128)S(1)} %pad_maximum_fusion.1), channel_id=1, source_target_pairs={{0,1},{1,0},{2,3},{3,2},{4,5},{5,4},{6,7},{7,6},{8,9},{9,8},{10,11... | collective-permute-start | bytes 36872 | tf_op jit(solution)/shard_map/ppermute | solution.py:428
  17.8 0.8 %collective-permute-done.5 = f32[24,128]{1,0:T(8,128)S(1)} collective-permute-done((f32[24,128]{1,0:T(8,128)S(1)}, f32[24,128]{1,0:T(8,128)S(1)}, u32[]{:S(2)}, u32[]{:S(2)}) %collective-permute-start.5) | collective-permute-done | bytes 12320 | tf_op jit(solution)/shard_map/ppermute | solution.py:428
  18.7 1.2 %collective-permute-start.6 = (f32[16,128]{1,0:T(8,128)S(1)}, f32[16,128]{1,0:T(8,128)S(1)}, u32[]{:S(2)}, u32[]{:S(2)}) collective-permute-start(f32[16,128]{1,0:T(8,128)S(1)} %slice.24), channel_id=1, source_target_pairs={{0,5},{1,4},{4,1},{5,0},{8,13},{9,12},{12,9},{13,8},{2,7},{3,6},{6... | collective-permute-start | bytes 24584 | tf_op jit(solution)/shard_map/ppermute | solution.py:432
  19.9 0.6 %shard_map.64 = f32[3,256]{1,0:T(4,128)} custom-call(f32[8,128]{1,0:T(8,128)S(1)} %slice.23.packed_ref), custom_call_target="tpu_custom_call" | custom-call | flops 1000 | bytes 1000 | tf_op jit(solution)/shard_map/pallas_call | solution.py:298
  20.5 1.3 %collective-permute-done.6 = f32[16,128]{1,0:T(8,128)S(1)} collective-permute-done((f32[16,128]{1,0:T(8,128)S(1)}, f32[16,128]{1,0:T(8,128)S(1)}, u32[]{:S(2)}, u32[]{:S(2)}) %collective-permute-start.6) | collective-permute-done | bytes 8224 | tf_op jit(solution)/shard_map/ppermute | solution.py:432
  21.8 1.9 %collective-permute-start.7 = (f32[16,128]{1,0:T(8,128)S(1)}, f32[16,128]{1,0:T(8,128)S(1)}, u32[]{:S(2)}, u32[]{:S(2)}) collective-permute-start(f32[16,128]{1,0:T(8,128)S(1)} %slice_add_fusion.1), channel_id=1, source_target_pairs={{0,9},{1,8},{4,13},{5,12},{8,1},{9,0},{12,5},{13,4},{2,11},{3,10},... | collective-permute-start | bytes 24584 | tf_op jit(solution)/shard_map/ppermute | solution.py:432
  23.6 2.1 %collective-permute-done.7 = f32[16,128]{1,0:T(8,128)S(1)} collective-permute-done((f32[16,128]{1,0:T(8,128)S(1)}, f32[16,128]{1,0:T(8,128)S(1)}, u32[]{:S(2)}, u32[]{:S(2)}) %collective-permute-start.7) | collective-permute-done | bytes 8224 | tf_op jit(solution)/shard_map/ppermute | solution.py:432
  25.7 0.7 %shard_map.65 = f32[1,9]{1,0:T(1,128)} custom-call(f32[16,128]{1,0:T(8,128)S(1)} %add.15.sums_ref), custom_call_target="tpu_custom_call" | custom-call | flops 1000 | bytes 1000 | tf_op jit(solution)/shard_map/pallas_call | solution.py:298
  (15 shorter events, 0.1 us)
Async XLA Ops:
  1.4 3.2 %collective-permute-start = (f32[4,256]{1,0:T(4,128)S(1)}, f32[4,256]{1,0:T(4,128)S(1)}, u32[]{:S(2)}, u32[]{:S(2)}) collective-permute-start(f32[4,256]{1,0:T(4,128)S(1)} %get-tuple-element.28), channel_id=1, source_target_pairs={{0,1},{1,0},{2,3},{3,2},{4,5},{5,4},{6,7},{7,6},{8,9},{9,8},{10,11... | collective-permute-start | bytes 12296 | tf_op jit(solution)/shard_map/ppermute | solution.py:355
  1.9 4.9 %collective-permute-start.1 = (f32[6,256]{1,0:T(8,128)S(1)}, f32[6,256]{1,0:T(8,128)S(1)}, u32[]{:S(2)}, u32[]{:S(2)}) collective-permute-start(f32[6,256]{1,0:T(8,128)S(1)} %get-tuple-element.29.source_ref), channel_id=1, source_target_pairs={{0,5},{1,4},{4,1},{5,0},{8,13},{9,12},{12,9},{13,8},{2,7},{3,6},{6... | collective-permute-start | bytes 18440 | tf_op jit(solution)/shard_map/ppermute | solution.py:360
  4.6 4.1 %collective-permute-start.2 = (f32[4,512]{1,0:T(4,128)S(1)}, f32[4,512]{1,0:T(4,128)S(1)}, u32[]{:S(2)}, u32[]{:S(2)}) collective-permute-start(f32[4,512]{1,0:T(4,128)S(1)} %constant_dynamic-update-slice_fusion.target_ref), channel_id=1, source_target_pairs={{0,3},{1,2},{2,1},{3,0},{4,7},{5,6},{6,5},{7,4},{8,11},{9,10},{10,... | collective-permute-start | bytes 24584 | tf_op jit(solution)/shard_map/ppermute | solution.py:355
  6.9 4.1 %collective-permute-start.3 = (f32[6,512]{1,0:T(8,128)S(1)}, f32[6,512]{1,0:T(8,128)S(1)}, u32[]{:S(2)}, u32[]{:S(2)}) collective-permute-start(f32[6,512]{1,0:T(8,128)S(1)} %constant_dynamic-update-slice_fusion.2.source_ref), channel_id=1, source_target_pairs={{0,9},{1,8},{4,13},{5,12},{8,1},{9,0},{12,5},{13,4},{2,11},{3,10},... | collective-permute-start | bytes 36872 | tf_op jit(solution)/shard_map/ppermute | solution.py:385
  14.1 3.2 %collective-permute-start.4 = (f32[32,128]{1,0:T(8,128)S(1)}, f32[32,128]{1,0:T(8,128)S(1)}, u32[]{:S(2)}, u32[]{:S(2)}) collective-permute-start(f32[32,128]{1,0:T(8,128)S(1)} %get-tuple-element.51), channel_id=1, source_target_pairs={{0,3},{1,2},{2,1},{3,0},{4,7},{5,6},{6,5},{7,4},{8,11},{9,10},{10,... | collective-permute-start | bytes 49160 | tf_op jit(solution)/shard_map/ppermute | solution.py:428
  17.3 1.4 %collective-permute-start.5 = (f32[24,128]{1,0:T(8,128)S(1)}, f32[24,128]{1,0:T(8,128)S(1)}, u32[]{:S(2)}, u32[]{:S(2)}) collective-permute-start(f32[24,128]{1,0:T(8,128)S(1)} %pad_maximum_fusion.1), channel_id=1, source_target_pairs={{0,1},{1,0},{2,3},{3,2},{4,5},{5,4},{6,7},{7,6},{8,9},{9,8},{10,11... | collective-permute-start | bytes 36872 | tf_op jit(solution)/shard_map/ppermute | solution.py:428
  18.7 3.1 %collective-permute-start.6 = (f32[16,128]{1,0:T(8,128)S(1)}, f32[16,128]{1,0:T(8,128)S(1)}, u32[]{:S(2)}, u32[]{:S(2)}) collective-permute-start(f32[16,128]{1,0:T(8,128)S(1)} %slice.24), channel_id=1, source_target_pairs={{0,5},{1,4},{4,1},{5,0},{8,13},{9,12},{12,9},{13,8},{2,7},{3,6},{6... | collective-permute-start | bytes 24584 | tf_op jit(solution)/shard_map/ppermute | solution.py:432
  21.8 4.0 %collective-permute-start.7 = (f32[16,128]{1,0:T(8,128)S(1)}, f32[16,128]{1,0:T(8,128)S(1)}, u32[]{:S(2)}, u32[]{:S(2)}) collective-permute-start(f32[16,128]{1,0:T(8,128)S(1)} %slice_add_fusion.1), channel_id=1, source_target_pairs={{0,9},{1,8},{4,13},{5,12},{8,1},{9,0},{12,5},{13,4},{2,11},{3,10},... | collective-permute-start | bytes 24584 | tf_op jit(solution)/shard_map/ppermute | solution.py:432

commit v7 on v6

--- a/solution.py
+++ b/solution.py
@@ -24,7 +24,9 @@
 AXES = ("tgt", "src", "sub")
 
 
-def add_pairs(points_ref, source_ref, before_ref, total_ref, scaled, beside=None, shift=0):
+def add_pairs(
+    points_ref, source_ref, before_ref, total_ref, scaled, beside=None, shift=0, unrolled=1
+):
     count = total_ref.shape[1] - shift
     blocks = source_ref.shape[1] // LANES
     together = math.gcd(blocks, BLOCKS_AT_ONCE)
@@ -49,7 +51,7 @@
         return terms if sums is None else tuple(one + term for one, term in zip(sums, terms))
 
     def tile_step(step, unused):
-        first = pl.multiple_of(step * LANES, LANES)
+        first = step * LANES if isinstance(step, int) else pl.multiple_of(step * LANES, LANES)
         if beside is not None:
             beside(first)
         for group in range(LANES // SUBLANES):
@@ -76,7 +78,12 @@
                 total_ref[k, pl.ds(first + shift + group * SUBLANES, SUBLANES), :] = sums[k]
         return unused
 
-    lax.fori_loop(0, count // LANES, tile_step, 0)
+    tiles = count // LANES
+    if tiles <= unrolled:
+        for tile in range(tiles):
+            tile_step(tile, 0)
+    else:
+        lax.fori_loop(0, tiles, tile_step, 0)
 
 
 def head_kernel(
@@ -147,7 +154,14 @@
     @pl.when(first_half if early else jnp.logical_not(first_half))
     def _():
         place_targets(0, target_ref, owner_ref, points_ref, match_ref)
-        add_pairs(points_ref.at[:, near, :], source_ref, None, total_ref.at[:, near, :], scaled)
+        add_pairs(
+            points_ref.at[:, near, :],
+            source_ref,
+            None,
+            total_ref.at[:, near, :],
+            scaled,
+            unrolled=4,
+        )
 
 
 def middle_kernel(count, target_ref, source_ref, owner_ref, *refs):
@@ -155,6 +169,7 @@
     half, sources = target_ref.shape[1], source_ref.shape[1]
     near, far, rest = pl.ds(0, half), pl.ds(half, half), sources - count
     some = total_ref.at[:, near, :]
+    place_targets(half, target_ref, owner_ref, points_ref, match_ref)
     if rest:
         add_pairs(
             points_ref.at[:, near, :],
@@ -162,8 +177,8 @@
             some,
             some,
             scaled.at[:, pl.ds(0, rest)],
+            unrolled=4,
         )
-    place_targets(half, target_ref, owner_ref, points_ref, match_ref)
     add_pairs(points_ref.at[:, far, :], source_ref, None, total_ref.at[:, far, :], scaled)
 
 

time: 26.6 us -> 26.5 us (level)
    pallas_call x7, Pallas kernels: 8.36 us -> 8.1 us  [call(): pl.pallas_call(kernel, out_shape=[jax.ShapeDtypeStruct(shape, dtype) for...]
  transfers between devices with their start and end apart: 8 -> 8, of which waited for: 4 -> 4; matrix products, arithmetic and copies ran while one was open for 0% -> 0% of each run, Pallas kernels for 15% -> 14%
where the time goes in v7:
time: 26.5 us; the launch traced here: 26.3 us
  starting transfers between devices  11.1 us (42%)
  Pallas kernels  8.1 us (31%)
  waiting for transfers between devices  6.29 us (24%)
  between operations  0.7 us (3%)
    pallas_call x7, Pallas kernels, call(): pl.pallas_call(kernel, out_shape=[jax.ShapeDtypeStruct(shape, dtype) for...  8.1 us
    ppermute x2, starting transfers between devices, on_device(): coming = lax.ppermute(sources, axis, pairs)  4.64 us
    ppermute x2, waiting for transfers between devices, on_device(): coming = lax.ppermute(sums, axis, pairs)  3.46 us
    ppermute x2, starting transfers between devices, on_device(): coming = lax.ppermute(sums, axis, pairs)  2.99 us
    ppermute x2, waiting for transfers between devices, on_device(): both = keep + lax.ppermute(send, axis, pairs)  2.82 us
    ppermute x2, starting transfers between devices, on_device(): arriving = lax.ppermute(targets, axis, pairs)  1.8 us
    ppermute x2, starting transfers between devices, on_device(): both = keep + lax.ppermute(send, axis, pairs)  1.71 us
  transfers between devices with their start and end apart: 8, of which 4 were waited for; matrix products, arithmetic and copies ran while one was open for 0% of the time, Pallas kernels for 14%

profile of v7, /device:TPU:0, one launch (start us, length us, event | category | flops | bytes accessed | tf_op | source)
XLA Modules:
  0.0 26.3 jit_solution(10885447951577667157)
XLA Ops:
  0.6 0.8 %shard_map.59 = (f32[6,256]{1,0:T(8,128)S(1)}, f32[4,256]{1,0:T(4,128)S(1)}, s32[1,16]{1,0:T(1,128)S(1)}) custom-call(f32[3,256]{1,0:T(4,128)} %position_in.1, f32[3,256]{1,0:T(4,128)} %force_in.1, s32[1,256]{1,0:T(1,128)} %bitcast.3, s32[1,16]{1,0:T(1,128)} %bitcast.4), custom_call_target="tpu_custom_call" | custom-call | flops 1000 | bytes 1000 | tf_op jit(solution)/shard_map/pallas_call | solution.py:313
  1.4 0.6 %collective-permute-start = (f32[4,256]{1,0:T(4,128)S(1)}, f32[4,256]{1,0:T(4,128)S(1)}, u32[]{:S(2)}, u32[]{:S(2)}) collective-permute-start(f32[4,256]{1,0:T(4,128)S(1)} %get-tuple-element.28), channel_id=1, source_target_pairs={{0,1},{1,0},{2,3},{3,2},{4,5},{5,4},{6,7},{7,6},{8,9},{9,8},{10,11... | collective-permute-start | bytes 12296 | tf_op jit(solution)/shard_map/ppermute | solution.py:370
  1.9 2.7 %collective-permute-start.1 = (f32[6,256]{1,0:T(8,128)S(1)}, f32[6,256]{1,0:T(8,128)S(1)}, u32[]{:S(2)}, u32[]{:S(2)}) collective-permute-start(f32[6,256]{1,0:T(8,128)S(1)} %get-tuple-element.29.source_ref), channel_id=1, source_target_pairs={{0,5},{1,4},{4,1},{5,0},{8,13},{9,12},{12,9},{13,8},{2,7},{3,6},{6... | collective-permute-start | bytes 18440 | tf_op jit(solution)/shard_map/ppermute | solution.py:375
  4.6 0.0 collective-permute-done
  4.6 1.2 %collective-permute-start.2 = (f32[4,512]{1,0:T(4,128)S(1)}, f32[4,512]{1,0:T(4,128)S(1)}, u32[]{:S(2)}, u32[]{:S(2)}) collective-permute-start(f32[4,512]{1,0:T(4,128)S(1)} %constant_dynamic-update-slice_fusion.target_ref), channel_id=1, source_target_pairs={{0,3},{1,2},{2,1},{3,0},{4,7},{5,6},{6,5},{7,4},{8,11},{9,10},{10,... | collective-permute-start | bytes 24584 | tf_op jit(solution)/shard_map/ppermute | solution.py:370
  5.9 0.8 %shard_map.60 = (f32[3,1024,128]{2,1,0:T(8,128)S(1)}, f32[3,1024,128]{2,1,0:T(8,128)S(1)}, bf16[16,1024]{1,0:T(8,128)(2,1)S(1)}) custom-call(f32[4,512]{1,0:T(4,128)S(1)} %constant_dynamic-update-slice_fusion.target_ref, f32[6,256]{1,0:T(8,128)S(1)} %get-tuple-element.29.source_ref, s32[1,16]{1,0:T(1,128)S(1)} %get-tuple-element.30.owner_ref), custom_call_target="tpu_custom_call" | custom-call | flops 5243880 | bytes 1000 | tf_op jit(solution)/shard_map/pallas_call | solution.py:313
  6.7 0.0 collective-permute-done.1
  6.7 2.0 %collective-permute-start.3 = (f32[6,512]{1,0:T(8,128)S(1)}, f32[6,512]{1,0:T(8,128)S(1)}, u32[]{:S(2)}, u32[]{:S(2)}) collective-permute-start(f32[6,512]{1,0:T(8,128)S(1)} %constant_dynamic-update-slice_fusion.2.source_ref), channel_id=1, source_target_pairs={{0,9},{1,8},{4,13},{5,12},{8,1},{9,0},{12,5},{13,4},{2,11},{3,10},... | collective-permute-start | bytes 36872 | tf_op jit(solution)/shard_map/ppermute | solution.py:400
  8.7 0.0 collective-permute-done.2.target_ref
  8.7 2.2 %shard_map.62 = (f32[3,1024,128]{2,1,0:T(8,128)S(1)}, f32[3,1024,128]{2,1,0:T(8,128)S(1)}, bf16[16,1024]{1,0:T(8,128)(2,1)S(1)}) custom-call(f32[4,512]{1,0:T(4,128)S(1)} %collective-permute-done.2.target_ref, f32[6,512]{1,0:T(8,128)S(1)} %constant_dynamic-update-slice_fusion.2.source_ref, ...), custom_call_target="tpu_custom_call", output_to_operand_aliasing={{0}: (3, {}), {1}: (4, {}), {2}: (5, {})} | custom-call | flops 15729640 | bytes 1000 | tf_op jit(solution)/shard_map/pallas_call | solution.py:313
  10.9 0.0 collective-permute-done.3.source_ref
  10.9 3.0 %shard_map.63 = (f32[32,128]{1,0:T(8,128)S(1)}, f32[32,128]{1,0:T(8,128)S(1)}) custom-call(f32[3,1024,128]{2,1,0:T(8,128)S(1)} %get-tuple-element.45.points_ref, f32[6,512]{1,0:T(8,128)S(1)} %collective-permute-done.3.source_ref, f32[3,1024,128]{2,1,0:T(8,128)S(1)} %get-tuple-element.48.before_ref, bf16[16,1024]{1,0:T(8,128)(2,1)S(1)} %get-tuple-element.49.match_ref, ...), custom_call_target="tpu_custom_call" | custom-call | flops 20972520 | bytes 1000 | tf_op jit(solution)/shard_map/pallas_call | solution.py:313
  14.0 1.2 %collective-permute-start.4 = (f32[32,128]{1,0:T(8,128)S(1)}, f32[32,128]{1,0:T(8,128)S(1)}, u32[]{:S(2)}, u32[]{:S(2)}) collective-permute-start(f32[32,128]{1,0:T(8,128)S(1)} %get-tuple-element.51), channel_id=1, source_target_pairs={{0,3},{1,2},{2,1},{3,0},{4,7},{5,6},{6,5},{7,4},{8,11},{9,10},{10,... | collective-permute-start | bytes 49160 | tf_op jit(solution)/shard_map/ppermute | solution.py:443
  15.2 2.0 %collective-permute-done.4 = f32[32,128]{1,0:T(8,128)S(1)} collective-permute-done((f32[32,128]{1,0:T(8,128)S(1)}, f32[32,128]{1,0:T(8,128)S(1)}, u32[]{:S(2)}, u32[]{:S(2)}) %collective-permute-start.4) | collective-permute-done | bytes 16416 | tf_op jit(solution)/shard_map/ppermute | solution.py:443
  17.2 0.5 %collective-permute-start.5 = (f32[24,128]{1,0:T(8,128)S(1)}, f32[24,128]{1,0:T(8,128)S(1)}, u32[]{:S(2)}, u32[]{:S(2)}) collective-permute-start(f32[24,128]{1,0:T(8,128)S(1)} %pad_maximum_fusion.1), channel_id=1, source_target_pairs={{0,1},{1,0},{2,3},{3,2},{4,5},{5,4},{6,7},{7,6},{8,9},{9,8},{10,11... | collective-permute-start | bytes 36872 | tf_op jit(solution)/shard_map/ppermute | solution.py:443
  17.7 0.8 %collective-permute-done.5 = f32[24,128]{1,0:T(8,128)S(1)} collective-permute-done((f32[24,128]{1,0:T(8,128)S(1)}, f32[24,128]{1,0:T(8,128)S(1)}, u32[]{:S(2)}, u32[]{:S(2)}) %collective-permute-start.5) | collective-permute-done | bytes 12320 | tf_op jit(solution)/shard_map/ppermute | solution.py:443
  18.5 1.2 %collective-permute-start.6 = (f32[16,128]{1,0:T(8,128)S(1)}, f32[16,128]{1,0:T(8,128)S(1)}, u32[]{:S(2)}, u32[]{:S(2)}) collective-permute-start(f32[16,128]{1,0:T(8,128)S(1)} %slice.24), channel_id=1, source_target_pairs={{0,5},{1,4},{4,1},{5,0},{8,13},{9,12},{12,9},{13,8},{2,7},{3,6},{6... | collective-permute-start | bytes 24584 | tf_op jit(solution)/shard_map/ppermute | solution.py:447
  19.8 0.6 %shard_map.64 = f32[3,256]{1,0:T(4,128)} custom-call(f32[8,128]{1,0:T(8,128)S(1)} %slice.23.packed_ref), custom_call_target="tpu_custom_call" | custom-call | flops 1000 | bytes 1000 | tf_op jit(solution)/shard_map/pallas_call | solution.py:313
  20.4 1.2 %collective-permute-done.6 = f32[16,128]{1,0:T(8,128)S(1)} collective-permute-done((f32[16,128]{1,0:T(8,128)S(1)}, f32[16,128]{1,0:T(8,128)S(1)}, u32[]{:S(2)}, u32[]{:S(2)}) %collective-permute-start.6) | collective-permute-done | bytes 8224 | tf_op jit(solution)/shard_map/ppermute | solution.py:447
  21.6 1.7 %collective-permute-start.7 = (f32[16,128]{1,0:T(8,128)S(1)}, f32[16,128]{1,0:T(8,128)S(1)}, u32[]{:S(2)}, u32[]{:S(2)}) collective-permute-start(f32[16,128]{1,0:T(8,128)S(1)} %slice_add_fusion.1), channel_id=1, source_target_pairs={{0,9},{1,8},{4,13},{5,12},{8,1},{9,0},{12,5},{13,4},{2,11},{3,10},... | collective-permute-start | bytes 24584 | tf_op jit(solution)/shard_map/ppermute | solution.py:447
  23.4 2.2 %collective-permute-done.7 = f32[16,128]{1,0:T(8,128)S(1)} collective-permute-done((f32[16,128]{1,0:T(8,128)S(1)}, f32[16,128]{1,0:T(8,128)S(1)}, u32[]{:S(2)}, u32[]{:S(2)}) %collective-permute-start.7) | collective-permute-done | bytes 8224 | tf_op jit(solution)/shard_map/ppermute | solution.py:447
  25.6 0.7 %shard_map.65 = f32[1,9]{1,0:T(1,128)} custom-call(f32[16,128]{1,0:T(8,128)S(1)} %add.15.sums_ref), custom_call_target="tpu_custom_call" | custom-call | flops 1000 | bytes 1000 | tf_op jit(solution)/shard_map/pallas_call | solution.py:313
  (15 shorter events, 0.1 us)
Async XLA Ops:
  1.4 3.2 %collective-permute-start = (f32[4,256]{1,0:T(4,128)S(1)}, f32[4,256]{1,0:T(4,128)S(1)}, u32[]{:S(2)}, u32[]{:S(2)}) collective-permute-start(f32[4,256]{1,0:T(4,128)S(1)} %get-tuple-element.28), channel_id=1, source_target_pairs={{0,1},{1,0},{2,3},{3,2},{4,5},{5,4},{6,7},{7,6},{8,9},{9,8},{10,11... | collective-permute-start | bytes 12296 | tf_op jit(solution)/shard_map/ppermute | solution.py:370
  1.9 4.8 %collective-permute-start.1 = (f32[6,256]{1,0:T(8,128)S(1)}, f32[6,256]{1,0:T(8,128)S(1)}, u32[]{:S(2)}, u32[]{:S(2)}) collective-permute-start(f32[6,256]{1,0:T(8,128)S(1)} %get-tuple-element.29.source_ref), channel_id=1, source_target_pairs={{0,5},{1,4},{4,1},{5,0},{8,13},{9,12},{12,9},{13,8},{2,7},{3,6},{6... | collective-permute-start | bytes 18440 | tf_op jit(solution)/shard_map/ppermute | solution.py:375
  4.6 4.1 %collective-permute-start.2 = (f32[4,512]{1,0:T(4,128)S(1)}, f32[4,512]{1,0:T(4,128)S(1)}, u32[]{:S(2)}, u32[]{:S(2)}) collective-permute-start(f32[4,512]{1,0:T(4,128)S(1)} %constant_dynamic-update-slice_fusion.target_ref), channel_id=1, source_target_pairs={{0,3},{1,2},{2,1},{3,0},{4,7},{5,6},{6,5},{7,4},{8,11},{9,10},{10,... | collective-permute-start | bytes 24584 | tf_op jit(solution)/shard_map/ppermute | solution.py:370
  6.7 4.2 %collective-permute-start.3 = (f32[6,512]{1,0:T(8,128)S(1)}, f32[6,512]{1,0:T(8,128)S(1)}, u32[]{:S(2)}, u32[]{:S(2)}) collective-permute-start(f32[6,512]{1,0:T(8,128)S(1)} %constant_dynamic-update-slice_fusion.2.source_ref), channel_id=1, source_target_pairs={{0,9},{1,8},{4,13},{5,12},{8,1},{9,0},{12,5},{13,4},{2,11},{3,10},... | collective-permute-start | bytes 36872 | tf_op jit(solution)/shard_map/ppermute | solution.py:400
  14.0 3.2 %collective-permute-start.4 = (f32[32,128]{1,0:T(8,128)S(1)}, f32[32,128]{1,0:T(8,128)S(1)}, u32[]{:S(2)}, u32[]{:S(2)}) collective-permute-start(f32[32,128]{1,0:T(8,128)S(1)} %get-tuple-element.51), channel_id=1, source_target_pairs={{0,3},{1,2},{2,1},{3,0},{4,7},{5,6},{6,5},{7,4},{8,11},{9,10},{10,... | collective-permute-start | bytes 49160 | tf_op jit(solution)/shard_map/ppermute | solution.py:443
  17.2 1.3 %collective-permute-start.5 = (f32[24,128]{1,0:T(8,128)S(1)}, f32[24,128]{1,0:T(8,128)S(1)}, u32[]{:S(2)}, u32[]{:S(2)}) collective-permute-start(f32[24,128]{1,0:T(8,128)S(1)} %pad_maximum_fusion.1), channel_id=1, source_target_pairs={{0,1},{1,0},{2,3},{3,2},{4,5},{5,4},{6,7},{7,6},{8,9},{9,8},{10,11... | collective-permute-start | bytes 36872 | tf_op jit(solution)/shard_map/ppermute | solution.py:443
  18.5 3.1 %collective-permute-start.6 = (f32[16,128]{1,0:T(8,128)S(1)}, f32[16,128]{1,0:T(8,128)S(1)}, u32[]{:S(2)}, u32[]{:S(2)}) collective-permute-start(f32[16,128]{1,0:T(8,128)S(1)} %slice.24), channel_id=1, source_target_pairs={{0,5},{1,4},{4,1},{5,0},{8,13},{9,12},{12,9},{13,8},{2,7},{3,6},{6... | collective-permute-start | bytes 24584 | tf_op jit(solution)/shard_map/ppermute | solution.py:447
  21.6 4.0 %collective-permute-start.7 = (f32[16,128]{1,0:T(8,128)S(1)}, f32[16,128]{1,0:T(8,128)S(1)}, u32[]{:S(2)}, u32[]{:S(2)}) collective-permute-start(f32[16,128]{1,0:T(8,128)S(1)} %slice_add_fusion.1), channel_id=1, source_target_pairs={{0,9},{1,8},{4,13},{5,12},{8,1},{9,0},{12,5},{13,4},{2,11},{3,10},... | collective-permute-start | bytes 24584 | tf_op jit(solution)/shard_map/ppermute | solution.py:447

commit v8 on v7

--- a/solution.py
+++ b/solution.py
@@ -83,7 +83,7 @@
         for tile in range(tiles):
             tile_step(tile, 0)
     else:
-        lax.fori_loop(0, tiles, tile_step, 0)
+        lax.fori_loop(0, tiles, tile_step, 0, unroll=2 if tiles % 2 == 0 else 1)
 
 
 def head_kernel(
@@ -125,14 +125,17 @@
     row = lax.broadcasted_iota(jnp.int32, (16, 3 * LANES), 0)
     lane = lax.broadcasted_iota(jnp.int32, (16, 3 * LANES), 1)
     chosen = jnp.where((row % 3 == lane // LANES) & (row < 9), 1.0, 0.0)
-    points = lax.dot_general(
-        jnp.concatenate(parts, axis=0).astype(jnp.bfloat16),
-        chosen.astype(jnp.bfloat16),
-        (((0,), (0,)), ((), ())),
-        preferred_element_type=jnp.float32,
-    )
-    for k in range(3):
-        points_ref[k, offset : offset + count, :] = points[:, k * LANES : (k + 1) * LANES]
+    stacked = jnp.concatenate(parts, axis=0).astype(jnp.bfloat16)
+    for start in range(0, count, LANES):
+        points = lax.dot_general(
+            stacked[:, start : start + LANES],
+            chosen.astype(jnp.bfloat16),
+            (((0,), (0,)), ((), ())),
+            preferred_element_type=jnp.float32,
+        )
+        rows = slice(offset + start, offset + start + LANES)
+        for k in range(3):
+            points_ref[k, rows, :] = points[:, k * LANES : (k + 1) * LANES]
     aggregates = match_ref.shape[0]
     labels = lax.broadcasted_iota(jnp.int32, (aggregates, count), 0)
     member = jnp.where(labels == target_ref[3:4, :].astype(jnp.int32), 1.0, 0.0)

time: 26.5 us -> 26.5 us (level)
  no operation moved by 1% of the time
where the time goes in v8:
time: 26.5 us; the launch traced here: 26.3 us
  starting transfers between devices  11.2 us (42%)
  Pallas kernels  8.07 us (30%)
  waiting for transfers between devices  6.3 us (24%)
  between operations  0.7 us (3%)
    pallas_call x7, Pallas kernels, call(): pl.pallas_call(kernel, out_shape=[jax.ShapeDtypeStruct(shape, dtype) for...  8.07 us
    ppermute x2, starting transfers between devices, on_device(): coming = lax.ppermute(sources, axis, pairs)  4.65 us
    ppermute x2, waiting for transfers between devices, on_device(): coming = lax.ppermute(sums, axis, pairs)  3.47 us
    ppermute x2, starting transfers between devices, on_device(): coming = lax.ppermute(sums, axis, pairs)  2.98 us
    ppermute x2, waiting for transfers between devices, on_device(): both = keep + lax.ppermute(send, axis, pairs)  2.82 us
    ppermute x2, starting transfers between devices, on_device(): arriving = lax.ppermute(targets, axis, pairs)  1.8 us
    ppermute x2, starting transfers between devices, on_device(): both = keep + lax.ppermute(send, axis, pairs)  1.73 us
  transfers between devices with their start and end apart: 8, of which 4 were waited for; matrix products, arithmetic and copies ran while one was open for 0% of the time, Pallas kernels for 14%

profile of v8, /device:TPU:0, one launch (start us, length us, event | category | flops | bytes accessed | tf_op | source)
XLA Modules:
  0.0 26.3 jit_solution(8542355835467876021)
XLA Ops:
  0.6 0.8 %shard_map.59 = (f32[6,256]{1,0:T(8,128)S(1)}, f32[4,256]{1,0:T(4,128)S(1)}, s32[1,16]{1,0:T(1,128)S(1)}) custom-call(f32[3,256]{1,0:T(4,128)} %position_in.1, f32[3,256]{1,0:T(4,128)} %force_in.1, s32[1,256]{1,0:T(1,128)} %bitcast.3, s32[1,16]{1,0:T(1,128)} %bitcast.4), custom_call_target="tpu_custom_call" | custom-call | flops 1000 | bytes 1000 | tf_op jit(solution)/shard_map/pallas_call | solution.py:316
  1.4 0.6 %collective-permute-start = (f32[4,256]{1,0:T(4,128)S(1)}, f32[4,256]{1,0:T(4,128)S(1)}, u32[]{:S(2)}, u32[]{:S(2)}) collective-permute-start(f32[4,256]{1,0:T(4,128)S(1)} %get-tuple-element.28), channel_id=1, source_target_pairs={{0,1},{1,0},{2,3},{3,2},{4,5},{5,4},{6,7},{7,6},{8,9},{9,8},{10,11... | collective-permute-start | bytes 12296 | tf_op jit(solution)/shard_map/ppermute | solution.py:373
  1.9 2.7 %collective-permute-start.1 = (f32[6,256]{1,0:T(8,128)S(1)}, f32[6,256]{1,0:T(8,128)S(1)}, u32[]{:S(2)}, u32[]{:S(2)}) collective-permute-start(f32[6,256]{1,0:T(8,128)S(1)} %get-tuple-element.29.source_ref), channel_id=1, source_target_pairs={{0,5},{1,4},{4,1},{5,0},{8,13},{9,12},{12,9},{13,8},{2,7},{3,6},{6... | collective-permute-start | bytes 18440 | tf_op jit(solution)/shard_map/ppermute | solution.py:378
  4.6 0.0 collective-permute-done
  4.6 1.2 %collective-permute-start.2 = (f32[4,512]{1,0:T(4,128)S(1)}, f32[4,512]{1,0:T(4,128)S(1)}, u32[]{:S(2)}, u32[]{:S(2)}) collective-permute-start(f32[4,512]{1,0:T(4,128)S(1)} %constant_dynamic-update-slice_fusion.target_ref), channel_id=1, source_target_pairs={{0,3},{1,2},{2,1},{3,0},{4,7},{5,6},{6,5},{7,4},{8,11},{9,10},{10,... | collective-permute-start | bytes 24584 | tf_op jit(solution)/shard_map/ppermute | solution.py:373
  5.9 0.8 %shard_map.60 = (f32[3,1024,128]{2,1,0:T(8,128)S(1)}, f32[3,1024,128]{2,1,0:T(8,128)S(1)}, bf16[16,1024]{1,0:T(8,128)(2,1)S(1)}) custom-call(f32[4,512]{1,0:T(4,128)S(1)} %constant_dynamic-update-slice_fusion.target_ref, f32[6,256]{1,0:T(8,128)S(1)} %get-tuple-element.29.source_ref, s32[1,16]{1,0:T(1,128)S(1)} %get-tuple-element.30.owner_ref), custom_call_target="tpu_custom_call" | custom-call | flops 5243880 | bytes 1000 | tf_op jit(solution)/shard_map/pallas_call | solution.py:316
  6.7 0.0 collective-permute-done.1
  6.7 2.0 %collective-permute-start.3 = (f32[6,512]{1,0:T(8,128)S(1)}, f32[6,512]{1,0:T(8,128)S(1)}, u32[]{:S(2)}, u32[]{:S(2)}) collective-permute-start(f32[6,512]{1,0:T(8,128)S(1)} %constant_dynamic-update-slice_fusion.2.source_ref), channel_id=1, source_target_pairs={{0,9},{1,8},{4,13},{5,12},{8,1},{9,0},{12,5},{13,4},{2,11},{3,10},... | collective-permute-start | bytes 36872 | tf_op jit(solution)/shard_map/ppermute | solution.py:403
  8.7 0.0 collective-permute-done.2.target_ref
  8.7 2.2 %shard_map.62 = (f32[3,1024,128]{2,1,0:T(8,128)S(1)}, f32[3,1024,128]{2,1,0:T(8,128)S(1)}, bf16[16,1024]{1,0:T(8,128)(2,1)S(1)}) custom-call(f32[4,512]{1,0:T(4,128)S(1)} %collective-permute-done.2.target_ref, f32[6,512]{1,0:T(8,128)S(1)} %constant_dynamic-update-slice_fusion.2.source_ref, ...), custom_call_target="tpu_custom_call", output_to_operand_aliasing={{0}: (3, {}), {1}: (4, {}), {2}: (5, {})} | custom-call | flops 15729640 | bytes 1000 | tf_op jit(solution)/shard_map/pallas_call | solution.py:316
  10.9 0.0 collective-permute-done.3.source_ref
  10.9 3.0 %shard_map.63 = (f32[32,128]{1,0:T(8,128)S(1)}, f32[32,128]{1,0:T(8,128)S(1)}) custom-call(f32[3,1024,128]{2,1,0:T(8,128)S(1)} %get-tuple-element.45.points_ref, f32[6,512]{1,0:T(8,128)S(1)} %collective-permute-done.3.source_ref, f32[3,1024,128]{2,1,0:T(8,128)S(1)} %get-tuple-element.48.before_ref, bf16[16,1024]{1,0:T(8,128)(2,1)S(1)} %get-tuple-element.49.match_ref, ...), custom_call_target="tpu_custom_call" | custom-call | flops 20972520 | bytes 1000 | tf_op jit(solution)/shard_map/pallas_call | solution.py:316
  13.9 1.2 %collective-permute-start.4 = (f32[32,128]{1,0:T(8,128)S(1)}, f32[32,128]{1,0:T(8,128)S(1)}, u32[]{:S(2)}, u32[]{:S(2)}) collective-permute-start(f32[32,128]{1,0:T(8,128)S(1)} %get-tuple-element.51), channel_id=1, source_target_pairs={{0,3},{1,2},{2,1},{3,0},{4,7},{5,6},{6,5},{7,4},{8,11},{9,10},{10,... | collective-permute-start | bytes 49160 | tf_op jit(solution)/shard_map/ppermute | solution.py:446
  15.1 2.0 %collective-permute-done.4 = f32[32,128]{1,0:T(8,128)S(1)} collective-permute-done((f32[32,128]{1,0:T(8,128)S(1)}, f32[32,128]{1,0:T(8,128)S(1)}, u32[]{:S(2)}, u32[]{:S(2)}) %collective-permute-start.4) | collective-permute-done | bytes 16416 | tf_op jit(solution)/shard_map/ppermute | solution.py:446
  17.2 0.5 %collective-permute-start.5 = (f32[24,128]{1,0:T(8,128)S(1)}, f32[24,128]{1,0:T(8,128)S(1)}, u32[]{:S(2)}, u32[]{:S(2)}) collective-permute-start(f32[24,128]{1,0:T(8,128)S(1)} %pad_maximum_fusion.1), channel_id=1, source_target_pairs={{0,1},{1,0},{2,3},{3,2},{4,5},{5,4},{6,7},{7,6},{8,9},{9,8},{10,11... | collective-permute-start | bytes 36872 | tf_op jit(solution)/shard_map/ppermute | solution.py:446
  17.7 0.8 %collective-permute-done.5 = f32[24,128]{1,0:T(8,128)S(1)} collective-permute-done((f32[24,128]{1,0:T(8,128)S(1)}, f32[24,128]{1,0:T(8,128)S(1)}, u32[]{:S(2)}, u32[]{:S(2)}) %collective-permute-start.5) | collective-permute-done | bytes 12320 | tf_op jit(solution)/shard_map/ppermute | solution.py:446
  18.5 1.2 %collective-permute-start.6 = (f32[16,128]{1,0:T(8,128)S(1)}, f32[16,128]{1,0:T(8,128)S(1)}, u32[]{:S(2)}, u32[]{:S(2)}) collective-permute-start(f32[16,128]{1,0:T(8,128)S(1)} %slice.24), channel_id=1, source_target_pairs={{0,5},{1,4},{4,1},{5,0},{8,13},{9,12},{12,9},{13,8},{2,7},{3,6},{6... | collective-permute-start | bytes 24584 | tf_op jit(solution)/shard_map/ppermute | solution.py:450
  19.8 0.6 %shard_map.64 = f32[3,256]{1,0:T(4,128)} custom-call(f32[8,128]{1,0:T(8,128)S(1)} %slice.23.packed_ref), custom_call_target="tpu_custom_call" | custom-call | flops 1000 | bytes 1000 | tf_op jit(solution)/shard_map/pallas_call | solution.py:316
  20.4 1.2 %collective-permute-done.6 = f32[16,128]{1,0:T(8,128)S(1)} collective-permute-done((f32[16,128]{1,0:T(8,128)S(1)}, f32[16,128]{1,0:T(8,128)S(1)}, u32[]{:S(2)}, u32[]{:S(2)}) %collective-permute-start.6) | collective-permute-done | bytes 8224 | tf_op jit(solution)/shard_map/ppermute | solution.py:450
  21.6 1.7 %collective-permute-start.7 = (f32[16,128]{1,0:T(8,128)S(1)}, f32[16,128]{1,0:T(8,128)S(1)}, u32[]{:S(2)}, u32[]{:S(2)}) collective-permute-start(f32[16,128]{1,0:T(8,128)S(1)} %slice_add_fusion.1), channel_id=1, source_target_pairs={{0,9},{1,8},{4,13},{5,12},{8,1},{9,0},{12,5},{13,4},{2,11},{3,10},... | collective-permute-start | bytes 24584 | tf_op jit(solution)/shard_map/ppermute | solution.py:450
  23.4 2.2 %collective-permute-done.7 = f32[16,128]{1,0:T(8,128)S(1)} collective-permute-done((f32[16,128]{1,0:T(8,128)S(1)}, f32[16,128]{1,0:T(8,128)S(1)}, u32[]{:S(2)}, u32[]{:S(2)}) %collective-permute-start.7) | collective-permute-done | bytes 8224 | tf_op jit(solution)/shard_map/ppermute | solution.py:450
  25.6 0.7 %shard_map.65 = f32[1,9]{1,0:T(1,128)} custom-call(f32[16,128]{1,0:T(8,128)S(1)} %add.15.sums_ref), custom_call_target="tpu_custom_call" | custom-call | flops 1000 | bytes 1000 | tf_op jit(solution)/shard_map/pallas_call | solution.py:316
  (15 shorter events, 0.1 us)
Async XLA Ops:
  1.4 3.2 %collective-permute-start = (f32[4,256]{1,0:T(4,128)S(1)}, f32[4,256]{1,0:T(4,128)S(1)}, u32[]{:S(2)}, u32[]{:S(2)}) collective-permute-start(f32[4,256]{1,0:T(4,128)S(1)} %get-tuple-element.28), channel_id=1, source_target_pairs={{0,1},{1,0},{2,3},{3,2},{4,5},{5,4},{6,7},{7,6},{8,9},{9,8},{10,11... | collective-permute-start | bytes 12296 | tf_op jit(solution)/shard_map/ppermute | solution.py:373
  1.9 4.8 %collective-permute-start.1 = (f32[6,256]{1,0:T(8,128)S(1)}, f32[6,256]{1,0:T(8,128)S(1)}, u32[]{:S(2)}, u32[]{:S(2)}) collective-permute-start(f32[6,256]{1,0:T(8,128)S(1)} %get-tuple-element.29.source_ref), channel_id=1, source_target_pairs={{0,5},{1,4},{4,1},{5,0},{8,13},{9,12},{12,9},{13,8},{2,7},{3,6},{6... | collective-permute-start | bytes 18440 | tf_op jit(solution)/shard_map/ppermute | solution.py:378
  4.6 4.1 %collective-permute-start.2 = (f32[4,512]{1,0:T(4,128)S(1)}, f32[4,512]{1,0:T(4,128)S(1)}, u32[]{:S(2)}, u32[]{:S(2)}) collective-permute-start(f32[4,512]{1,0:T(4,128)S(1)} %constant_dynamic-update-slice_fusion.target_ref), channel_id=1, source_target_pairs={{0,3},{1,2},{2,1},{3,0},{4,7},{5,6},{6,5},{7,4},{8,11},{9,10},{10,... | collective-permute-start | bytes 24584 | tf_op jit(solution)/shard_map/ppermute | solution.py:373
  6.7 4.2 %collective-permute-start.3 = (f32[6,512]{1,0:T(8,128)S(1)}, f32[6,512]{1,0:T(8,128)S(1)}, u32[]{:S(2)}, u32[]{:S(2)}) collective-permute-start(f32[6,512]{1,0:T(8,128)S(1)} %constant_dynamic-update-slice_fusion.2.source_ref), channel_id=1, source_target_pairs={{0,9},{1,8},{4,13},{5,12},{8,1},{9,0},{12,5},{13,4},{2,11},{3,10},... | collective-permute-start | bytes 36872 | tf_op jit(solution)/shard_map/ppermute | solution.py:403
  13.9 3.2 %collective-permute-start.4 = (f32[32,128]{1,0:T(8,128)S(1)}, f32[32,128]{1,0:T(8,128)S(1)}, u32[]{:S(2)}, u32[]{:S(2)}) collective-permute-start(f32[32,128]{1,0:T(8,128)S(1)} %get-tuple-element.51), channel_id=1, source_target_pairs={{0,3},{1,2},{2,1},{3,0},{4,7},{5,6},{6,5},{7,4},{8,11},{9,10},{10,... | collective-permute-start | bytes 49160 | tf_op jit(solution)/shard_map/ppermute | solution.py:446
  17.2 1.4 %collective-permute-start.5 = (f32[24,128]{1,0:T(8,128)S(1)}, f32[24,128]{1,0:T(8,128)S(1)}, u32[]{:S(2)}, u32[]{:S(2)}) collective-permute-start(f32[24,128]{1,0:T(8,128)S(1)} %pad_maximum_fusion.1), channel_id=1, source_target_pairs={{0,1},{1,0},{2,3},{3,2},{4,5},{5,4},{6,7},{7,6},{8,9},{9,8},{10,11... | collective-permute-start | bytes 36872 | tf_op jit(solution)/shard_map/ppermute | solution.py:446
  18.5 3.1 %collective-permute-start.6 = (f32[16,128]{1,0:T(8,128)S(1)}, f32[16,128]{1,0:T(8,128)S(1)}, u32[]{:S(2)}, u32[]{:S(2)}) collective-permute-start(f32[16,128]{1,0:T(8,128)S(1)} %slice.24), channel_id=1, source_target_pairs={{0,5},{1,4},{4,1},{5,0},{8,13},{9,12},{12,9},{13,8},{2,7},{3,6},{6... | collective-permute-start | bytes 24584 | tf_op jit(solution)/shard_map/ppermute | solution.py:450
  21.6 4.0 %collective-permute-start.7 = (f32[16,128]{1,0:T(8,128)S(1)}, f32[16,128]{1,0:T(8,128)S(1)}, u32[]{:S(2)}, u32[]{:S(2)}) collective-permute-start(f32[16,128]{1,0:T(8,128)S(1)} %slice_add_fusion.1), channel_id=1, source_target_pairs={{0,9},{1,8},{4,13},{5,12},{8,1},{9,0},{12,5},{13,4},{2,11},{3,10},... | collective-permute-start | bytes 24584 | tf_op jit(solution)/shard_map/ppermute | solution.py:450

commit v9 on v8

--- a/solution.py
+++ b/solution.py
@@ -17,6 +17,7 @@
 
 LANES = 128
 SUBLANES = 8
+GROUPS_AT_ONCE = 4
 BLOCKS_AT_ONCE = 4
 SUM_ROWS = 16
 SOURCE_AXES = ("tgt",)
@@ -34,48 +35,55 @@
     scaled[3:6, :] = ISO * source_ref[3:6, :]
     scaled[6:9, :] = DYAD * source_ref[3:6, :]
 
-    def add_block(point, base, block, sums):
+    def add_block(points, base, block, sums):
         lanes = pl.ds(pl.multiple_of(base + block * LANES, LANES), LANES)
         x, y, z, fx, fy, fz, gx, gy, gz = [
             jnp.broadcast_to(scaled[k : k + 1, lanes], (SUBLANES, LANES)) for k in range(9)
         ]
-        dx, dy, dz = point[0] - x, point[1] - y, point[2] - z
-        square = dx * dx + dy * dy + dz * dz
-        inverse = lax.rsqrt(jnp.maximum(square, SMALLEST))
-        held = jnp.minimum(inverse, TOUCH_INVERSE)
-        held_sq = held * held
-        iso = jnp.maximum(held * (held_sq + 2.0), NEAR - square * inverse)
-        along = dx * gx + dy * gy + dz * gz
-        dyad = (inverse * (held_sq * (2.0 / 3.0 - held_sq))) * along
-        terms = (iso * fx + dyad * dx, iso * fy + dyad * dy, iso * fz + dyad * dz)
-        return terms if sums is None else tuple(one + term for one, term in zip(sums, terms))
+        result = []
+        for number, point in enumerate(points):
+            dx, dy, dz = point[0] - x, point[1] - y, point[2] - z
+            square = dx * dx + dy * dy + dz * dz
+            inverse = lax.rsqrt(jnp.maximum(square, SMALLEST))
+            held = jnp.minimum(inverse, TOUCH_INVERSE)
+            held_sq = held * held
+            iso = jnp.maximum(held * (held_sq + 2.0), NEAR - square * inverse)
+            along = dx * gx + dy * gy + dz * gz
+            dyad = (inverse * (held_sq * (2.0 / 3.0 - held_sq))) * along
+            terms = (iso * fx + dyad * dx, iso * fy + dyad * dy, iso * fz + dyad * dz)
+            if sums is not None:
+                terms = tuple(one + term for one, term in zip(sums[number], terms))
+            result.append(terms)
+        return tuple(result)
 
     def tile_step(step, unused):
         first = step * LANES if isinstance(step, int) else pl.multiple_of(step * LANES, LANES)
         if beside is not None:
             beside(first)
-        for group in range(LANES // SUBLANES):
-            rows = pl.ds(first + group * SUBLANES, SUBLANES)
-            point = [points_ref[k, rows, :] for k in range(3)]
+        for group in range(0, LANES // SUBLANES, GROUPS_AT_ONCE):
+            starts = [(group + one) * SUBLANES for one in range(GROUPS_AT_ONCE)]
+            rows = [pl.ds(first + start, SUBLANES) for start in starts]
+            points = [[points_ref[k, one, :] for k in range(3)] for one in rows]
             sums = None
             if before_ref is not None:
-                sums = tuple(before_ref[k, rows, :] for k in range(3))
+                sums = tuple(tuple(before_ref[k, one, :] for k in range(3)) for one in rows)
             if blocks == together:
                 for block in range(together):
-                    sums = add_block(point, 0, block, sums)
+                    sums = add_block(points, 0, block, sums)
             else:
 
                 def source_step(number, sums):
                     for block in range(together):
-                        sums = add_block(point, number * (together * LANES), block, sums)
+                        sums = add_block(points, number * (together * LANES), block, sums)
                     return sums
 
                 zero = jnp.zeros((SUBLANES, LANES), jnp.float32)
                 sums = lax.fori_loop(
-                    0, blocks // together, source_step, sums or (zero, zero, zero)
+                    0, blocks // together, source_step, sums or ((zero,) * 3,) * GROUPS_AT_ONCE
                 )
-            for k in range(3):
-                total_ref[k, pl.ds(first + shift + group * SUBLANES, SUBLANES), :] = sums[k]
+            for start, one in zip(starts, sums):
+                for k in range(3):
+                    total_ref[k, pl.ds(first + shift + start, SUBLANES), :] = one[k]
         return unused
 
     tiles = count // LANES

time: 26.5 us -> 26.5 us (level)
  no operation moved by 1% of the time
where the time goes in v9:
time: 26.5 us; the launch traced here: 26.3 us
  starting transfers between devices  11.2 us (42%)
  Pallas kernels  8.07 us (30%)
  waiting for transfers between devices  6.29 us (24%)
  between operations  0.7 us (3%)
    pallas_call x7, Pallas kernels, call(): pl.pallas_call(kernel, out_shape=[jax.ShapeDtypeStruct(shape, dtype) for...  8.07 us
    ppermute x2, starting transfers between devices, on_device(): coming = lax.ppermute(sources, axis, pairs)  4.65 us
    ppermute x2, waiting for transfers between devices, on_device(): coming = lax.ppermute(sums, axis, pairs)  3.45 us
    ppermute x2, starting transfers between devices, on_device(): coming = lax.ppermute(sums, axis, pairs)  3 us
    ppermute x2, waiting for transfers between devices, on_device(): both = keep + lax.ppermute(send, axis, pairs)  2.82 us
    ppermute x2, starting transfers between devices, on_device(): arriving = lax.ppermute(targets, axis, pairs)  1.8 us
    ppermute x2, starting transfers between devices, on_device(): both = keep + lax.ppermute(send, axis, pairs)  1.72 us
  transfers between devices with their start and end apart: 8, of which 4 were waited for; matrix products, arithmetic and copies ran while one was open for 0% of the time, Pallas kernels for 14%

profile of v9, /device:TPU:0, one launch (start us, length us, event | category | flops | bytes accessed | tf_op | source)
XLA Modules:
  0.0 26.3 jit_solution(15736949318003079795)
XLA Ops:
  0.6 0.8 %shard_map.59 = (f32[6,256]{1,0:T(8,128)S(1)}, f32[4,256]{1,0:T(4,128)S(1)}, s32[1,16]{1,0:T(1,128)S(1)}) custom-call(f32[3,256]{1,0:T(4,128)} %position_in.1, f32[3,256]{1,0:T(4,128)} %force_in.1, s32[1,256]{1,0:T(1,128)} %bitcast.3, s32[1,16]{1,0:T(1,128)} %bitcast.4), custom_call_target="tpu_custom_call" | custom-call | flops 1000 | bytes 1000 | tf_op jit(solution)/shard_map/pallas_call | solution.py:324
  1.4 0.6 %collective-permute-start = (f32[4,256]{1,0:T(4,128)S(1)}, f32[4,256]{1,0:T(4,128)S(1)}, u32[]{:S(2)}, u32[]{:S(2)}) collective-permute-start(f32[4,256]{1,0:T(4,128)S(1)} %get-tuple-element.28), channel_id=1, source_target_pairs={{0,1},{1,0},{2,3},{3,2},{4,5},{5,4},{6,7},{7,6},{8,9},{9,8},{10,11... | collective-permute-start | bytes 12296 | tf_op jit(solution)/shard_map/ppermute | solution.py:381
  1.9 2.7 %collective-permute-start.1 = (f32[6,256]{1,0:T(8,128)S(1)}, f32[6,256]{1,0:T(8,128)S(1)}, u32[]{:S(2)}, u32[]{:S(2)}) collective-permute-start(f32[6,256]{1,0:T(8,128)S(1)} %get-tuple-element.29.source_ref), channel_id=1, source_target_pairs={{0,5},{1,4},{4,1},{5,0},{8,13},{9,12},{12,9},{13,8},{2,7},{3,6},{6... | collective-permute-start | bytes 18440 | tf_op jit(solution)/shard_map/ppermute | solution.py:386
  4.6 0.0 collective-permute-done
  4.6 1.2 %collective-permute-start.2 = (f32[4,512]{1,0:T(4,128)S(1)}, f32[4,512]{1,0:T(4,128)S(1)}, u32[]{:S(2)}, u32[]{:S(2)}) collective-permute-start(f32[4,512]{1,0:T(4,128)S(1)} %constant_dynamic-update-slice_fusion.target_ref), channel_id=1, source_target_pairs={{0,3},{1,2},{2,1},{3,0},{4,7},{5,6},{6,5},{7,4},{8,11},{9,10},{10,... | collective-permute-start | bytes 24584 | tf_op jit(solution)/shard_map/ppermute | solution.py:381
  5.9 0.8 %shard_map.60 = (f32[3,1024,128]{2,1,0:T(8,128)S(1)}, f32[3,1024,128]{2,1,0:T(8,128)S(1)}, bf16[16,1024]{1,0:T(8,128)(2,1)S(1)}) custom-call(f32[4,512]{1,0:T(4,128)S(1)} %constant_dynamic-update-slice_fusion.target_ref, f32[6,256]{1,0:T(8,128)S(1)} %get-tuple-element.29.source_ref, s32[1,16]{1,0:T(1,128)S(1)} %get-tuple-element.30.owner_ref), custom_call_target="tpu_custom_call" | custom-call | flops 5243880 | bytes 1000 | tf_op jit(solution)/shard_map/pallas_call | solution.py:324
  6.7 0.0 collective-permute-done.1
  6.7 2.0 %collective-permute-start.3 = (f32[6,512]{1,0:T(8,128)S(1)}, f32[6,512]{1,0:T(8,128)S(1)}, u32[]{:S(2)}, u32[]{:S(2)}) collective-permute-start(f32[6,512]{1,0:T(8,128)S(1)} %constant_dynamic-update-slice_fusion.2.source_ref), channel_id=1, source_target_pairs={{0,9},{1,8},{4,13},{5,12},{8,1},{9,0},{12,5},{13,4},{2,11},{3,10},... | collective-permute-start | bytes 36872 | tf_op jit(solution)/shard_map/ppermute | solution.py:411
  8.7 0.0 collective-permute-done.2.target_ref
  8.7 2.2 %shard_map.62 = (f32[3,1024,128]{2,1,0:T(8,128)S(1)}, f32[3,1024,128]{2,1,0:T(8,128)S(1)}, bf16[16,1024]{1,0:T(8,128)(2,1)S(1)}) custom-call(f32[4,512]{1,0:T(4,128)S(1)} %collective-permute-done.2.target_ref, f32[6,512]{1,0:T(8,128)S(1)} %constant_dynamic-update-slice_fusion.2.source_ref, ...), custom_call_target="tpu_custom_call", output_to_operand_aliasing={{0}: (3, {}), {1}: (4, {}), {2}: (5, {})} | custom-call | flops 15729640 | bytes 1000 | tf_op jit(solution)/shard_map/pallas_call | solution.py:324
  10.9 0.0 collective-permute-done.3.source_ref
  10.9 3.0 %shard_map.63 = (f32[32,128]{1,0:T(8,128)S(1)}, f32[32,128]{1,0:T(8,128)S(1)}) custom-call(f32[3,1024,128]{2,1,0:T(8,128)S(1)} %get-tuple-element.45.points_ref, f32[6,512]{1,0:T(8,128)S(1)} %collective-permute-done.3.source_ref, f32[3,1024,128]{2,1,0:T(8,128)S(1)} %get-tuple-element.48.before_ref, bf16[16,1024]{1,0:T(8,128)(2,1)S(1)} %get-tuple-element.49.match_ref, ...), custom_call_target="tpu_custom_call" | custom-call | flops 20972520 | bytes 1000 | tf_op jit(solution)/shard_map/pallas_call | solution.py:324
  14.0 1.2 %collective-permute-start.4 = (f32[32,128]{1,0:T(8,128)S(1)}, f32[32,128]{1,0:T(8,128)S(1)}, u32[]{:S(2)}, u32[]{:S(2)}) collective-permute-start(f32[32,128]{1,0:T(8,128)S(1)} %get-tuple-element.51), channel_id=1, source_target_pairs={{0,3},{1,2},{2,1},{3,0},{4,7},{5,6},{6,5},{7,4},{8,11},{9,10},{10,... | collective-permute-start | bytes 49160 | tf_op jit(solution)/shard_map/ppermute | solution.py:454
  15.2 2.0 %collective-permute-done.4 = f32[32,128]{1,0:T(8,128)S(1)} collective-permute-done((f32[32,128]{1,0:T(8,128)S(1)}, f32[32,128]{1,0:T(8,128)S(1)}, u32[]{:S(2)}, u32[]{:S(2)}) %collective-permute-start.4) | collective-permute-done | bytes 16416 | tf_op jit(solution)/shard_map/ppermute | solution.py:454
  17.2 0.5 %collective-permute-start.5 = (f32[24,128]{1,0:T(8,128)S(1)}, f32[24,128]{1,0:T(8,128)S(1)}, u32[]{:S(2)}, u32[]{:S(2)}) collective-permute-start(f32[24,128]{1,0:T(8,128)S(1)} %pad_maximum_fusion.1), channel_id=1, source_target_pairs={{0,1},{1,0},{2,3},{3,2},{4,5},{5,4},{6,7},{7,6},{8,9},{9,8},{10,11... | collective-permute-start | bytes 36872 | tf_op jit(solution)/shard_map/ppermute | solution.py:454
  17.7 0.8 %collective-permute-done.5 = f32[24,128]{1,0:T(8,128)S(1)} collective-permute-done((f32[24,128]{1,0:T(8,128)S(1)}, f32[24,128]{1,0:T(8,128)S(1)}, u32[]{:S(2)}, u32[]{:S(2)}) %collective-permute-start.5) | collective-permute-done | bytes 12320 | tf_op jit(solution)/shard_map/ppermute | solution.py:454
  18.5 1.2 %collective-permute-start.6 = (f32[16,128]{1,0:T(8,128)S(1)}, f32[16,128]{1,0:T(8,128)S(1)}, u32[]{:S(2)}, u32[]{:S(2)}) collective-permute-start(f32[16,128]{1,0:T(8,128)S(1)} %slice.24), channel_id=1, source_target_pairs={{0,5},{1,4},{4,1},{5,0},{8,13},{9,12},{12,9},{13,8},{2,7},{3,6},{6... | collective-permute-start | bytes 24584 | tf_op jit(solution)/shard_map/ppermute | solution.py:458
  19.8 0.6 %shard_map.64 = f32[3,256]{1,0:T(4,128)} custom-call(f32[8,128]{1,0:T(8,128)S(1)} %slice.23.packed_ref), custom_call_target="tpu_custom_call" | custom-call | flops 1000 | bytes 1000 | tf_op jit(solution)/shard_map/pallas_call | solution.py:324
  20.4 1.2 %collective-permute-done.6 = f32[16,128]{1,0:T(8,128)S(1)} collective-permute-done((f32[16,128]{1,0:T(8,128)S(1)}, f32[16,128]{1,0:T(8,128)S(1)}, u32[]{:S(2)}, u32[]{:S(2)}) %collective-permute-start.6) | collective-permute-done | bytes 8224 | tf_op jit(solution)/shard_map/ppermute | solution.py:458
  21.6 1.8 %collective-permute-start.7 = (f32[16,128]{1,0:T(8,128)S(1)}, f32[16,128]{1,0:T(8,128)S(1)}, u32[]{:S(2)}, u32[]{:S(2)}) collective-permute-start(f32[16,128]{1,0:T(8,128)S(1)} %slice_add_fusion.1), channel_id=1, source_target_pairs={{0,9},{1,8},{4,13},{5,12},{8,1},{9,0},{12,5},{13,4},{2,11},{3,10},... | collective-permute-start | bytes 24584 | tf_op jit(solution)/shard_map/ppermute | solution.py:458
  23.4 2.2 %collective-permute-done.7 = f32[16,128]{1,0:T(8,128)S(1)} collective-permute-done((f32[16,128]{1,0:T(8,128)S(1)}, f32[16,128]{1,0:T(8,128)S(1)}, u32[]{:S(2)}, u32[]{:S(2)}) %collective-permute-start.7) | collective-permute-done | bytes 8224 | tf_op jit(solution)/shard_map/ppermute | solution.py:458
  25.6 0.7 %shard_map.65 = f32[1,9]{1,0:T(1,128)} custom-call(f32[16,128]{1,0:T(8,128)S(1)} %add.15.sums_ref), custom_call_target="tpu_custom_call" | custom-call | flops 1000 | bytes 1000 | tf_op jit(solution)/shard_map/pallas_call | solution.py:324
  (15 shorter events, 0.1 us)
Async XLA Ops:
  1.4 3.2 %collective-permute-start = (f32[4,256]{1,0:T(4,128)S(1)}, f32[4,256]{1,0:T(4,128)S(1)}, u32[]{:S(2)}, u32[]{:S(2)}) collective-permute-start(f32[4,256]{1,0:T(4,128)S(1)} %get-tuple-element.28), channel_id=1, source_target_pairs={{0,1},{1,0},{2,3},{3,2},{4,5},{5,4},{6,7},{7,6},{8,9},{9,8},{10,11... | collective-permute-start | bytes 12296 | tf_op jit(solution)/shard_map/ppermute | solution.py:381
  1.9 4.8 %collective-permute-start.1 = (f32[6,256]{1,0:T(8,128)S(1)}, f32[6,256]{1,0:T(8,128)S(1)}, u32[]{:S(2)}, u32[]{:S(2)}) collective-permute-start(f32[6,256]{1,0:T(8,128)S(1)} %get-tuple-element.29.source_ref), channel_id=1, source_target_pairs={{0,5},{1,4},{4,1},{5,0},{8,13},{9,12},{12,9},{13,8},{2,7},{3,6},{6... | collective-permute-start | bytes 18440 | tf_op jit(solution)/shard_map/ppermute | solution.py:386
  4.6 4.1 %collective-permute-start.2 = (f32[4,512]{1,0:T(4,128)S(1)}, f32[4,512]{1,0:T(4,128)S(1)}, u32[]{:S(2)}, u32[]{:S(2)}) collective-permute-start(f32[4,512]{1,0:T(4,128)S(1)} %constant_dynamic-update-slice_fusion.target_ref), channel_id=1, source_target_pairs={{0,3},{1,2},{2,1},{3,0},{4,7},{5,6},{6,5},{7,4},{8,11},{9,10},{10,... | collective-permute-start | bytes 24584 | tf_op jit(solution)/shard_map/ppermute | solution.py:381
  6.7 4.2 %collective-permute-start.3 = (f32[6,512]{1,0:T(8,128)S(1)}, f32[6,512]{1,0:T(8,128)S(1)}, u32[]{:S(2)}, u32[]{:S(2)}) collective-permute-start(f32[6,512]{1,0:T(8,128)S(1)} %constant_dynamic-update-slice_fusion.2.source_ref), channel_id=1, source_target_pairs={{0,9},{1,8},{4,13},{5,12},{8,1},{9,0},{12,5},{13,4},{2,11},{3,10},... | collective-permute-start | bytes 36872 | tf_op jit(solution)/shard_map/ppermute | solution.py:411
  14.0 3.2 %collective-permute-start.4 = (f32[32,128]{1,0:T(8,128)S(1)}, f32[32,128]{1,0:T(8,128)S(1)}, u32[]{:S(2)}, u32[]{:S(2)}) collective-permute-start(f32[32,128]{1,0:T(8,128)S(1)} %get-tuple-element.51), channel_id=1, source_target_pairs={{0,3},{1,2},{2,1},{3,0},{4,7},{5,6},{6,5},{7,4},{8,11},{9,10},{10,... | collective-permute-start | bytes 49160 | tf_op jit(solution)/shard_map/ppermute | solution.py:454
  17.2 1.4 %collective-permute-start.5 = (f32[24,128]{1,0:T(8,128)S(1)}, f32[24,128]{1,0:T(8,128)S(1)}, u32[]{:S(2)}, u32[]{:S(2)}) collective-permute-start(f32[24,128]{1,0:T(8,128)S(1)} %pad_maximum_fusion.1), channel_id=1, source_target_pairs={{0,1},{1,0},{2,3},{3,2},{4,5},{5,4},{6,7},{7,6},{8,9},{9,8},{10,11... | collective-permute-start | bytes 36872 | tf_op jit(solution)/shard_map/ppermute | solution.py:454
  18.5 3.1 %collective-permute-start.6 = (f32[16,128]{1,0:T(8,128)S(1)}, f32[16,128]{1,0:T(8,128)S(1)}, u32[]{:S(2)}, u32[]{:S(2)}) collective-permute-start(f32[16,128]{1,0:T(8,128)S(1)} %slice.24), channel_id=1, source_target_pairs={{0,5},{1,4},{4,1},{5,0},{8,13},{9,12},{12,9},{13,8},{2,7},{3,6},{6... | collective-permute-start | bytes 24584 | tf_op jit(solution)/shard_map/ppermute | solution.py:458
  21.6 4.0 %collective-permute-start.7 = (f32[16,128]{1,0:T(8,128)S(1)}, f32[16,128]{1,0:T(8,128)S(1)}, u32[]{:S(2)}, u32[]{:S(2)}) collective-permute-start(f32[16,128]{1,0:T(8,128)S(1)} %slice_add_fusion.1), channel_id=1, source_target_pairs={{0,9},{1,8},{4,13},{5,12},{8,1},{9,0},{12,5},{13,4},{2,11},{3,10},... | collective-permute-start | bytes 24584 | tf_op jit(solution)/shard_map/ppermute | solution.py:458
